TPU v7x, 32 devices: a whole 2x2x4 slice. The times are simulated.
32 devices in a mesh: lat: 4 (over y, x), lon: 8 (over z, core).
Axes of the slice: x: 2, y: 2, z: 4, core: 2. Of those that a mesh axis runs over, the one named last changes fastest.
Arguments:
- inputs: bfloat16 [360, 360, 256], P('lat', 'lon'), may hold values from -6 to 6
- kernel: bfloat16 [3, 3, 256, 256], replicated, may hold values from -0.125 to 0.125
- cotangent: bfloat16 [360, 360, 256], P('lat', 'lon'), may hold values from -6 to 6
Outputs:
- outputs: bfloat16 [360, 360, 256], P('lat', 'lon')
- input_grad: bfloat16 [360, 360, 256], P('lat', 'lon')
- kernel_grad: float32 [3, 3, 256, 256], replicated
All inputs are finite; a program needn't handle non-finite values.
Results may differ from a plain program's by a relative error of at most 0.001.
Values may be sent and summed in bfloat16 or wider, within the bound.
No kernel may reach another device: no remote copies, remote signals or barrier semaphores. Data moves between devices by JAX's collectives and lax.ppermute only.
A program may use at most 192 MiB of HBM per device.

v0:
```python
import math

import jax
import jax.numpy as jnp
from jax import lax
from jax.sharding import PartitionSpec as P


def with_halo(cells, sides, width):
    for axis, dim in sides:
        count = lax.axis_size(axis)
        head = lax.slice_in_dim(cells, 0, width, axis=dim)
        tail = lax.slice_in_dim(cells, cells.shape[dim] - width, cells.shape[dim], axis=dim)
        cells = jnp.concatenate(
            [
                lax.ppermute(tail, axis, [(i, (i + 1) % count) for i in range(count)]),
                cells,
                lax.ppermute(head, axis, [((i + 1) % count, i) for i in range(count)]),
            ],
            axis=dim,
        )
    return cells


def from_behind(value, axis, steps):
    count = lax.axis_size(axis)
    pairs = [(source, (source + steps) % count) for source in range(count)]
    return lax.ppermute(value, axis, pairs)


def patches(padded, rows, cols):
    pieces = [
        padded[row_tap : row_tap + rows, col_tap : col_tap + cols]
        for row_tap in range(3)
        for col_tap in range(3)
    ]
    return jnp.concatenate(pieces, axis=-1).reshape(rows * cols, -1)


def surround(field):
    return with_halo(field, (("lat", 0), ("lon", 1)), 1)


def polar(padded):
    both = jnp.stack([padded[1], padded[-2]])
    moved = from_behind(both, "lon", lax.axis_size("lon") // 2)
    return (moved[0], moved[1])


def edge_term(row_data, weights, cols, width):
    stacked = jnp.concatenate([row_data[offset : offset + cols] for offset in range(3)], axis=-1)
    return jnp.dot(stacked, weights.reshape(-1, width), preferred_element_type=jnp.float32)


def local(inputs, kernel, cotangent):
    rows, cols, width = inputs.shape
    north = lax.axis_index("lat") == 0
    south = lax.axis_index("lat") == lax.axis_size("lat") - 1
    padded = surround(inputs)
    top, bottom = polar(padded)
    padded = jnp.concatenate(
        [
            jnp.where(north, top, padded[0])[None],
            padded[1:-1],
            jnp.where(south, bottom, padded[-1])[None],
        ],
        0,
    )
    columns = patches(padded, rows, cols)
    outputs = jnp.dot(columns, kernel.reshape(-1, width), preferred_element_type=jnp.float32)
    outputs = outputs.reshape(rows, cols, width).astype(jnp.bfloat16)
    flat_grad = cotangent.reshape(-1, width)
    local_grad = lax.dot_general(
        columns, flat_grad, (((0,), (0,)), ((), ())), preferred_element_type=jnp.float32
    )
    local_grad = local_grad.reshape(3, 3, width, width)
    padded_grad = surround(cotangent)
    grad_top, grad_bottom = polar(padded_grad)
    empty_row = jnp.zeros_like(padded_grad[0])
    padded_grad = jnp.concatenate(
        [
            jnp.where(north, empty_row, padded_grad[0])[None],
            padded_grad[1:-1],
            jnp.where(south, empty_row, padded_grad[-1])[None],
        ],
        0,
    )
    flipped = jnp.transpose(kernel[::-1, ::-1], (0, 1, 3, 2))
    input_grad = jnp.dot(
        patches(padded_grad, rows, cols),
        flipped.reshape(-1, width),
        preferred_element_type=jnp.float32,
    )
    input_grad = input_grad.reshape(rows, cols, width)
    north_term = edge_term(grad_top, flipped[2], cols, width)
    south_term = edge_term(grad_bottom, flipped[0], cols, width)
    input_grad = input_grad.at[0].add(jnp.where(north, north_term, 0.0))
    input_grad = input_grad.at[-1].add(jnp.where(south, south_term, 0.0))
    factor = 1.0 / math.sqrt(rows * cols * lax.axis_size("lat") * lax.axis_size("lon"))
    partial_sum = lax.psum(local_grad, "lon")
    summed = lax.psum(partial_sum, "lat")
    return (outputs, input_grad.astype(jnp.bfloat16), summed * factor)


def solution(mesh):
    in_specs = (P("lat", "lon", None), P(), P("lat", "lon", None))
    out_specs = (P("lat", "lon", None), P("lat", "lon", None), P())
    return jax.shard_map(local, mesh=mesh, in_specs=in_specs, out_specs=out_specs, check_vma=False)
```

profile of v0, /device:TPU:0, one launch (start us, length us, event | category | flops | bytes accessed | tf_op | source)
XLA Modules:
  0.0 271.3 jit_solution(15557798716294932809)
XLA Ops:
  8.0 3.9 %collective-permute-start.1 = (bf16[1,45,256]{2,1,0:T(8,128)(2,1)S(1)}, bf16[1,45,256]{2,1,0:T(8,128)(2,1)S(1)}, u32[]{:S(2)}, u32[]{:S(2)}) collective-permute-start(bf16[1,45,256]{2,1,0:T(8,128)(2,1)S(1)} %get-tuple-element.37), channel_id=1, source_target_pairs={{8,0},{16,8},{24,16},{0,24},{9,1},{17,9},{25,17},{1,25},{10,2},{18... | collective-permute-start | bytes 69128 | tf_op jit(solution)/shard_map/ppermute | solution.py:18
  13.3 2.9 %collective-permute-start.6 = (bf16[1,45,256]{2,1,0:T(8,128)(2,1)}, bf16[1,45,256]{2,1,0:T(8,128)(2,1)S(1)}, u32[]{:S(2)}, u32[]{:S(2)}) collective-permute-start(bf16[1,45,256]{2,1,0:T(8,128)(2,1)} %get-tuple-element.35), channel_id=1, source_target_pairs={{8,0},{16,8},{24,16},{0,24},{9,1},{17,9},{25,17},{1,25},{10,2},{18... | collective-permute-start | bytes 69128 | tf_op jit(solution)/shard_map/ppermute | solution.py:18
  19.9 1.9 reshape.103
  22.2 3.5 %collective-permute-start.8 = (bf16[92,1,256]{2,1,0:T(2,128)(2,1)S(1)}, bf16[92,1,256]{2,1,0:T(2,128)(2,1)S(1)}, u32[]{:S(2)}, u32[]{:S(2)}) collective-permute-start(bf16[92,1,256]{2,1,0:T(2,128)(2,1)S(1)} %get-tuple-element.32), channel_id=1, source_target_pairs={{1,0},{2,1},{3,2},{4,3},{5,4},{6,5},{7,6},{0,7},{9,8},{10,9},{11,1... | collective-permute-start | bytes 141320 | tf_op jit(solution)/shard_map/ppermute | solution.py:18
  26.2 3.5 %collective-permute-start.3 = (bf16[92,1,256]{2,1,0:T(2,128)(2,1)S(1)}, bf16[92,1,256]{2,1,0:T(2,128)(2,1)S(1)}, u32[]{:S(2)}, u32[]{:S(2)}) collective-permute-start(bf16[92,1,256]{2,1,0:T(2,128)(2,1)S(1)} %get-tuple-element.34), channel_id=1, source_target_pairs={{1,0},{2,1},{3,2},{4,3},{5,4},{6,5},{7,6},{0,7},{9,8},{10,9},{11,1... | collective-permute-start | bytes 141320 | tf_op jit(solution)/shard_map/ppermute | solution.py:18
  29.8 2.6 collective-permute-done.2
  34.6 1.6 fusion.7
  36.2 2.8 %fusion.5 = bf16[90,45,2304]{2,1,0:T(8,128)(2,1)} fusion(bf16[90,45,2304]{2,1,0:T(8,128)(2,1)} %fusion.7, bf16[1,47,256]{2,1,0:T(8,128)(2,1)S(1)} %get-tuple-element.30, bf16[90,47,256]{2,1,0:T(8,128)(2,1)S(1)} %slice.295), kind=kLoop, calls=%fused_computation.15 | loop fusion | flops 4147200 | bytes 4401664
  40.7 1.7 fusion.15
  42.5 2.7 %fusion.13 = bf16[90,45,2304]{2,1,0:T(8,128)(2,1)} fusion(bf16[90,45,2304]{2,1,0:T(8,128)(2,1)} %fusion.15, bf16[1,47,256]{2,1,0:T(8,128)(2,1)S(1)} %get-tuple-element.28, bf16[90,47,256]{2,1,0:T(8,128)(2,1)S(1)} %slice.283), kind=kLoop, calls=%fused_computation.23 | loop fusion | flops 4147200 | bytes 4401664
  45.2 2.8 %fusion.23 = bf16[90,45,2304]{2,1,0:T(8,128)(2,1)} fusion(bf16[90,45,2304]{2,1,0:T(8,128)(2,1)} %fusion.13, bf16[90,47,256]{2,1,0:T(8,128)(2,1)S(1)} %slice.283, bf16[1,47,256]{2,1,0:T(8,128)(2,1)S(1)} %get-tuple-element.28), kind=kLoop, calls=%fused_computation.41 | loop fusion | flops 4147200 | bytes 4401664
  48.0 2.9 %fusion.22 = bf16[90,45,2304]{2,1,0:T(8,128)(2,1)} fusion(bf16[90,45,2304]{2,1,0:T(8,128)(2,1)} %fusion.23, bf16[92,45,256]{2,1,0:T(8,128)(2,1)S(1)} %constant_dynamic-update-slice_fusion, bf16[92,1,256]{2,1,0:T(2,128)(2,1)S(1)} %collective-permute-done.2), kind=kLoop, calls=%fused_computation.39 | loop fusion | flops 4147200 | bytes 4378624
  50.8 1.7 constant_dynamic-update-slice_fusion.3
  52.5 3.1 %fusion.21 = bf16[90,45,2304]{2,1,0:T(8,128)(2,1)} fusion(bf16[90,45,2304]{2,1,0:T(8,128)(2,1)} %constant_dynamic-update-slice_fusion.3, bf16[92,1,256]{2,1,0:T(2,128)(2,1)S(1)} %collective-permute-done.3, bf16[92,45,256]{2,1,0:T(8,128)(2,1)S(1)} %constant_dynamic-update-slice_fusion), kind=kLoop, calls=%fused_computation.37 | loop fusion | flops 4147200 | bytes 4378624
  55.6 1.7 fusion.11
  57.3 2.8 %fusion.9 = bf16[90,45,2304]{2,1,0:T(8,128)(2,1)} fusion(bf16[90,45,2304]{2,1,0:T(8,128)(2,1)} %fusion.11, bf16[1,47,256]{2,1,0:T(8,128)(2,1)S(1)} %get-tuple-element.27, bf16[90,47,256]{2,1,0:T(8,128)(2,1)S(1)} %slice.283), kind=kLoop, calls=%fused_computation.19 | loop fusion | flops 4147200 | bytes 4401664
  60.0 3.1 %fusion.20 = bf16[90,45,2304]{2,1,0:T(8,128)(2,1)} fusion(bf16[90,45,2304]{2,1,0:T(8,128)(2,1)} %fusion.9, bf16[1,47,256]{2,1,0:T(8,128)(2,1)S(1)} %get-tuple-element.27, bf16[90,47,256]{2,1,0:T(8,128)(2,1)S(1)} %slice.283), kind=kLoop, calls=%fused_computation.35 | loop fusion | flops 4147200 | bytes 4401664 | tf_op jit(solution)/shard_map/concatenate | solution.py:37
  63.2 19.5 %reshape.99 = bf16[4050,2304]{1,0:T(8,128)(2,1)} reshape(bf16[90,45,2304]{2,1,0:T(8,128)(2,1)} %fusion.20) | data formatting | bytes 37324800 | tf_op jit(solution)/shard_map/reshape | solution.py:37
  82.7 23.0 %copy.7 = bf16[4050,2304]{0,1:T(8,128)(2,1)} copy(bf16[4050,2304]{1,0:T(8,128)(2,1)} %reshape.99) | data formatting | bytes 37324800 | tf_op jit(solution)/shard_map/reshape | solution.py:37
  105.7 10.6 %fusion.24 = f32[3,3,256,256]{3,2,1,0:T(8,128)} fusion(bf16[3,3,256,4050]{3,2,1,0:T(8,128)(2,1)} %bitcast.46, bf16[4050,256,1,1]{1,0,2,3:T(8,128)(2,1)} %reshape.103), kind=kOutput, calls=%fused_computation.42 | convolution fusion | flops 4777574400 | bytes 23095296 | tf_op jit(solution)/shard_map/dot_general | solution.py:73
  116.4 2.7 fusion.19
  119.1 2.8 %fusion.18 = bf16[90,45,2304]{2,1,0:T(8,128)(2,1)} fusion(bf16[90,45,2304]{2,1,0:T(8,128)(2,1)} %fusion.19, bf16[92,45,256]{2,1,0:T(8,128)(2,1)S(1)} %copy-done.1, bf16[92,1,256]{2,1,0:T(2,128)(2,1)S(1)} %collective-permute-done.7), kind=kLoop, calls=%fused_computation.31 | loop fusion | flops 4147200 | bytes 4378624
  121.9 1.6 constant_dynamic-update-slice_fusion.7
  123.4 2.9 %fusion.17 = bf16[90,45,2304]{2,1,0:T(8,128)(2,1)} fusion(bf16[90,45,2304]{2,1,0:T(8,128)(2,1)} %constant_dynamic-update-slice_fusion.7, bf16[92,1,256]{2,1,0:T(2,128)(2,1)S(1)} %collective-permute-done.8, bf16[92,45,256]{2,1,0:T(8,128)(2,1)S(1)} %copy-done.1), kind=kLoop, calls=%fused_computation.29 | loop fusion | flops 4147200 | bytes 4378624
  127.9 2.7 %fusion.1 = bf16[90,45,2304]{2,1,0:T(8,128)(2,1)} fusion(bf16[90,45,2304]{2,1,0:T(8,128)(2,1)} %fusion.3, bf16[1,47,256]{2,1,0:T(8,128)(2,1)S(1)} %get-tuple-element.29, bf16[90,47,256]{2,1,0:T(8,128)(2,1)S(1)} %slice.295), kind=kLoop, calls=%fused_computation.11 | loop fusion | flops 4147200 | bytes 4401664
  130.7 2.7 fusion.16
  133.4 51.7 %all-reduce.3.cloned.1.call-done = f32[3,3,256,256]{3,2,1,0:T(8,128)} async-done(((f32[3,3,256,256]{3,2,1,0:T(8,128)}), f32[3,3,256,256]{3,2,1,0:T(8,128)}) %all-reduce.3.cloned.1.call-update) | async-done | bytes 2359312 | tf_op jit(solution)/shard_map/psum | solution.py:100
  185.2 9.9 %fusion.72 = f32[90,45,256]{2,1,0:T(8,128)S(1)} fusion(bf16[90,45,2304]{2,1,0:T(8,128)(2,1)} %fusion.16, bf16[2304,256,1]{1,0,2:T(8,128)(2,1)S(1)} %bitcast.50), kind=kOutput, calls=%fused_computation.114 | convolution fusion | flops 4777574400 | bytes 23989248 | tf_op jit(solution)/shard_map/dot_general | solution.py:89
  195.6 1.6 convert_element_type.7
  197.2 11.6 %convolution_convert_fusion = bf16[90,45,256]{2,1,0:T(8,128)(2,1)} fusion(bf16[90,45,2304]{2,1,0:T(8,128)(2,1)} %fusion.20, bf16[2304,256,1]{1,0,2:T(8,128)(2,1)S(1)} %bitcast.49), kind=kOutput, calls=%fused_computation.44 | convolution fusion | flops 4778611200 | bytes 21915648 | tf_op jit(solution)/shard_map/dot_general | solution.py:70
  208.8 52.4 %all-reduce.5.cloned.1.call-done = f32[3,3,256,256]{3,2,1,0:T(8,128)} async-done(((f32[3,3,256,256]{3,2,1,0:T(8,128)}), f32[3,3,256,256]{3,2,1,0:T(8,128)}) %all-reduce.5.cloned.1.call-update) | async-done | bytes 2359312 | tf_op jit(solution)/shard_map/psum | solution.py:101
  261.2 3.3 %broadcast_multiply_fusion = f32[3,3,256,256]{3,2,1,0:T(8,128)} fusion(f32[3,3,256,256]{3,2,1,0:T(8,128)} %all-reduce.5.cloned.1.call-done), kind=kLoop, calls=%fused_computation.45 | loop fusion | flops 589824 | bytes 4718592 | tf_op jit(solution)/shard_map/mul | solution.py:102
  (63 shorter events, 12.7 us)
Async XLA Ops:
  7.2 178.0 %all-reduce.3.cloned.1.call-start = ((), (), s32[]{:S(2)}) async-start(), calls=%async_computation | async-start | bytes 4718592 | tf_op jit(solution)/shard_map/psum | solution.py:100
  8.0 18.0 %collective-permute-start.1 = (bf16[1,45,256]{2,1,0:T(8,128)(2,1)S(1)}, bf16[1,45,256]{2,1,0:T(8,128)(2,1)S(1)}, u32[]{:S(2)}, u32[]{:S(2)}) collective-permute-start(bf16[1,45,256]{2,1,0:T(8,128)(2,1)S(1)} %get-tuple-element.37), channel_id=1, source_target_pairs={{8,0},{16,8},{24,16},{0,24},{9,1},{17,9},{25,17},{1,25},{10,2},{18... | collective-permute-start | bytes 69128 | tf_op jit(solution)/shard_map/ppermute | solution.py:18
  11.9 13.9 %collective-permute-start = (bf16[1,45,256]{2,1,0:T(8,128)(2,1)S(1)}, bf16[1,45,256]{2,1,0:T(8,128)(2,1)S(1)}, u32[]{:S(2)}, u32[]{:S(2)}) collective-permute-start(bf16[1,45,256]{2,1,0:T(8,128)(2,1)S(1)} %get-tuple-element.38), channel_id=1, source_target_pairs={{0,8},{8,16},{16,24},{24,0},{1,9},{9,17},{17,25},{25,1},{2,10},{10... | collective-permute-start | bytes 69128 | tf_op jit(solution)/shard_map/ppermute | solution.py:16
  13.3 8.7 %collective-permute-start.6 = (bf16[1,45,256]{2,1,0:T(8,128)(2,1)}, bf16[1,45,256]{2,1,0:T(8,128)(2,1)S(1)}, u32[]{:S(2)}, u32[]{:S(2)}) collective-permute-start(bf16[1,45,256]{2,1,0:T(8,128)(2,1)} %get-tuple-element.35), channel_id=1, source_target_pairs={{8,0},{16,8},{24,16},{0,24},{9,1},{17,9},{25,17},{1,25},{10,2},{18... | collective-permute-start | bytes 69128 | tf_op jit(solution)/shard_map/ppermute | solution.py:18
  16.2 5.6 %collective-permute-start.5 = (bf16[1,45,256]{2,1,0:T(8,128)(2,1)}, bf16[1,45,256]{2,1,0:T(8,128)(2,1)S(1)}, u32[]{:S(2)}, u32[]{:S(2)}) collective-permute-start(bf16[1,45,256]{2,1,0:T(8,128)(2,1)} %get-tuple-element.36), channel_id=1, source_target_pairs={{0,8},{8,16},{16,24},{24,0},{1,9},{9,17},{17,25},{25,1},{2,10},{10... | collective-permute-start | bytes 69128 | tf_op jit(solution)/shard_map/ppermute | solution.py:16
  17.9 2.0 copy-start.2
  21.8 4.0 %copy-start.4 = (bf16[90,45,256]{2,1,0:T(8,128)(2,1)S(1)}, bf16[90,45,256]{2,1,0:T(8,128)(2,1)}, u32[]{:S(2)}) copy-start(bf16[90,45,256]{2,1,0:T(8,128)(2,1)} %param.7) | copy-start | bytes 6220804
  22.0 12.5 %copy-start = (bf16[92,45,256]{2,1,0:T(8,128)(2,1)}, bf16[92,45,256]{2,1,0:T(8,128)(2,1)S(1)}, u32[]{:S(2)}) copy-start(bf16[92,45,256]{2,1,0:T(8,128)(2,1)S(1)} %constant_dynamic-update-slice_fusion.4) | copy-start | bytes 6359044
  22.2 7.5 %collective-permute-start.7 = (bf16[92,1,256]{2,1,0:T(2,128)(2,1)S(1)}, bf16[92,1,256]{2,1,0:T(2,128)(2,1)S(1)}, u32[]{:S(2)}, u32[]{:S(2)}) collective-permute-start(bf16[92,1,256]{2,1,0:T(2,128)(2,1)S(1)} %get-tuple-element.31), channel_id=1, source_target_pairs={{0,1},{1,2},{2,3},{3,4},{4,5},{5,6},{6,7},{7,0},{8,9},{9,10},{10,1... | collective-permute-start | bytes 141320 | tf_op jit(solution)/shard_map/ppermute | solution.py:16
  22.2 7.5 %collective-permute-start.8 = (bf16[92,1,256]{2,1,0:T(2,128)(2,1)S(1)}, bf16[92,1,256]{2,1,0:T(2,128)(2,1)S(1)}, u32[]{:S(2)}, u32[]{:S(2)}) collective-permute-start(bf16[92,1,256]{2,1,0:T(2,128)(2,1)S(1)} %get-tuple-element.32), channel_id=1, source_target_pairs={{1,0},{2,1},{3,2},{4,3},{5,4},{6,5},{7,6},{0,7},{9,8},{10,9},{11,1... | collective-permute-start | bytes 141320 | tf_op jit(solution)/shard_map/ppermute | solution.py:18
  26.1 6.3 %collective-permute-start.2 = (bf16[92,1,256]{2,1,0:T(2,128)(2,1)S(1)}, bf16[92,1,256]{2,1,0:T(2,128)(2,1)S(1)}, u32[]{:S(2)}, u32[]{:S(2)}) collective-permute-start(bf16[92,1,256]{2,1,0:T(2,128)(2,1)S(1)} %get-tuple-element.33), channel_id=1, source_target_pairs={{0,1},{1,2},{2,3},{3,4},{4,5},{5,6},{6,7},{7,0},{8,9},{9,10},{10,1... | collective-permute-start | bytes 141320 | tf_op jit(solution)/shard_map/ppermute | solution.py:16
  26.2 6.2 %collective-permute-start.3 = (bf16[92,1,256]{2,1,0:T(2,128)(2,1)S(1)}, bf16[92,1,256]{2,1,0:T(2,128)(2,1)S(1)}, u32[]{:S(2)}, u32[]{:S(2)}) collective-permute-start(bf16[92,1,256]{2,1,0:T(2,128)(2,1)S(1)} %get-tuple-element.34), channel_id=1, source_target_pairs={{1,0},{2,1},{3,2},{4,3},{5,4},{6,5},{7,6},{0,7},{9,8},{10,9},{11,1... | collective-permute-start | bytes 141320 | tf_op jit(solution)/shard_map/ppermute | solution.py:18
  29.8 165.3 %collective-permute-start.9 = (bf16[2,47,256]{2,1,0:T(8,128)(2,1)S(1)}, bf16[2,47,256]{2,1,0:T(8,128)(2,1)S(1)}, u32[]{:S(2)}, u32[]{:S(2)}) collective-permute-start(bf16[2,47,256]{2,1,0:T(8,128)(2,1)S(1)} %fusion.57), channel_id=1, source_target_pairs={{0,4},{1,5},{2,6},{3,7},{4,0},{5,1},{6,2},{7,3},{8,12},{9,13},{10,... | collective-permute-start | bytes 144392 | tf_op jit(solution)/shard_map/ppermute | solution.py:28
  32.4 8.3 %collective-permute-start.4 = (bf16[2,47,256]{2,1,0:T(8,128)(2,1)S(1)}, bf16[2,47,256]{2,1,0:T(8,128)(2,1)S(1)}, u32[]{:S(2)}, u32[]{:S(2)}) collective-permute-start(bf16[2,47,256]{2,1,0:T(8,128)(2,1)S(1)} %fusion.54), channel_id=1, source_target_pairs={{0,4},{1,5},{2,6},{3,7},{4,0},{5,1},{6,2},{7,3},{8,12},{9,13},{10,... | collective-permute-start | bytes 144392 | tf_op jit(solution)/shard_map/ppermute | solution.py:28
  116.3 144.9 %all-reduce.5.cloned.1.call-start = ((), (), s32[]{:S(2)}) async-start(), calls=%async_computation.1 | async-start | bytes 4718592 | tf_op jit(solution)/shard_map/psum | solution.py:101
  116.4 2.7 %copy-start.1 = (bf16[92,45,256]{2,1,0:T(8,128)(2,1)S(1)}, bf16[92,45,256]{2,1,0:T(8,128)(2,1)}, u32[]{:S(2)}) copy-start(bf16[92,45,256]{2,1,0:T(8,128)(2,1)} %copy-done) | copy-start | bytes 6359044
  119.1 2.8 %copy-start.3 = (bf16[90,45,256]{2,1,0:T(8,128)(2,1)S(1)}, bf16[90,45,256]{2,1,0:T(8,128)(2,1)}, u32[]{:S(2)}) copy-start(bf16[90,45,256]{2,1,0:T(8,128)(2,1)} %param.9) | copy-start | bytes 6220804
  133.4 51.8 %copy-start.8 = (bf16[3,3,256,256]{2,3,1,0:T(8,128)(2,1)S(1)}, bf16[3,3,256,256]{2,3,1,0:T(8,128)(2,1)}, u32[]{:S(2)}) copy-start(bf16[3,3,256,256]{2,3,1,0:T(8,128)(2,1)} %rev.3) | copy-start | bytes 3538948
  185.2 9.9 %copy-start.6 = (bf16[1,3,256,256]{3,2,1,0:T(8,128)(2,1)S(1)}, bf16[1,3,256,256]{3,2,1,0:T(8,128)(2,1)}, u32[]{:S(2)}) copy-start(bf16[1,3,256,256]{3,2,1,0:T(8,128)(2,1)} %get-tuple-element.40) | copy-start | bytes 1179652
  185.2 10.2 %copy-start.5 = (bf16[1,3,256,256]{3,2,1,0:T(8,128)(2,1)S(1)}, bf16[1,3,256,256]{3,2,1,0:T(8,128)(2,1)}, u32[]{:S(2)}) copy-start(bf16[1,3,256,256]{3,2,1,0:T(8,128)(2,1)} %get-tuple-element.39) | copy-start | bytes 1179652
  195.5 1.6 copy-start.7
Sparse Core Ops, SparseCore 0:
  116.4 68.6 all-reduce.2
  188.3 72.8 all-reduce.4
where the time goes:
time: 272 us; the launch traced here: 271 us
  waiting for transfers between devices  107 us (39%)
  local copies, waits for them, and re-layouts  54.5 us (20%)
  other arithmetic  48.6 us (18%)
  matrix products  32.5 us (12%)
  starting transfers between devices  14.6 us (5%)
  between operations  14.3 us (5%)
    psum x1, waiting for transfers between devices, local(): summed = lax.psum(partial_sum, 'lat')  52.4 us
    psum x1, waiting for transfers between devices, local(): partial_sum = lax.psum(local_grad, 'lon')  51.7 us
    reshape x2, local copies, waits for them, and re-layouts, patches(): return jnp.concatenate(pieces, axis=-1).reshape(rows * cols, -1)  42.5 us
    unnamed x14, other arithmetic  34.7 us
    ppermute x4, starting transfers between devices, with_halo(): lax.ppermute(head, axis, [((i + 1) % count, i) for i in range(count)])  13.9 us
    dot_general x1, matrix products, local(): jnp.dot(columns, kernel.reshape(-1, width), preferred_element_type=jnp.fl...  11.6 us
    dot_general x1, matrix products, local(): lax.dot_general(columns, flat_grad, (((0,), (0,)), ((), ())), preferred_e...  10.6 us
    dot_general x1, matrix products, local(): jnp.dot(patches(padded_grad, rows, cols), flipped.reshape(-1, width), pre...  9.87 us
  transfers between devices with their start and end apart: 12, of which 3 were waited for; matrix products, arithmetic and copies ran while one was open for 48% of the time, Pallas kernels for 0%

commit v1 on v0

v1 whole, which is shorter than its diff:
```python
import functools
import math

import jax
import jax.numpy as jnp
from jax import lax
from jax.experimental import pallas as pl
from jax.experimental.pallas import tpu as pltpu
from jax.sharding import PartitionSpec as P

F32 = jnp.float32
BF16 = jnp.bfloat16
VMEM = pl.BlockSpec(memory_space=pltpu.VMEM)
SMEM = pl.BlockSpec(memory_space=pltpu.SMEM)
HBM = pl.BlockSpec(memory_space=pltpu.HBM)


def padded_width(cols):
    return -(-(cols + 3) // 16) * 16


def params(mib):
    return pltpu.CompilerParams(vmem_limit_bytes=mib << 20)


def shifted(row, left, right, wide):
    cols, width = row.shape
    middle = jnp.zeros((wide - cols - 2, width), F32)
    base = jnp.concatenate([row.astype(F32), right, middle, left], 0)
    return (
        pltpu.roll(base, 1, 0).astype(BF16),
        base.astype(BF16),
        pltpu.roll(base, wide - 1, 0).astype(BF16),
    )


def fill_window(field, ends, sides, side_rows, window, first, rows):
    total, cols, width = field.shape
    wide = padded_width(cols)
    side_rows[...] = sides[...].astype(F32)

    def put(slot, row, at):
        parts = shifted(row, side_rows[0, pl.ds(at, 1)], side_rows[1, pl.ds(at, 1)], wide)
        start = slot * wide if isinstance(slot, int) else pl.multiple_of(slot * wide, 16)
        for tap, part in enumerate(parts):
            window[pl.ds(start, wide), tap * width : (tap + 1) * width] = part

    low = 0
    if first == 0:
        put(0, ends[0], 0)
        low = 1
    high = rows + 2
    if first + rows == total:
        put(rows + 1, ends[1], total + 1)
        high = rows + 1

    @pl.loop(low, high)
    def _(slot):
        put(slot, field[first + slot - 1], first + slot)


def block_rows(rows):
    return max(n for n in range(1, 6) if rows % n == 0)


def conv_kernel(taps, field, ends, sides, weights, out, window, side_rows, result, sem, *, first, rows):
    total, cols, width = field.shape
    wide = padded_width(cols)
    fill_window(field, ends, sides, side_rows, window, first, rows)
    step = block_rows(rows)

    def rows_of(start, count, which):
        acc = None
        for a in range(3):
            at = start + a
            at = at * wide if isinstance(at, int) else pl.multiple_of(at * wide, 16)
            term = jnp.dot(window[pl.ds(at, count * wide), :], weights[which[a]], preferred_element_type=F32)
            acc = term if acc is None else acc + term
        return acc.reshape(count, wide, width)[:, :cols].astype(BF16)

    @pl.loop(0, rows // step)
    def _(i):
        result[pl.ds(i * step, step)] = rows_of(i * step, step, (0, 1, 2))

    if first == 0:
        result[0:1] = rows_of(0, 1, (taps[0], 1, 2))
    if first + rows == total:
        result[rows - 1 : rows] = rows_of(rows - 1, 1, (0, 1, taps[1]))
    copy = pltpu.make_async_copy(result, out, sem)
    copy.start()
    copy.wait()


def conv(taps, field, ends, sides, weights, first, rows):
    total, cols, width = field.shape
    wide = padded_width(cols)
    return pl.pallas_call(
        functools.partial(conv_kernel, first=first, rows=rows),
        out_shape=jax.ShapeDtypeStruct((rows, cols, width), BF16),
        in_specs=[SMEM, VMEM, VMEM, VMEM, VMEM],
        out_specs=HBM,
        scratch_shapes=[
            pltpu.VMEM(((rows + 2) * wide, 3 * width), BF16),
            pltpu.VMEM((2, total + 2, width), F32),
            pltpu.VMEM((rows, cols, width), BF16),
            pltpu.SemaphoreType.DMA,
        ],
        compiler_params=params(24),
        cost_estimate=pl.CostEstimate(
            flops=18 * rows * wide * width * width, bytes_accessed=4 * rows * wide * width, transcendentals=0
        ),
    )(taps, field, ends, sides, weights)


def weight_kernel(half, field, cot, ends, sides, send, keep, window, side_rows, turned, tap_out):
    total, cols, width = field.shape
    wide = padded_width(cols)
    fill_window(field, ends, sides, side_rows, window, 0, total)
    blank = jnp.zeros((wide - cols, width), F32)
    group = 128 // math.gcd(128, wide)
    span = group * wide

    def chunk(start, count):
        return [part for j in range(count) for part in (cot[start + j].astype(F32), blank)]

    @pl.loop(0, total // group)
    def _(i):
        value = jnp.concatenate(chunk(i * group, group), 0)
        turned[:, pl.ds(pl.multiple_of(i * span, 128), span)] = value.T.astype(BF16)

    rest = total % group
    if rest:
        start = total - rest
        value = jnp.concatenate(chunk(start, rest) + [jnp.zeros((span - rest * wide, width), F32)], 0)
        turned[:, start * wide : start * wide + span] = value.T.astype(BF16)
    mine = half[0]
    part = width // 2
    for a in range(3):
        value = jnp.dot(
            turned[:, : total * wide],
            window[a * wide : (a + total) * wide, :],
            preferred_element_type=F32,
        )
        for b in range(3):
            tap = 3 * a + b
            tap_out[tap] = value[:, b * width : (b + 1) * width].T
            keep[tap * part : (tap + 1) * part] = tap_out[tap, pl.ds(pl.multiple_of(mine * part, part), part)]
            send[tap * part : (tap + 1) * part] = tap_out[tap, pl.ds(pl.multiple_of((1 - mine) * part, part), part)]


def weight_terms(half, field, cot, ends, sides):
    total, cols, width = field.shape
    wide = padded_width(cols)
    group = 128 // math.gcd(128, wide)
    shape = jax.ShapeDtypeStruct((9 * width // 2, width), F32)
    return pl.pallas_call(
        weight_kernel,
        out_shape=(shape, shape),
        in_specs=[SMEM, VMEM, VMEM, VMEM, VMEM],
        out_specs=(VMEM, VMEM),
        scratch_shapes=[
            pltpu.VMEM(((total + 2) * wide, 3 * width), BF16),
            pltpu.VMEM((2, total + 2, width), F32),
            pltpu.VMEM((width, -(-total // group) * group * wide), BF16),
            pltpu.VMEM((9, width, width), F32),
        ],
        compiler_params=params(32),
        cost_estimate=pl.CostEstimate(
            flops=18 * total * wide * width * width, bytes_accessed=4 * total * wide * width, transcendentals=0
        ),
    )(half, field, cot, ends, sides)


def add_blocks(places, terms, blocks, scale=None):
    rows, width = terms[0].shape
    size = rows // blocks
    count = len(places)
    order = jnp.stack(places).astype(jnp.int32)

    def body(where, *refs):
        sources, outs = refs[: len(terms)], refs[len(terms) :]
        for k in range(count):
            at = pl.ds(pl.multiple_of(where[k] * size, 8), size)
            value = sources[0][at]
            for source in sources[1:]:
                value = value + source[at]
            outs[k][...] = value if scale is None else value * scale

    shape = jax.ShapeDtypeStruct((size, width), F32)
    return pl.pallas_call(
        body,
        out_shape=(shape,) * count,
        in_specs=[SMEM] + [VMEM] * len(terms),
        out_specs=(VMEM,) * count,
        compiler_params=params(8),
        cost_estimate=pl.CostEstimate(
            flops=rows * width, bytes_accessed=4 * rows * width * (len(terms) + 1), transcendentals=0
        ),
    )(order, *terms)


def lay_out(places, parts):
    size, width = parts[0].shape
    order = jnp.stack(places).astype(jnp.int32)

    def body(where, *refs):
        for k in range(len(parts)):
            refs[-1][pl.ds(pl.multiple_of(where[k] * size, 8), size)] = refs[k][...]

    return pl.pallas_call(
        body,
        out_shape=jax.ShapeDtypeStruct((size * len(parts), width), F32),
        in_specs=[SMEM] + [VMEM] * len(parts),
        out_specs=VMEM,
        compiler_params=params(8),
        cost_estimate=pl.CostEstimate(
            flops=0, bytes_accessed=8 * size * width * len(parts), transcendentals=0
        ),
    )(order, *parts)


def finish(half, own, other):
    rows, width = own.shape
    part = width // 2
    shape = (rows // part, part, width)

    def body(mine, own, other, out, sems):
        at = mine[0]
        copies = [
            pltpu.make_async_copy(own, out.at[:, at], sems.at[0]),
            pltpu.make_async_copy(other, out.at[:, 1 - at], sems.at[1]),
        ]
        for copy in copies:
            copy.start()
        for copy in copies:
            copy.wait()

    out = pl.pallas_call(
        body,
        out_shape=jax.ShapeDtypeStruct((rows // part, 2, part, width), F32),
        in_specs=[SMEM, VMEM, VMEM],
        out_specs=HBM,
        scratch_shapes=[pltpu.SemaphoreType.DMA((2,))],
        compiler_params=params(8),
    )(half, own.reshape(shape), other.reshape(shape))
    return out.reshape(3, 3, width, width)


def swap(value, axis, mask):
    count = lax.axis_size(axis)
    return lax.ppermute(value, axis, [(i, i ^ mask) for i in range(count)])


def swap_next(value, axis):
    count = lax.axis_size(axis)
    return lax.ppermute(value, axis, [(i, (i + (1 if i % 2 else -1)) % count) for i in range(count)])


def swap_rows(value):
    bands, sectors = lax.axis_size("lat"), lax.axis_size("lon")
    pairs = []
    for band in range(bands):
        for sector in range(sectors):
            if band == 0 or band == bands - 1:
                other = (band, (sector + sectors // 2) % sectors)
            else:
                other = (band + (1 if band % 2 else -1), sector)
            pairs.append((band * sectors + sector, other[0] * sectors + other[1]))
    return lax.ppermute(value, ("lat", "lon"), pairs)


def halos(inputs, cotangent):
    even_band = lax.axis_index("lat") % 2 == 0
    even_sector = lax.axis_index("lon") % 2 == 0
    first = jnp.stack([inputs[0], cotangent[0]])
    last = jnp.stack([inputs[-1], cotangent[-1]])
    near = swap(jnp.where(even_band, last, first), "lat", 1)
    far = swap_rows(jnp.where(even_band, first, last))
    top = jnp.where(even_band, far, near)
    bottom = jnp.where(even_band, near, far)
    ends = jnp.stack([top, bottom], 1)

    def side(column):
        return jnp.stack(
            [
                jnp.concatenate([ends[k, :1, column], field[:, column], ends[k, 1:, column]], 0)
                for k, field in enumerate((inputs, cotangent))
            ]
        )

    first, last = side(0), side(-1)
    near = swap(jnp.where(even_sector, last, first), "lon", 1)
    far = swap_next(jnp.where(even_sector, first, last), "lon")
    left = jnp.where(even_sector, far, near)
    right = jnp.where(even_sector, near, far)
    sides = jnp.stack([left, right], 1)
    return ends, sides


def local(inputs, kernel, cotangent):
    rows, cols, width = inputs.shape
    bands, sectors = lax.axis_size("lat"), lax.axis_size("lon")
    band, sector = lax.axis_index("lat"), lax.axis_index("lon")
    ends, sides = halos(inputs, cotangent)
    half = (sector % 2).astype(jnp.int32)[None]
    send, keep = weight_terms(half, inputs, cotangent, ends[0], sides[0])

    got = swap(send, "lon", 1)
    parts = add_blocks([band ^ m for m in range(bands)], [keep, got], bands)
    got = [swap(parts[m], "lat", m) for m in range(1, bands)]
    place = (sector // 2) % 2
    keep, send = add_blocks([place, 1 - place], [parts[0], *got], 2)
    got = swap(send, "lon", 2)
    factor = 1.0 / math.sqrt(rows * cols * bands * sectors)
    mask = 4
    terms = [keep, got]
    zero = jnp.int32(0)
    while mask < sectors:
        (value,) = add_blocks([zero], terms, 1)
        terms = [value, swap(value, "lon", mask)]
        mask *= 2
    (value,) = add_blocks([zero], terms, 1, factor)
    got = swap(value, "lon", 2)
    value = lay_out([place, 1 - place], [value, got])
    got = [swap(value, "lat", m) for m in range(1, bands)]
    value = lay_out([band ^ m for m in range(bands)], [value, *got])
    got = swap(value, "lon", 1)
    kernel_grad = finish(half, value, got)

    weights = kernel.reshape(3, 3 * width, width)
    flipped = jnp.transpose(kernel[::-1, ::-1], (0, 1, 3, 2)).reshape(3, 3 * width, width)
    plain = jnp.array([0, 2], jnp.int32)
    poles = jnp.stack([jnp.where(band == 0, 2, 0), jnp.where(band == bands - 1, 0, 2)]).astype(jnp.int32)
    outputs = conv(plain, inputs, ends[0], sides[0], weights, 0, rows)
    input_grad = conv(poles, cotangent, ends[1], sides[1], flipped, 0, rows)
    return (outputs, input_grad, kernel_grad)


def solution(mesh):
    in_specs = (P("lat", "lon", None), P(), P("lat", "lon", None))
    out_specs = (P("lat", "lon", None), P("lat", "lon", None), P())
    return jax.shard_map(local, mesh=mesh, in_specs=in_specs, out_specs=out_specs, check_vma=False)
```

time: 272 us -> 108 us (0.40)
  waiting for transfers between devices: 107 us -> 45.7 us
  other arithmetic: 48.6 us -> 1.68 us
  local copies, waits for them, and re-layouts: 54.5 us -> 7.73 us
  Pallas kernels: 0 us -> 37.5 us
  matrix products: 32.5 us -> 0 us
  between operations: 14.3 us -> 0.95 us
    psum x2 -> x0, waiting for transfers between devices: 104 us -> none  [the longest x1 52.4 us: local(): summed = lax.psum(partial_sum, 'lat')]
    reshape x3 -> x0, local copies, waits for them, and re-layouts: 44.5 us -> none  [the longest x2 42.5 us: patches(): return jnp.concatenate(pieces, axis=-1).reshape(rows * cols, -1)]
    ppermute x10 -> x15, waiting for transfers between devices: 2.59 us -> 45.7 us  [the longest x13 41.8 us: swap(): return lax.ppermute(value, axis, [(i, i ^ mask) for i in range(count)])]
    pallas_call x0 -> x10, Pallas kernels: none -> 37.5 us  [the longest x2 24.1 us: conv(): pl.pallas_call(functools.partial(conv_kernel, first=first, rows=rows), ou...]
    unnamed x14 -> x0, other arithmetic: 34.7 us -> none
    dot_general x5 -> x0, matrix products: 32.5 us -> none  [the longest x1 11.6 us: local(): jnp.dot(columns, kernel.reshape(-1, width), preferred_element_type=jnp.fl...]
    concatenate x4 -> x0, other arithmetic: 8.95 us -> none  [the longest x2 5.83 us: patches(): return jnp.concatenate(pieces, axis=-1).reshape(rows * cols, -1)]
    unnamed x25 -> x22, local copies, waits for them, and re-layouts: 5.17 us -> 1.71 us
  transfers between devices with their start and end apart: 12 -> 15, of which waited for: 3 -> 11; matrix products, arithmetic and copies ran while one was open for 48% -> 6% of each run, Pallas kernels for 0% -> 22%
where the time goes in v1:
time: 108 us
  waiting for transfers between devices  45.7 us (42%)
  Pallas kernels  37.5 us (35%)
  starting transfers between devices  14.3 us (13%)
  local copies, waits for them, and re-layouts  7.73 us (7%)
  other arithmetic  1.68 us (2%)
    ppermute x13, waiting for transfers between devices, swap(): return lax.ppermute(value, axis, [(i, i ^ mask) for i in range(count)])  41.8 us
    pallas_call x2, Pallas kernels, conv(): pl.pallas_call(functools.partial(conv_kernel, first=first, rows=rows), ou...  24.1 us
    pallas_call x1, Pallas kernels, weight_terms(): pl.pallas_call(weight_kernel, out_shape=(shape, shape), in_specs=[SMEM, V...  9.44 us
    ppermute x13, starting transfers between devices, swap(): return lax.ppermute(value, axis, [(i, i ^ mask) for i in range(count)])  8.72 us
    ppermute x1, starting transfers between devices, swap_rows(): return lax.ppermute(value, ('lat', 'lon'), pairs)  4.13 us
    ppermute x1, waiting for transfers between devices, swap_next(): lax.ppermute(value, axis, [(i, (i + (1 if i % 2 else -1)) % count) for i...  3.85 us
    transpose x2, local copies, waits for them, and re-layouts, local(): jnp.transpose(kernel[::-1, ::-1], (0, 1, 3, 2)).reshape(3, 3 * width, width)  2.66 us
    slice x2, local copies, waits for them, and re-layouts, side(): field[:, column]  2.5 us
  transfers between devices with their start and end apart: 15, of which 11 were waited for; matrix products, arithmetic and copies ran while one was open for 6% of the time, Pallas kernels for 22%

profile of v1, /device:TPU:0, one launch (start us, length us, event | category | flops | bytes accessed | tf_op | source)
XLA Modules:
  0.0 107.8 jit_solution(18085018673419585139)
XLA Ops:
  0.6 0.8 fusion.10
  1.5 4.1 %collective-permute-start = (bf16[2,45,256]{2,1,0:T(8,128)(2,1)S(1)}, bf16[2,45,256]{2,1,0:T(8,128)(2,1)S(1)}, u32[]{:S(2)}, u32[]{:S(2)}) collective-permute-start(bf16[2,45,256]{2,1,0:T(8,128)(2,1)S(1)} %get-tuple-element.39), channel_id=1, source_target_pairs={{0,4},{1,5},{2,6},{3,7},{4,0},{5,1},{6,2},{7,3},{8,16},{9,17},{10,... | collective-permute-start | bytes 138248 | tf_op jit(solution)/shard_map/ppermute | solution.py:269
  6.0 1.2 %fusion.8 = (bf16[90,1,256]{2,1,0:T(2,128)(2,1)S(1)}, bf16[90,1,256]{2,1,0:T(2,128)(2,1)S(1)}) fusion(bf16[90,45,256]{2,1,0:T(8,128)(2,1)} %field.5), kind=kLoop, calls=%fused_computation.47 | loop fusion | bytes 184320 | tf_op jit(solution)/shard_map/slice | solution.py:286
  7.2 1.3 %fusion.9 = (bf16[90,1,256]{2,1,0:T(2,128)(2,1)S(1)}, bf16[90,1,256]{2,1,0:T(2,128)(2,1)S(1)}) fusion(bf16[90,45,256]{2,1,0:T(8,128)(2,1)} %cot.1), kind=kLoop, calls=%fused_computation.48 | loop fusion | bytes 184320 | tf_op jit(solution)/shard_map/slice | solution.py:286
  8.6 1.1 %collective-permute-done.1 = bf16[2,45,256]{2,1,0:T(8,128)(2,1)S(1)} collective-permute-done((bf16[2,45,256]{2,1,0:T(8,128)(2,1)S(1)}, bf16[2,45,256]{2,1,0:T(8,128)(2,1)S(1)}, u32[]{:S(2)}, u32[]{:S(2)}) %collective-permute-start.1) | collective-permute-done | bytes 46112 | tf_op jit(solution)/shard_map/ppermute | solution.py:251
  9.9 1.5 %collective-permute-start.2 = (bf16[2,92,256]{2,1,0:T(8,128)(2,1)S(1)}, bf16[2,92,256]{2,1,0:T(8,128)(2,1)S(1)}, u32[]{:S(2)}, u32[]{:S(2)}) collective-permute-start(bf16[2,92,256]{2,1,0:T(8,128)(2,1)S(1)} %get-tuple-element.32), channel_id=1, source_target_pairs={{0,7},{1,2},{2,1},{3,4},{4,3},{5,6},{6,5},{7,0},{8,15},{9,10},{10,... | collective-permute-start | bytes 282632 | tf_op jit(solution)/shard_map/ppermute | solution.py:256
  11.6 0.6 fusion.5
  12.3 3.8 %collective-permute-done.2 = bf16[2,92,256]{2,1,0:T(8,128)(2,1)S(1)} collective-permute-done((bf16[2,92,256]{2,1,0:T(8,128)(2,1)S(1)}, bf16[2,92,256]{2,1,0:T(8,128)(2,1)S(1)}, u32[]{:S(2)}, u32[]{:S(2)}) %collective-permute-start.2) | collective-permute-done | bytes 94240 | tf_op jit(solution)/shard_map/ppermute | solution.py:256
  16.1 0.7 fusion.2
  16.8 1.7 %copy-done.9 = bf16[90,45,256]{2,1,0:T(8,128)(2,1)S(1)} copy-done((bf16[90,45,256]{2,1,0:T(8,128)(2,1)S(1)}, bf16[90,45,256]{2,1,0:T(8,128)(2,1)}, u32[]{:S(2)}) %copy-start.9) | copy-done | bytes 2073624
  18.5 9.4 %shard_map.69 = (f32[1152,256]{1,0:T(8,128)}, f32[1152,256]{1,0:T(8,128)S(1)}) custom-call(s32[1]{0:T(128)} %bitcast.31.half.mine, bf16[90,45,256]{2,1,0:T(8,128)(2,1)S(1)} %copy-done.7, bf16[90,45,256]{2,1,0:T(8,128)(2,1)S(1)} %copy-done.9, bf16[2,45,256]{2,1,0:T(8,128)(2,1)S(1)} %get-tuple-element.34.ends, bf16[2,92,256]{2,1,0:T(8,128)(2,1)S(1)} %get-tuple-element.28.sides), custom_call_target="tpu_custom_call" | custom-call | flops 5096079360 | bytes 4423680 | tf_op jit(solution)/shard_map/pallas_call | solution.py:156
  28.0 3.0 %collective-permute-done.4.refs_1_ = f32[1152,256]{1,0:T(8,128)S(1)} collective-permute-done((f32[1152,256]{1,0:T(8,128)}, f32[1152,256]{1,0:T(8,128)S(1)}, u32[]{:S(2)}, u32[]{:S(2)}) %collective-permute-start.4) | collective-permute-done | bytes 1179680 | tf_op jit(solution)/shard_map/ppermute | solution.py:251
  31.0 0.7 shard_map.70
  31.6 1.1 %collective-permute-start.5 = (f32[288,256]{1,0:T(8,128)S(1)}, f32[288,256]{1,0:T(8,128)S(1)}, u32[]{:S(2)}, u32[]{:S(2)}) collective-permute-start(f32[288,256]{1,0:T(8,128)S(1)} %get-tuple-element.14), channel_id=1, source_target_pairs={{0,8},{8,0},{16,24},{24,16},{1,9},{9,1},{17,25},{25,17},{2,10},{10... | collective-permute-start | bytes 884744 | tf_op jit(solution)/shard_map/ppermute | solution.py:251
  32.8 1.8 %collective-permute-start.6 = (f32[288,256]{1,0:T(8,128)S(1)}, f32[288,256]{1,0:T(8,128)S(1)}, u32[]{:S(2)}, u32[]{:S(2)}) collective-permute-start(f32[288,256]{1,0:T(8,128)S(1)} %get-tuple-element.15), channel_id=1, source_target_pairs={{0,16},{8,24},{16,0},{24,8},{1,17},{9,25},{17,1},{25,9},{2,18},{10... | collective-permute-start | bytes 884744 | tf_op jit(solution)/shard_map/ppermute | solution.py:251
  34.5 0.7 collective-permute-start.7
  35.3 6.3 %collective-permute-done.5.refs_1_ = f32[288,256]{1,0:T(8,128)S(1)} collective-permute-done((f32[288,256]{1,0:T(8,128)S(1)}, f32[288,256]{1,0:T(8,128)S(1)}, u32[]{:S(2)}, u32[]{:S(2)}) %collective-permute-start.5) | collective-permute-done | bytes 294944 | tf_op jit(solution)/shard_map/ppermute | solution.py:251
  41.6 5.6 %collective-permute-done.6.refs_2_ = f32[288,256]{1,0:T(8,128)S(1)} collective-permute-done((f32[288,256]{1,0:T(8,128)S(1)}, f32[288,256]{1,0:T(8,128)S(1)}, u32[]{:S(2)}, u32[]{:S(2)}) %collective-permute-start.6) | collective-permute-done | bytes 294944 | tf_op jit(solution)/shard_map/ppermute | solution.py:251
  47.1 0.8 collective-permute-done.7.refs_3_
  48.9 4.9 %collective-permute-done.8.refs_1_ = f32[144,256]{1,0:T(8,128)S(1)} collective-permute-done((f32[144,256]{1,0:T(8,128)S(1)}, f32[144,256]{1,0:T(8,128)S(1)}, u32[]{:S(2)}, u32[]{:S(2)}) %collective-permute-start.8) | collective-permute-done | bytes 147488 | tf_op jit(solution)/shard_map/ppermute | solution.py:251
  54.3 7.2 %collective-permute-done.9.refs_1_ = f32[144,256]{1,0:T(8,128)S(1)} collective-permute-done((f32[144,256]{1,0:T(8,128)S(1)}, f32[144,256]{1,0:T(8,128)S(1)}, u32[]{:S(2)}, u32[]{:S(2)}) %collective-permute-start.9) | collective-permute-done | bytes 147488 | tf_op jit(solution)/shard_map/ppermute | solution.py:251
  61.6 5.1 %collective-permute-done.10.refs_1_ = f32[144,256]{1,0:T(8,128)S(1)} collective-permute-done((f32[144,256]{1,0:T(8,128)S(1)}, f32[144,256]{1,0:T(8,128)S(1)}, u32[]{:S(2)}, u32[]{:S(2)}) %collective-permute-start.10) | collective-permute-done | bytes 147488 | tf_op jit(solution)/shard_map/ppermute | solution.py:251
  67.3 1.5 %collective-permute-start.11 = (f32[288,256]{1,0:T(8,128)S(1)}, f32[288,256]{1,0:T(8,128)S(1)}, u32[]{:S(2)}, u32[]{:S(2)}) collective-permute-start(f32[288,256]{1,0:T(8,128)S(1)} %shard_map.74.refs_0_), channel_id=1, source_target_pairs={{0,8},{8,0},{16,24},{24,16},{1,9},{9,1},{17,25},{25,17},{2,10},{10... | collective-permute-start | bytes 884744 | tf_op jit(solution)/shard_map/ppermute | solution.py:251
  69.2 1.7 %collective-permute-start.13 = (f32[288,256]{1,0:T(8,128)S(1)}, f32[288,256]{1,0:T(8,128)S(1)}, u32[]{:S(2)}, u32[]{:S(2)}) collective-permute-start(f32[288,256]{1,0:T(8,128)S(1)} %shard_map.74.refs_0_), channel_id=1, source_target_pairs={{0,24},{8,16},{16,8},{24,0},{1,25},{9,17},{17,9},{25,1},{2,26},{10... | collective-permute-start | bytes 884744 | tf_op jit(solution)/shard_map/ppermute | solution.py:251
  70.9 1.1 %reverse_bitcast_fusion = bf16[3,3,256,256]{2,3,1,0:T(8,128)(2,1)} fusion(bf16[3,3,256,256]{3,2,1,0:T(8,128)(2,1)S(1)} %copy-done), kind=kLoop, calls=%fused_computation | loop fusion | bytes 2359296 | tf_op jit(solution)/shard_map/transpose | solution.py:331
  72.0 1.6 %copy.13 = bf16[3,3,256,256]{3,2,1,0:T(8,128)(2,1)S(1)} copy(bf16[3,3,256,256]{2,3,1,0:T(8,128)(2,1)} %reverse_bitcast_fusion) | data formatting | bytes 2359296 | tf_op jit(solution)/shard_map/transpose | solution.py:331
  73.6 3.5 %collective-permute-done.11.refs_1_ = f32[288,256]{1,0:T(8,128)S(1)} collective-permute-done((f32[288,256]{1,0:T(8,128)S(1)}, f32[288,256]{1,0:T(8,128)S(1)}, u32[]{:S(2)}, u32[]{:S(2)}) %collective-permute-start.11) | collective-permute-done | bytes 294944 | tf_op jit(solution)/shard_map/ppermute | solution.py:251
  77.1 4.2 %collective-permute-done.12.refs_2_ = f32[288,256]{1,0:T(8,128)S(1)} collective-permute-done((f32[288,256]{1,0:T(8,128)S(1)}, f32[288,256]{1,0:T(8,128)S(1)}, u32[]{:S(2)}, u32[]{:S(2)}) %collective-permute-start.12) | collective-permute-done | bytes 294944 | tf_op jit(solution)/shard_map/ppermute | solution.py:251
  81.4 0.6 shard_map.75
  82.2 12.1 %shard_map.67 = bf16[90,45,256]{2,1,0:T(8,128)(2,1)} custom-call(s32[2]{0:T(128)S(1)} %iota_multiply_fusion.taps, bf16[90,45,256]{2,1,0:T(8,128)(2,1)S(1)} %copy-done.8, bf16[2,45,256]{2,1,0:T(8,128)(2,1)S(1)} %copy-done.6, bf16[2,92,256]{2,1,0:T(8,128)(2,1)S(1)} %copy-done.3, bf16[3,768,256]{2,1,0:T(8,128)(2,1)S(1)} %bitcast.71), custom_call_target="tpu_custom_call" | custom-call | flops 5096079360 | bytes 4423680 | tf_op jit(solution)/shard_map/pallas_call | solution.py:97
  94.3 12.1 %shard_map.68 = bf16[90,45,256]{2,1,0:T(8,128)(2,1)} custom-call(s32[2]{0:T(128)S(1)} %pad_add_fusion.taps, bf16[90,45,256]{2,1,0:T(8,128)(2,1)S(1)} %copy-done.10, bf16[2,45,256]{2,1,0:T(8,128)(2,1)S(1)} %copy-done.4, bf16[2,92,256]{2,1,0:T(8,128)(2,1)S(1)} %copy-done.1, bf16[3,768,256]{2,1,0:T(8,128)(2,1)S(1)} %bitcast.72), custom_call_target="tpu_custom_call" | custom-call | flops 5096079360 | bytes 4423680 | tf_op jit(solution)/shard_map/pallas_call | solution.py:97
  106.4 1.4 %shard_map.76 = f32[9,2,128,256]{3,2,1,0:T(8,128)} custom-call(s32[1]{0:T(128)} %bitcast.31.half.mine, f32[9,128,256]{2,1,0:T(8,128)S(1)} %bitcast.69, f32[9,128,256]{2,1,0:T(8,128)S(1)} %bitcast.70), custom_call_target="tpu_custom_call" | custom-call | tf_op jit(solution)/shard_map/pallas_call | solution.py:238
  (53 shorter events, 3.7 us)
Async XLA Ops:
  1.5 7.1 %collective-permute-start = (bf16[2,45,256]{2,1,0:T(8,128)(2,1)S(1)}, bf16[2,45,256]{2,1,0:T(8,128)(2,1)S(1)}, u32[]{:S(2)}, u32[]{:S(2)}) collective-permute-start(bf16[2,45,256]{2,1,0:T(8,128)(2,1)S(1)} %get-tuple-element.39), channel_id=1, source_target_pairs={{0,4},{1,5},{2,6},{3,7},{4,0},{5,1},{6,2},{7,3},{8,16},{9,17},{10,... | collective-permute-start | bytes 138248 | tf_op jit(solution)/shard_map/ppermute | solution.py:269
  5.6 4.1 %collective-permute-start.1 = (bf16[2,45,256]{2,1,0:T(8,128)(2,1)S(1)}, bf16[2,45,256]{2,1,0:T(8,128)(2,1)S(1)}, u32[]{:S(2)}, u32[]{:S(2)}) collective-permute-start(bf16[2,45,256]{2,1,0:T(8,128)(2,1)S(1)} %get-tuple-element.38), channel_id=1, source_target_pairs={{0,8},{8,0},{16,24},{24,16},{1,9},{9,1},{17,25},{25,17},{2,10},{10... | collective-permute-start | bytes 138248 | tf_op jit(solution)/shard_map/ppermute | solution.py:251
  8.5 8.3 %copy-start.7 = (bf16[90,45,256]{2,1,0:T(8,128)(2,1)S(1)}, bf16[90,45,256]{2,1,0:T(8,128)(2,1)}, u32[]{:S(2)}) copy-start(bf16[90,45,256]{2,1,0:T(8,128)(2,1)} %field.5) | copy-start | bytes 6220804
  9.9 6.2 %collective-permute-start.2 = (bf16[2,92,256]{2,1,0:T(8,128)(2,1)S(1)}, bf16[2,92,256]{2,1,0:T(8,128)(2,1)S(1)}, u32[]{:S(2)}, u32[]{:S(2)}) collective-permute-start(bf16[2,92,256]{2,1,0:T(8,128)(2,1)S(1)} %get-tuple-element.32), channel_id=1, source_target_pairs={{0,7},{1,2},{2,1},{3,4},{4,3},{5,6},{6,5},{7,0},{8,15},{9,10},{10,... | collective-permute-start | bytes 282632 | tf_op jit(solution)/shard_map/ppermute | solution.py:256
  11.3 4.8 %collective-permute-start.3 = (bf16[2,92,256]{2,1,0:T(8,128)(2,1)S(1)}, bf16[2,92,256]{2,1,0:T(8,128)(2,1)S(1)}, u32[]{:S(2)}, u32[]{:S(2)}) collective-permute-start(bf16[2,92,256]{2,1,0:T(8,128)(2,1)S(1)} %get-tuple-element.31), channel_id=1, source_target_pairs={{0,1},{1,0},{2,3},{3,2},{4,5},{5,4},{6,7},{7,6},{8,9},{9,8},{10,11... | collective-permute-start | bytes 282632 | tf_op jit(solution)/shard_map/ppermute | solution.py:251
  12.3 15.6 %copy-start.5 = (bf16[2,45,256]{2,1,0:T(8,128)(2,1)}, bf16[2,45,256]{2,1,0:T(8,128)(2,1)S(1)}, u32[]{:S(2)}) copy-start(bf16[2,45,256]{2,1,0:T(8,128)(2,1)S(1)} %get-tuple-element.34.ends) | copy-start | bytes 138244
  16.8 11.1 %copy-start.2 = (bf16[2,92,256]{2,1,0:T(8,128)(2,1)}, bf16[2,92,256]{2,1,0:T(8,128)(2,1)S(1)}, u32[]{:S(2)}) copy-start(bf16[2,92,256]{2,1,0:T(8,128)(2,1)S(1)} %get-tuple-element.28.sides) | copy-start | bytes 282628
  16.8 1.7 %copy-start.9 = (bf16[90,45,256]{2,1,0:T(8,128)(2,1)S(1)}, bf16[90,45,256]{2,1,0:T(8,128)(2,1)}, u32[]{:S(2)}) copy-start(bf16[90,45,256]{2,1,0:T(8,128)(2,1)} %cot.1) | copy-start | bytes 6220804
  27.9 3.1 %collective-permute-start.4 = (f32[1152,256]{1,0:T(8,128)}, f32[1152,256]{1,0:T(8,128)S(1)}, u32[]{:S(2)}, u32[]{:S(2)}) collective-permute-start(f32[1152,256]{1,0:T(8,128)} %get-tuple-element.12), channel_id=1, source_target_pairs={{0,1},{1,0},{2,3},{3,2},{4,5},{5,4},{6,7},{7,6},{8,9},{9,8},{10,11... | collective-permute-start | bytes 3538952 | tf_op jit(solution)/shard_map/ppermute | solution.py:251
  31.6 9.9 %collective-permute-start.5 = (f32[288,256]{1,0:T(8,128)S(1)}, f32[288,256]{1,0:T(8,128)S(1)}, u32[]{:S(2)}, u32[]{:S(2)}) collective-permute-start(f32[288,256]{1,0:T(8,128)S(1)} %get-tuple-element.14), channel_id=1, source_target_pairs={{0,8},{8,0},{16,24},{24,16},{1,9},{9,1},{17,25},{25,17},{2,10},{10... | collective-permute-start | bytes 884744 | tf_op jit(solution)/shard_map/ppermute | solution.py:251
  32.8 14.4 %collective-permute-start.6 = (f32[288,256]{1,0:T(8,128)S(1)}, f32[288,256]{1,0:T(8,128)S(1)}, u32[]{:S(2)}, u32[]{:S(2)}) collective-permute-start(f32[288,256]{1,0:T(8,128)S(1)} %get-tuple-element.15), channel_id=1, source_target_pairs={{0,16},{8,24},{16,0},{24,8},{1,17},{9,25},{17,1},{25,9},{2,18},{10... | collective-permute-start | bytes 884744 | tf_op jit(solution)/shard_map/ppermute | solution.py:251
  34.5 13.4 %collective-permute-start.7 = (f32[288,256]{1,0:T(8,128)S(1)}, f32[288,256]{1,0:T(8,128)S(1)}, u32[]{:S(2)}, u32[]{:S(2)}) collective-permute-start(f32[288,256]{1,0:T(8,128)S(1)} %get-tuple-element.16), channel_id=1, source_target_pairs={{0,24},{8,16},{16,8},{24,0},{1,25},{9,17},{17,9},{25,1},{2,26},{10... | collective-permute-start | bytes 884744 | tf_op jit(solution)/shard_map/ppermute | solution.py:251
  48.0 22.9 %copy-start = (bf16[3,3,256,256]{3,2,1,0:T(8,128)(2,1)S(1)}, bf16[3,3,256,256]{3,2,1,0:T(8,128)(2,1)}, u32[]{:S(2)}) copy-start(bf16[3,3,256,256]{3,2,1,0:T(8,128)(2,1)} %param.5) | copy-start | bytes 3538948
  48.6 5.2 %collective-permute-start.8 = (f32[144,256]{1,0:T(8,128)S(1)}, f32[144,256]{1,0:T(8,128)S(1)}, u32[]{:S(2)}, u32[]{:S(2)}) collective-permute-start(f32[144,256]{1,0:T(8,128)S(1)} %get-tuple-element.18), channel_id=1, source_target_pairs={{0,2},{1,3},{2,0},{3,1},{4,6},{5,7},{6,4},{7,5},{8,10},{9,11},{10,... | collective-permute-start | bytes 442376 | tf_op jit(solution)/shard_map/ppermute | solution.py:251
  53.8 7.7 %collective-permute-start.9 = (f32[144,256]{1,0:T(8,128)S(1)}, f32[144,256]{1,0:T(8,128)S(1)}, u32[]{:S(2)}, u32[]{:S(2)}) collective-permute-start(f32[144,256]{1,0:T(8,128)S(1)} %shard_map.72.refs_0_), channel_id=1, source_target_pairs={{0,4},{1,5},{2,6},{3,7},{4,0},{5,1},{6,2},{7,3},{8,12},{9,13},{10,... | collective-permute-start | bytes 442376 | tf_op jit(solution)/shard_map/ppermute | solution.py:251
  61.6 5.2 %collective-permute-start.10 = (f32[144,256]{1,0:T(8,128)S(1)}, f32[144,256]{1,0:T(8,128)S(1)}, u32[]{:S(2)}, u32[]{:S(2)}) collective-permute-start(f32[144,256]{1,0:T(8,128)S(1)} %shard_map.73.refs_0_), channel_id=1, source_target_pairs={{0,2},{1,3},{2,0},{3,1},{4,6},{5,7},{6,4},{7,5},{8,10},{9,11},{10,... | collective-permute-start | bytes 442376 | tf_op jit(solution)/shard_map/ppermute | solution.py:251
  67.3 9.8 %collective-permute-start.11 = (f32[288,256]{1,0:T(8,128)S(1)}, f32[288,256]{1,0:T(8,128)S(1)}, u32[]{:S(2)}, u32[]{:S(2)}) collective-permute-start(f32[288,256]{1,0:T(8,128)S(1)} %shard_map.74.refs_0_), channel_id=1, source_target_pairs={{0,8},{8,0},{16,24},{24,16},{1,9},{9,1},{17,25},{25,17},{2,10},{10... | collective-permute-start | bytes 884744 | tf_op jit(solution)/shard_map/ppermute | solution.py:251
  68.8 12.6 %collective-permute-start.12 = (f32[288,256]{1,0:T(8,128)S(1)}, f32[288,256]{1,0:T(8,128)S(1)}, u32[]{:S(2)}, u32[]{:S(2)}) collective-permute-start(f32[288,256]{1,0:T(8,128)S(1)} %shard_map.74.refs_0_), channel_id=1, source_target_pairs={{0,16},{8,24},{16,0},{24,8},{1,17},{9,25},{17,1},{25,9},{2,18},{10... | collective-permute-start | bytes 884744 | tf_op jit(solution)/shard_map/ppermute | solution.py:251
  69.2 12.1 %collective-permute-start.13 = (f32[288,256]{1,0:T(8,128)S(1)}, f32[288,256]{1,0:T(8,128)S(1)}, u32[]{:S(2)}, u32[]{:S(2)}) collective-permute-start(f32[288,256]{1,0:T(8,128)S(1)} %shard_map.74.refs_0_), channel_id=1, source_target_pairs={{0,24},{8,16},{16,8},{24,0},{1,25},{9,17},{17,9},{25,1},{2,26},{10... | collective-permute-start | bytes 884744 | tf_op jit(solution)/shard_map/ppermute | solution.py:251
  73.6 8.6 %copy-start.3 = (bf16[2,92,256]{2,1,0:T(8,128)(2,1)S(1)}, bf16[2,92,256]{2,1,0:T(8,128)(2,1)}, u32[]{:S(2)}) copy-start(bf16[2,92,256]{2,1,0:T(8,128)(2,1)} %copy-done.2) | copy-start | bytes 282628
  73.6 8.6 %copy-start.6 = (bf16[2,45,256]{2,1,0:T(8,128)(2,1)S(1)}, bf16[2,45,256]{2,1,0:T(8,128)(2,1)}, u32[]{:S(2)}) copy-start(bf16[2,45,256]{2,1,0:T(8,128)(2,1)} %copy-done.5) | copy-start | bytes 138244
  73.6 8.6 %copy-start.8 = (bf16[90,45,256]{2,1,0:T(8,128)(2,1)S(1)}, bf16[90,45,256]{2,1,0:T(8,128)(2,1)}, u32[]{:S(2)}) copy-start(bf16[90,45,256]{2,1,0:T(8,128)(2,1)} %field.5) | copy-start | bytes 6220804
  82.0 24.4 %collective-permute-start.14 = (f32[1152,256]{1,0:T(8,128)S(1)}, f32[1152,256]{1,0:T(8,128)S(1)}, u32[]{:S(2)}, u32[]{:S(2)}) collective-permute-start(f32[1152,256]{1,0:T(8,128)S(1)} %shard_map.75), channel_id=1, source_target_pairs={{0,1},{1,0},{2,3},{3,2},{4,5},{5,4},{6,7},{7,6},{8,9},{9,8},{10,11... | collective-permute-start | bytes 3538952 | tf_op jit(solution)/shard_map/ppermute | solution.py:251
  82.2 12.1 %copy-start.1 = (bf16[2,92,256]{2,1,0:T(8,128)(2,1)S(1)}, bf16[2,92,256]{2,1,0:T(8,128)(2,1)}, u32[]{:S(2)}) copy-start(bf16[2,92,256]{2,1,0:T(8,128)(2,1)} %get-tuple-element.27.sides) | copy-start | bytes 282628
  82.2 12.1 %copy-start.4 = (bf16[2,45,256]{2,1,0:T(8,128)(2,1)S(1)}, bf16[2,45,256]{2,1,0:T(8,128)(2,1)}, u32[]{:S(2)}) copy-start(bf16[2,45,256]{2,1,0:T(8,128)(2,1)} %get-tuple-element.33.ends) | copy-start | bytes 138244
  82.2 12.1 %copy-start.10 = (bf16[90,45,256]{2,1,0:T(8,128)(2,1)S(1)}, bf16[90,45,256]{2,1,0:T(8,128)(2,1)}, u32[]{:S(2)}) copy-start(bf16[90,45,256]{2,1,0:T(8,128)(2,1)} %cot.1) | copy-start | bytes 6220804

commit v2 on v1

v2 whole, which is shorter than its diff:
```python
import math

import jax
import jax.numpy as jnp
from jax import lax
from jax.experimental import pallas as pl
from jax.experimental.pallas import tpu as pltpu
from jax.sharding import PartitionSpec as P


F32 = jnp.float32
BF16 = jnp.bfloat16
HALF = jnp.float16
VMEM = pl.BlockSpec(memory_space=pltpu.VMEM)
SMEM = pl.BlockSpec(memory_space=pltpu.SMEM)
HBM = pl.BlockSpec(memory_space=pltpu.HBM)


def padded_width(cols):
    return -(-(cols + 3) // 16) * 16


def params(mib):
    return pltpu.CompilerParams(vmem_limit_bytes=mib << 20)


def shifted(row, left, right, wide):
    cols, width = row.shape
    middle = jnp.zeros((wide - cols - 2, width), F32)
    base = jnp.concatenate([row.astype(F32), right, middle, left], 0)
    return (
        pltpu.roll(base, 1, 0).astype(BF16),
        base.astype(BF16),
        pltpu.roll(base, wide - 1, 0).astype(BF16),
    )


def fill_window(field, ends, sides, side_rows, window, first, rows):
    total, cols, width = field.shape
    wide = padded_width(cols)
    side_rows[...] = sides[...].astype(F32)

    def put(slot, row, at):
        parts = shifted(row, side_rows[0, pl.ds(at, 1)], side_rows[1, pl.ds(at, 1)], wide)
        start = slot * wide if isinstance(slot, int) else pl.multiple_of(slot * wide, 16)
        for tap, part in enumerate(parts):
            window[pl.ds(start, wide), tap * width : (tap + 1) * width] = part

    low = 0
    if first == 0:
        put(0, ends[0], 0)
        low = 1
    high = rows + 2
    if first + rows == total:
        put(rows + 1, ends[1], total + 1)
        high = rows + 1

    @pl.loop(low, high)
    def _(slot):
        put(slot, field[first + slot - 1], first + slot)


def block_rows(rows):
    return max(n for n in range(1, 6) if rows % n == 0)


def conv_rows(taps, window, weights, result, out, sem, cols, first, rows, total):
    width = weights.shape[-1]
    wide = padded_width(cols)
    step = block_rows(rows)

    def rows_of(start, count, which):
        acc = None
        for a in range(3):
            at = start + a
            at = at * wide if isinstance(at, int) else pl.multiple_of(at * wide, 16)
            term = jnp.dot(window[pl.ds(at, count * wide), :], weights[which[a]], preferred_element_type=F32)
            acc = term if acc is None else acc + term
        return acc.reshape(count, wide, width)[:, :cols].astype(BF16)

    def write(at):
        return pltpu.make_async_copy(result.at[pl.ds(at, step)], out.at[pl.ds(first + at, step)], sem)

    count = rows // step
    low = int(first == 0 and taps is not None)
    high = count - int(first + rows == total and taps is not None)

    @pl.loop(low, high)
    def _(i):
        result[pl.ds(i * step, step)] = rows_of(i * step, step, (0, 1, 2))
        write(i * step).start()

    if low:
        result[0:step] = rows_of(0, step, (0, 1, 2))
        result[0:1] = rows_of(0, 1, (taps[0], 1, 2))
        write(0).start()
    if high < count:
        result[rows - step : rows] = rows_of(rows - step, step, (0, 1, 2))
        result[rows - 1 : rows] = rows_of(rows - 1, 1, (0, 1, taps[1]))
        write(rows - step).start()
    pltpu.make_async_copy(result, out.at[pl.ds(first, rows)], sem).wait()


def conv_cost(rows, cols, width):
    wide = padded_width(cols)
    return pl.CostEstimate(
        flops=18 * rows * wide * width * width, bytes_accessed=4 * rows * wide * width, transcendentals=0
    )


def backward(taps, field, ends, sides, weights, first, rows, out=None):
    total, cols, width = field.shape
    wide = padded_width(cols)
    more = [] if out is None else [out]

    def body(taps, field, ends, sides, weights, *rest):
        out, window, side_rows, result, sem = rest[-5:]
        fill_window(field, ends, sides, side_rows, window, first, rows)
        conv_rows(taps, window, weights, result, out, sem, cols, first, rows, total)

    return pl.pallas_call(
        body,
        out_shape=jax.ShapeDtypeStruct((total, cols, width), BF16),
        in_specs=[SMEM, VMEM, VMEM, VMEM, VMEM] + [HBM] * len(more),
        out_specs=HBM,
        scratch_shapes=[
            pltpu.VMEM(((rows + 2) * wide, 3 * width), BF16),
            pltpu.VMEM((2, total + 2, width), F32),
            pltpu.VMEM((rows, cols, width), BF16),
            pltpu.SemaphoreType.DMA,
        ],
        input_output_aliases={5: 0} if more else {},
        compiler_params=params(20),
        cost_estimate=conv_cost(rows, cols, width),
    )(taps, field, ends, sides, weights, *more)


def patch(window, ends, sides):
    _, cols, width = ends.shape
    wide = padded_width(cols)
    total = sides.shape[1] - 2

    def body(old, ends, sides, window, side_rows):
        side_rows[...] = sides[...].astype(F32)
        for slot, k in ((0, 0), (total + 1, 1)):
            parts = shifted(ends[k], side_rows[0, slot : slot + 1], side_rows[1, slot : slot + 1], wide)
            for tap, part in enumerate(parts):
                window[slot * wide : (slot + 1) * wide, tap * width : (tap + 1) * width] = part
        place = lax.broadcasted_iota(jnp.int32, (16, width), 0)
        last = (cols - 1) // 16 * 16

        @pl.loop(1, total + 1)
        def _(slot):
            for k, (offset, at) in enumerate(((0, 0), (last, cols - 1 - last))):
                where = (pl.ds(pl.multiple_of(slot * wide + offset, 16), 16), slice(2 * k * width, (2 * k + 1) * width))
                value = window[where].astype(F32)
                window[where] = jnp.where(place == at, side_rows[k, pl.ds(slot, 1)], value).astype(BF16)

    return pl.pallas_call(
        body,
        out_shape=jax.ShapeDtypeStruct(window.shape, BF16),
        in_specs=[VMEM] * 3,
        out_specs=VMEM,
        scratch_shapes=[pltpu.VMEM((2, total + 2, width), F32)],
        input_output_aliases={0: 0},
        compiler_params=params(8),
        cost_estimate=pl.CostEstimate(flops=0, bytes_accessed=256 * total * width, transcendentals=0),
    )(window, ends, sides)


def forward(window, weights, shape, first, rows, out=None):
    total, cols, width = shape
    wide = padded_width(cols)
    more = [] if out is None else [out]

    def body(window, weights, *rest):
        out, result, sem = rest[-3:]
        view = window.at[first * wide : (first + rows + 2) * wide]
        conv_rows(None, view, weights, result, out, sem, cols, first, rows, total)

    return pl.pallas_call(
        body,
        out_shape=jax.ShapeDtypeStruct(shape, BF16),
        in_specs=[VMEM, VMEM] + [HBM] * len(more),
        out_specs=HBM,
        scratch_shapes=[pltpu.VMEM((rows, cols, width), BF16), pltpu.SemaphoreType.DMA],
        input_output_aliases={2: 0} if more else {},
        compiler_params=params(8),
        cost_estimate=conv_cost(rows, cols, width),
    )(window, weights, *more)


def turn_group(wide):
    return 128 // math.gcd(128, wide)


def row_messages(rows, inputs, cotangent):
    _, cols, width = inputs.shape

    def body(rows, inputs, cotangent, near, far, sem):
        copies = [
            pltpu.make_async_copy(field.at[rows[k]], out.at[j], sem.at[2 * k + j])
            for k, out in enumerate((near, far))
            for j, field in enumerate((inputs, cotangent))
        ]
        for copy in copies:
            copy.start()
        for copy in copies:
            copy.wait()

    shape = jax.ShapeDtypeStruct((2, cols, width), BF16)
    return pl.pallas_call(
        body,
        out_shape=(shape, shape),
        in_specs=[SMEM, HBM, HBM],
        out_specs=(VMEM, VMEM),
        scratch_shapes=[pltpu.SemaphoreType.DMA((4,))],
        compiler_params=params(8),
    )(rows, inputs, cotangent)


def fetch_chunk(total):
    return max(n for n in range(1, 33) if total % n == 0)


def begin_kernel(field_hbm, cot_hbm, columns, window, turned, taps, cot, field, column_rows, sems):
    total, cols, width = field.shape
    wide = padded_width(cols)
    part = fetch_chunk(total)
    copies = [
        pltpu.make_async_copy(source.at[pl.ds(at, part)], target.at[pl.ds(at, part)], sems.at[at // part, j])
        for at in range(0, total, part)
        for j, (source, target) in enumerate(((cot_hbm, cot), (field_hbm, field)))
    ]
    for copy in copies:
        copy.start()
    empty = jnp.zeros((1, width), F32)
    blank = jnp.zeros((wide - cols, width), F32)
    group = turn_group(wide)
    span = group * wide
    for k in range(3):
        window[0:wide, k * width : (k + 1) * width] = jnp.zeros((wide, width), BF16)
        window[(total + 1) * wide : (total + 2) * wide, k * width : (k + 1) * width] = jnp.zeros((wide, width), BF16)

    for at in range(0, total, part):
        copies[2 * (at // part)].wait()
        copies[2 * (at // part) + 1].wait()

        @pl.loop(at, at + part)
        def _(r):
            row, other = field[r], cot[r]
            start = pl.multiple_of((r + 1) * wide, 16)
            for tap, piece in enumerate(shifted(row, empty, empty, wide)):
                window[pl.ds(start, wide), tap * width : (tap + 1) * width] = piece
            for k, value in enumerate((row, other)):
                value = value.astype(F32)
                column_rows[2 * k, pl.ds(r, 1)] = value[0:1]
                column_rows[2 * k + 1, pl.ds(r, 1)] = value[cols - 1 : cols]

    columns[...] = column_rows[...].astype(BF16)

    def chunk(start, count):
        return [part for j in range(count) for part in (cot[start + j].astype(F32), blank)]

    @pl.loop(0, total // group)
    def _(i):
        value = jnp.concatenate(chunk(i * group, group), 0)
        turned[:, pl.ds(pl.multiple_of(i * span, 128), span)] = value.T.astype(BF16)

    rest = total % group
    if rest:
        start = total - rest
        value = jnp.concatenate(chunk(start, rest) + [jnp.zeros((span - rest * wide, width), F32)], 0)
        turned[:, start * wide : start * wide + span] = value.T.astype(BF16)
    tap_row(turned, window, taps, total * wide, wide, 0)


def tap_row(turned, window, taps, cells, start, slot):
    width = taps.shape[-1]
    value = jnp.dot(turned[:, :cells], window[start : start + cells, :], preferred_element_type=F32)
    for b in range(3):
        taps[slot + b] = value[:, b * width : (b + 1) * width].T


def begin(field, cot):
    total, cols, width = field.shape
    wide = padded_width(cols)
    group = turn_group(wide)
    return pl.pallas_call(
        begin_kernel,
        out_shape=(
            jax.ShapeDtypeStruct((4, total, width), BF16),
            jax.ShapeDtypeStruct(((total + 2) * wide, 3 * width), BF16),
            jax.ShapeDtypeStruct((width, -(-total // group) * group * wide), BF16),
            jax.ShapeDtypeStruct((3, width, width), F32),
            jax.ShapeDtypeStruct(cot.shape, BF16),
        ),
        in_specs=[HBM, HBM],
        out_specs=(VMEM,) * 5,
        scratch_shapes=[
            pltpu.VMEM(field.shape, BF16),
            pltpu.VMEM((4, total, width), F32),
            pltpu.SemaphoreType.DMA((total // fetch_chunk(total), 2)),
        ],
        compiler_params=params(20),
        cost_estimate=pl.CostEstimate(
            flops=8 * total * wide * width * width, bytes_accessed=4 * total * wide * width, transcendentals=0
        ),
    )(field, cot)


def flip(kernel):
    width = kernel.shape[-1]

    def body(kernel, out):
        for tap in range(9):
            a, b = divmod(tap, 3)
            out[a, b * width : (b + 1) * width] = kernel[2 - a, 2 - b].astype(F32).T.astype(BF16)

    return pl.pallas_call(
        body,
        out_shape=jax.ShapeDtypeStruct((3, 3 * width, width), BF16),
        in_specs=[VMEM],
        out_specs=VMEM,
        compiler_params=params(8),
        cost_estimate=pl.CostEstimate(flops=0, bytes_accessed=36 * width * width, transcendentals=0),
    )(kernel)


def outer_taps(window, turned, total, wide):
    width = turned.shape[0]

    def body(window, turned, taps):
        tap_row(turned, window, taps, total * wide, 0, 0)
        tap_row(turned, window, taps, total * wide, 2 * wide, 3)

    return pl.pallas_call(
        body,
        out_shape=jax.ShapeDtypeStruct((6, width, width), F32),
        in_specs=[VMEM, VMEM],
        out_specs=VMEM,
        compiler_params=params(8),
        cost_estimate=pl.CostEstimate(
            flops=12 * total * wide * width * width, bytes_accessed=4 * total * wide * width, transcendentals=0
        ),
    )(window, turned)


def edge_kernel(half, middle, outer, ends, sides, rows, columns, send, keep, side_rows):
    _, cols, width = ends.shape
    wide = padded_width(cols)
    total = columns.shape[1]
    tall = -(-total // 16) * 16
    side_rows[...] = sides[...].astype(F32)
    empty = jnp.zeros((1, width), F32)
    end_parts = [shifted(ends[k], empty, empty, wide) for k in range(2)]
    blank = jnp.zeros((wide - cols, width), F32)
    row_parts = [jnp.concatenate([rows[k].astype(F32), blank], 0).astype(BF16) for k in range(2)]
    low = jnp.zeros((tall - total, width), F32)
    column_parts = [jnp.concatenate([columns[k].astype(F32), low], 0).astype(BF16) for k in range(2)]
    size = 9 * width // 2
    for tap in range(9):
        a, b = divmod(tap, 3)
        left, right = [], []
        if b != 1:
            side = b // 2
            left.append(jnp.concatenate([side_rows[side, a : a + total], low], 0).astype(BF16))
            right.append(column_parts[side])
        if a != 1:
            left.append(end_parts[a // 2][b])
            right.append(row_parts[a // 2])
        value = middle[b] if a == 1 else outer[3 * (a // 2) + b]
        if left:
            value = value + lax.dot_general(
                jnp.concatenate(left, 0),
                jnp.concatenate(right, 0),
                (((0,), (0,)), ((), ())),
                preferred_element_type=F32,
            )
        for part in range(2):
            start = tap * width + part * width // 2
            which, start = divmod(start, size)
            piece = value[part * width // 2 : (part + 1) * width // 2]
            at = slice(start, start + width // 2)

            @pl.when(half[0] == which)
            def _():
                keep[at] = piece

            @pl.when(half[0] != which)
            def _():
                send[at] = piece


def with_edges(half, middle, outer, ends, sides, rows, columns):
    _, _, width = ends.shape
    total = columns.shape[1]
    shape = jax.ShapeDtypeStruct((9 * width // 2, width), F32)
    return pl.pallas_call(
        edge_kernel,
        out_shape=(shape, shape),
        in_specs=[SMEM] + [VMEM] * 6,
        out_specs=(VMEM, VMEM),
        scratch_shapes=[pltpu.VMEM((2, total + 2, width), F32)],
        compiler_params=params(12),
        cost_estimate=pl.CostEstimate(
            flops=16 * 144 * width * width, bytes_accessed=72 * width * width, transcendentals=0
        ),
    )(half, middle, outer, ends, sides, rows, columns)


def add_blocks(places, terms, blocks, scale=None):
    rows, width = terms[0].shape
    size = rows // blocks
    count = places.shape[0]

    def body(where, *refs):
        sources, outs = refs[: len(terms)], refs[len(terms) :]
        for k in range(count):
            at = pl.ds(pl.multiple_of(where[k] * size, 8), size)
            value = sources[0][at]
            for source in sources[1:]:
                value = value + source[at]
            outs[k][...] = value if scale is None else value * scale

    shape = jax.ShapeDtypeStruct((size, width), F32)
    return pl.pallas_call(
        body,
        out_shape=(shape,) * count,
        in_specs=[SMEM] + [VMEM] * len(terms),
        out_specs=(VMEM,) * count,
        compiler_params=params(8),
        cost_estimate=pl.CostEstimate(
            flops=rows * width, bytes_accessed=4 * rows * width * (len(terms) + 1), transcendentals=0
        ),
    )(places, *terms)


def last_sum(terms, scale):
    rows, width = terms[0].shape

    def body(first, second, out):
        value = (first[...] + second[...]) * scale
        top = jnp.max(jnp.max(jnp.abs(value), axis=1, keepdims=True), axis=0, keepdims=True)
        exponent = jnp.ceil(jnp.log2(jnp.maximum(top, 1e-30)))
        out[:rows] = value * jnp.exp2(-exponent)
        out[rows:] = jnp.broadcast_to(exponent, (16, width))

    return pl.pallas_call(
        body,
        out_shape=jax.ShapeDtypeStruct((rows + 16, width), F32),
        in_specs=[VMEM] * 2,
        out_specs=VMEM,
        compiler_params=params(8),
        cost_estimate=pl.CostEstimate(flops=8 * rows * width, bytes_accessed=12 * rows * width, transcendentals=0),
    )(*terms)


def decode(coded):
    return coded[..., :-16, :].astype(F32) * jnp.exp2(coded[..., -1:, :].astype(F32))


def finish(places, own, other):
    blocks, size, width = own.shape

    def body(where, own, other, out, sem):
        for k in range(2 * blocks):
            source = own if k < blocks else other
            at = pl.multiple_of(where[k] * size, 8)
            pltpu.make_async_copy(source.at[k % blocks], out.at[pl.ds(at, size)], sem).start()
        pltpu.make_async_copy(out, out, sem).wait()

    out = pl.pallas_call(
        body,
        out_shape=jax.ShapeDtypeStruct((2 * blocks * size, width), F32),
        in_specs=[SMEM, VMEM, VMEM],
        out_specs=HBM,
        scratch_shapes=[pltpu.SemaphoreType.DMA],
        compiler_params=params(8),
    )(places, own, other)
    return out.reshape(3, 3, width, width)


def swap(value, axis, mask):
    count = lax.axis_size(axis)
    return lax.ppermute(value, axis, [(i, i ^ mask) for i in range(count)])


def swap_next(value, axis):
    count = lax.axis_size(axis)
    return lax.ppermute(value, axis, [(i, (i + (1 if i % 2 else -1)) % count) for i in range(count)])


def swap_rows(value):
    bands, sectors = lax.axis_size("lat"), lax.axis_size("lon")
    pairs = []
    for band in range(bands):
        for sector in range(sectors):
            if band == 0 or band == bands - 1:
                other = (band, (sector + sectors // 2) % sectors)
            else:
                other = (band + (1 if band % 2 else -1), sector)
            pairs.append((band * sectors + sector, other[0] * sectors + other[1]))
    return lax.ppermute(value, ("lat", "lon"), pairs)


def local(inputs, kernel, cotangent):
    rows, cols, width = inputs.shape
    bands, sectors = lax.axis_size("lat"), lax.axis_size("lon")
    band, sector = lax.axis_index("lat"), lax.axis_index("lon")

    def vector(*values):
        return jnp.stack([jnp.asarray(v, jnp.int32) for v in values])

    mine, place = sector & 1, (sector >> 1) & 1
    odd = band & 1
    facts = dict(
        even_band=odd == 0,
        even_sector=mine == 0,
        half=vector(mine),
        rows=vector((1 - odd) * (rows - 1), odd * (rows - 1)),
        lat=vector(*[band ^ m for m in range(bands)]),
        lon=vector(place, 1 - place),
        poles=vector(jnp.where(band == 0, 2, 0), jnp.where(band == bands - 1, 0, 2)),
        last=vector(
            *[
                (h * bands + (band ^ m)) * 2 + p
                for h in (mine, 1 - mine)
                for m in range(bands)
                for p in (place, 1 - place)
            ]
        ),
    )
    inputs, kernel, cotangent, facts = lax.optimization_barrier((inputs, kernel, cotangent, facts))
    even_band, even_sector, half = facts["even_band"], facts["even_sector"], facts["half"]

    near, far = row_messages(facts["rows"], inputs, cotangent)
    near = swap(near, "lat", 1)
    far = swap_rows(far)
    columns, window, turned, middle, cot = begin(inputs, cotangent)
    ends = jnp.stack([jnp.where(even_band, far, near), jnp.where(even_band, near, far)], 1)

    def side(place):
        column = 0 if place == 0 else cols - 1
        return jnp.stack(
            [
                jnp.concatenate([ends[k, :1, column], columns[2 * k + place], ends[k, 1:, column]], 0)
                for k in range(2)
            ]
        )

    first, last = side(0), side(1)
    near = swap(jnp.where(even_sector, last, first), "lon", 1)
    far = swap_next(jnp.where(even_sector, first, last), "lon")
    outer = outer_taps(window, turned, rows, padded_width(cols))
    sides = jnp.stack([jnp.where(even_sector, far, near), jnp.where(even_sector, near, far)], 1)

    edge_rows = jnp.stack([cotangent[0], cotangent[-1]])
    send, keep = with_edges(half, middle, outer, ends[0], sides[0], edge_rows, columns[2:])

    weights = kernel.reshape(3, 3 * width, width)
    flipped = flip(kernel)
    window = patch(window, ends[0], sides[0])
    outputs = input_grad = None
    for start, count in pieces(rows, FORWARD):
        outputs = forward(window, weights, inputs.shape, start, count, outputs)
    for start, count in pieces(rows, BACKWARD):
        input_grad = backward(facts["poles"], cot, ends[1], sides[1], flipped, start, count, input_grad)

    got = swap(send, "lon", 1)
    parts = add_blocks(facts["lat"], [keep, got], bands)
    got = []
    for m in range(1, bands):
        got.append(swap(parts[m], "lat", m))
    keep, send = add_blocks(facts["lon"], [parts[0], *got], 2)
    got = swap(send, "lon", 2)
    factor = 1.0 / math.sqrt(rows * cols * bands * sectors)
    mask = 4
    terms = [keep, got]
    while mask < sectors:
        value = terms[0] + terms[1]
        terms = [value, swap(value, "lon", mask)]
        mask *= 2

    coded = last_sum(terms, factor).astype(HALF)
    got = swap(coded, "lon", 2)
    coded = jnp.stack([coded, got])
    got = []
    for m in range(1, bands):
        got.append(swap(coded, "lat", m))
    coded = jnp.stack([coded, *got])
    got = swap(coded, "lon", 1)
    own, other = (decode(c).reshape(2 * bands, -1, width) for c in (coded, got))
    kernel_grad = finish(facts["last"], own, other)
    return (outputs, input_grad, kernel_grad)


FORWARD = (0, 90)
BACKWARD = (0, 30, 60, 75, 90)


def pieces(rows, cuts):
    if cuts[-1] != rows:
        cuts = (0, rows)
    return [(low, high - low) for low, high in zip(cuts, cuts[1:])]


def solution(mesh):
    in_specs = (P("lat", "lon", None), P(), P("lat", "lon", None))
    out_specs = (P("lat", "lon", None), P("lat", "lon", None), P())
    return jax.shard_map(local, mesh=mesh, in_specs=in_specs, out_specs=out_specs, check_vma=False)
```

time: 108 us -> 98.4 us (0.911)
  waiting for transfers between devices: 45.7 us -> 35.5 us
  Pallas kernels: 37.5 us -> 42.3 us
  local copies, waits for them, and re-layouts: 7.73 us -> 3.41 us
    ppermute x13, waiting for transfers between devices: 41.8 us -> 31.4 us  [swap(): return lax.ppermute(value, axis, [(i, i ^ mask) for i in range(count)])]
    pallas_call x6 -> x13, Pallas kernels: 36.2 us -> 41 us  [the longest x4 14.9 us: backward(): pl.pallas_call(body, out_shape=jax.ShapeDtypeStruct((total, cols, width),...]
    slice x3 -> x2, local copies, waits for them, and re-layouts: 3.31 us -> 0.01 us  [the longest x1 0.01 us: local(): columns[2:]]
    transpose x2 -> x0, local copies, waits for them, and re-layouts: 2.66 us -> none  [local(): jnp.transpose(kernel[::-1, ::-1], (0, 1, 3, 2)).reshape(3, 3 * width, width)]
    unnamed x22 -> x12, local copies, waits for them, and re-layouts: 1.71 us -> 3.27 us
    squeeze x2, other arithmetic: 1.29 us -> 0.03 us  [the longest x1 0.02 us: local(): sides[1]]
    ppermute x1, starting transfers between devices: 1.46 us -> 2.54 us  [swap_next(): lax.ppermute(value, axis, [(i, (i + (1 if i % 2 else -1)) % count) for i...]
  transfers between devices with their start and end apart: 15 -> 15, of which waited for: 11 -> 8; matrix products, arithmetic and copies ran while one was open for 6% -> 0% of each run, Pallas kernels for 22% -> 37%
where the time goes in v2:
time: 98.4 us; the launch traced here: 98.3 us
  Pallas kernels  42.3 us (43%)
  waiting for transfers between devices  35.5 us (36%)
  starting transfers between devices  15 us (15%)
  local copies, waits for them, and re-layouts  3.41 us (3%)
  between operations  1.06 us (1%)
    ppermute x13, waiting for transfers between devices, swap(): return lax.ppermute(value, axis, [(i, i ^ mask) for i in range(count)])  31.4 us
    pallas_call x4, Pallas kernels, backward(): pl.pallas_call(body, out_shape=jax.ShapeDtypeStruct((total, cols, width),...  14.9 us
    pallas_call x1, Pallas kernels, forward(): pl.pallas_call(body, out_shape=jax.ShapeDtypeStruct(shape, BF16), in_spec...  8.96 us
    ppermute x13, starting transfers between devices, swap(): return lax.ppermute(value, axis, [(i, i ^ mask) for i in range(count)])  8.34 us
    pallas_call x1, Pallas kernels, begin(): pl.pallas_call(begin_kernel, out_shape=(jax.ShapeDtypeStruct((4, total, w...  7.1 us
    ppermute x1, starting transfers between devices, swap_rows(): return lax.ppermute(value, ('lat', 'lon'), pairs)  4.13 us
    ppermute x1, waiting for transfers between devices, swap_next(): lax.ppermute(value, axis, [(i, (i + (1 if i % 2 else -1)) % count) for i...  4.03 us
    pallas_call x1, Pallas kernels, outer_taps(): pl.pallas_call(body, out_shape=jax.ShapeDtypeStruct((6, width, width), F3...  3.74 us
  transfers between devices with their start and end apart: 15, of which 8 were waited for; matrix products, arithmetic and copies ran while one was open for 0% of the time, Pallas kernels for 37%

profile of v2, /device:TPU:0, one launch (start us, length us, event | category | flops | bytes accessed | tf_op | source)
XLA Modules:
  0.0 98.3 jit_solution(3413084513141723195)
XLA Ops:
  1.0 1.6 %copy-done = bf16[90,45,256]{2,1,0:T(8,128)(2,1)S(1)} copy-done((bf16[90,45,256]{2,1,0:T(8,128)(2,1)S(1)}, bf16[90,45,256]{2,1,0:T(8,128)(2,1)}, u32[]{:S(2)}) %copy-start) | copy-done | bytes 2073624
  2.6 1.6 %copy-done.2 = bf16[90,45,256]{2,1,0:T(8,128)(2,1)S(1)} copy-done((bf16[90,45,256]{2,1,0:T(8,128)(2,1)S(1)}, bf16[90,45,256]{2,1,0:T(8,128)(2,1)}, u32[]{:S(2)}) %copy-start.2) | copy-done | bytes 2073624
  4.3 0.7 shard_map.59
  5.0 4.1 %collective-permute-start = (bf16[2,45,256]{2,1,0:T(8,128)(2,1)S(1)}, bf16[2,45,256]{2,1,0:T(8,128)(2,1)S(1)}, u32[]{:S(2)}, u32[]{:S(2)}) collective-permute-start(bf16[2,45,256]{2,1,0:T(8,128)(2,1)S(1)} %get-tuple-element.34), channel_id=1, source_target_pairs={{0,4},{1,5},{2,6},{3,7},{4,0},{5,1},{6,2},{7,3},{8,16},{9,17},{10,... | collective-permute-start | bytes 138248 | tf_op jit(solution)/shard_map/ppermute | solution.py:504
  9.1 0.4 collective-permute-start.1
  9.5 7.1 %shard_map.58 = (bf16[4,90,256]{2,1,0:T(8,128)(2,1)S(1)}, bf16[4416,768]{1,0:T(8,128)(2,1)S(1)}, bf16[256,4608]{1,0:T(8,128)(2,1)S(1)}, f32[3,256,256]{2,1,0:T(8,128)S(1)}, bf16[90,45,256]{2,1,0:T(8,128)(2,1)S(1)}) custom-call(bf16[90,45,256]{2,1,0:T(8,128)(2,1)S(1)} %copy-done.3, bf16[90,45,256]{2,1,0:T(8,128)(2,1)S(1)} %copy-done.1), custom_call_target="tpu_custom_call" | custom-call | flops 2264924160 | bytes 4423680 | tf_op jit(solution)/shard_map/pallas_call | solution.py:289
  16.7 3.7 %shard_map.67.outer = f32[6,256,256]{2,1,0:T(8,128)S(1)} custom-call(bf16[4416,768]{1,0:T(8,128)(2,1)S(1)} %get-tuple-element.31.old.window, bf16[256,4608]{1,0:T(8,128)(2,1)S(1)} %get-tuple-element.46.turned), custom_call_target="tpu_custom_call" | custom-call | flops 3397386240 | bytes 4423680 | tf_op jit(solution)/shard_map/pallas_call | solution.py:337
  20.7 2.5 %collective-permute-start.2 = (bf16[2,92,256]{2,1,0:T(8,128)(2,1)S(1)}, bf16[2,92,256]{2,1,0:T(8,128)(2,1)S(1)}, u32[]{:S(2)}, u32[]{:S(2)}) collective-permute-start(bf16[2,92,256]{2,1,0:T(8,128)(2,1)S(1)} %get-tuple-element.62), channel_id=1, source_target_pairs={{0,7},{1,2},{2,1},{3,4},{4,3},{5,6},{6,5},{7,0},{8,15},{9,10},{10,... | collective-permute-start | bytes 282632 | tf_op jit(solution)/shard_map/ppermute | solution.py:491
  23.2 4.0 %collective-permute-done.2 = bf16[2,92,256]{2,1,0:T(8,128)(2,1)S(1)} collective-permute-done((bf16[2,92,256]{2,1,0:T(8,128)(2,1)S(1)}, bf16[2,92,256]{2,1,0:T(8,128)(2,1)S(1)}, u32[]{:S(2)}, u32[]{:S(2)}) %collective-permute-start.2) | collective-permute-done | bytes 94240 | tf_op jit(solution)/shard_map/ppermute | solution.py:491
  27.3 2.2 %shard_map.68 = (f32[1152,256]{1,0:T(8,128)S(1)}, f32[1152,256]{1,0:T(8,128)S(1)}) custom-call(s32[1]{0:T(128)} %bitcast.half, f32[3,256,256]{2,1,0:T(8,128)S(1)} %get-tuple-element.45.middle, f32[6,256,256]{2,1,0:T(8,128)S(1)} %shard_map.67.outer, bf16[2,45,256]{2,1,0:T(8,128)(2,1)S(1)} %get-tuple-element.70.ends, ...), custom_call_target="tpu_custom_call" | custom-call | flops 150994944 | bytes 4718592 | tf_op jit(solution)/shard_map/pallas_call | solution.py:399
  29.6 2.8 %collective-permute-done.4.refs_1_ = f32[1152,256]{1,0:T(8,128)S(1)} collective-permute-done((f32[1152,256]{1,0:T(8,128)S(1)}, f32[1152,256]{1,0:T(8,128)S(1)}, u32[]{:S(2)}, u32[]{:S(2)}) %collective-permute-start.4) | collective-permute-done | bytes 1179680 | tf_op jit(solution)/shard_map/ppermute | solution.py:486
  32.4 0.7 shard_map.69
  33.1 1.0 %collective-permute-start.5 = (f32[288,256]{1,0:T(8,128)S(1)}, f32[288,256]{1,0:T(8,128)S(1)}, u32[]{:S(2)}, u32[]{:S(2)}) collective-permute-start(f32[288,256]{1,0:T(8,128)S(1)} %get-tuple-element.50), channel_id=1, source_target_pairs={{0,8},{8,0},{16,24},{24,16},{1,9},{9,1},{17,25},{25,17},{2,10},{10... | collective-permute-start | bytes 884744 | tf_op jit(solution)/shard_map/ppermute | solution.py:486
  34.1 1.8 %collective-permute-start.6 = (f32[288,256]{1,0:T(8,128)S(1)}, f32[288,256]{1,0:T(8,128)S(1)}, u32[]{:S(2)}, u32[]{:S(2)}) collective-permute-start(f32[288,256]{1,0:T(8,128)S(1)} %get-tuple-element.51), channel_id=1, source_target_pairs={{0,16},{8,24},{16,0},{24,8},{1,17},{9,25},{17,1},{25,9},{2,18},{10... | collective-permute-start | bytes 884744 | tf_op jit(solution)/shard_map/ppermute | solution.py:486
  35.9 0.8 collective-permute-start.7
  36.7 6.4 %collective-permute-done.5.refs_1_ = f32[288,256]{1,0:T(8,128)S(1)} collective-permute-done((f32[288,256]{1,0:T(8,128)S(1)}, f32[288,256]{1,0:T(8,128)S(1)}, u32[]{:S(2)}, u32[]{:S(2)}) %collective-permute-start.5) | collective-permute-done | bytes 294944 | tf_op jit(solution)/shard_map/ppermute | solution.py:486
  43.1 5.5 %collective-permute-done.6.refs_2_ = f32[288,256]{1,0:T(8,128)S(1)} collective-permute-done((f32[288,256]{1,0:T(8,128)S(1)}, f32[288,256]{1,0:T(8,128)S(1)}, u32[]{:S(2)}, u32[]{:S(2)}) %collective-permute-start.6) | collective-permute-done | bytes 294944 | tf_op jit(solution)/shard_map/ppermute | solution.py:486
  48.5 1.4 %collective-permute-done.7.refs_3_ = f32[288,256]{1,0:T(8,128)S(1)} collective-permute-done((f32[288,256]{1,0:T(8,128)S(1)}, f32[288,256]{1,0:T(8,128)S(1)}, u32[]{:S(2)}, u32[]{:S(2)}) %collective-permute-start.7) | collective-permute-done | bytes 294944 | tf_op jit(solution)/shard_map/ppermute | solution.py:486
  49.9 0.6 shard_map.70
  50.9 4.9 %collective-permute-done.8 = f32[144,256]{1,0:T(8,128)S(1)} collective-permute-done((f32[144,256]{1,0:T(8,128)S(1)}, f32[144,256]{1,0:T(8,128)S(1)}, u32[]{:S(2)}, u32[]{:S(2)}) %collective-permute-start.8) | collective-permute-done | bytes 147488 | tf_op jit(solution)/shard_map/ppermute | solution.py:486
  56.4 1.0 shard_map.60.window
  57.4 6.1 %collective-permute-done.9.second = f32[144,256]{1,0:T(8,128)S(1)} collective-permute-done((f32[144,256]{1,0:T(8,128)S(1)}, f32[144,256]{1,0:T(8,128)S(1)}, u32[]{:S(2)}, u32[]{:S(2)}) %collective-permute-start.9) | collective-permute-done | bytes 147488 | tf_op jit(solution)/shard_map/ppermute | solution.py:486
  63.8 4.4 %collective-permute-done.10 = f16[160,256]{1,0:T(8,128)(2,1)S(1)} collective-permute-done((f16[160,256]{1,0:T(8,128)(2,1)S(1)}, f16[160,256]{1,0:T(8,128)(2,1)S(1)}, u32[]{:S(2)}, u32[]{:S(2)}) %collective-permute-start.10) | collective-permute-done | bytes 81952 | tf_op jit(solution)/shard_map/ppermute | solution.py:486
  68.2 1.1 %collective-permute-start.11 = (f16[2,160,256]{2,1,0:T(8,128)(2,1)S(1)}, f16[2,160,256]{2,1,0:T(8,128)(2,1)S(1)}, u32[]{:S(2)}, u32[]{:S(2)}) collective-permute-start(f16[2,160,256]{2,1,0:T(8,128)(2,1)S(1)} %get-tuple-element.68), channel_id=1, source_target_pairs={{0,8},{8,0},{16,24},{24,16},{1,9},{9,1},{17,25},{25,17},{2,10},{10... | collective-permute-start | bytes 491528 | tf_op jit(solution)/shard_map/ppermute | solution.py:486
  69.4 1.0 collective-permute-start.12
  70.3 1.5 %collective-permute-start.13 = (f16[2,160,256]{2,1,0:T(8,128)(2,1)S(1)}, f16[2,160,256]{2,1,0:T(8,128)(2,1)S(1)}, u32[]{:S(2)}, u32[]{:S(2)}) collective-permute-start(f16[2,160,256]{2,1,0:T(8,128)(2,1)S(1)} %get-tuple-element.68), channel_id=1, source_target_pairs={{0,24},{8,16},{16,8},{24,0},{1,25},{9,17},{17,9},{25,1},{2,26},{10... | collective-permute-start | bytes 491528 | tf_op jit(solution)/shard_map/ppermute | solution.py:486
  71.8 9.0 %shard_map.61 = bf16[90,45,256]{2,1,0:T(8,128)(2,1)} custom-call(bf16[4416,768]{1,0:T(8,128)(2,1)S(1)} %shard_map.60.window, bf16[3,768,256]{2,1,0:T(8,128)(2,1)S(1)} %bitcast.100), custom_call_target="tpu_custom_call" | custom-call | flops 5096079360 | bytes 4423680 | tf_op jit(solution)/shard_map/pallas_call | solution.py:181
  80.8 4.6 %shard_map.63.rest_0_ = bf16[90,45,256]{2,1,0:T(8,128)(2,1)} custom-call(s32[2]{0:T(128)S(1)} %get-tuple-element.39.taps, bf16[90,45,256]{2,1,0:T(8,128)(2,1)S(1)} %get-tuple-element.40.field, bf16[2,45,256]{2,1,0:T(8,128)(2,1)S(1)} %get-tuple-element.69.ends, bf16[2,92,256]{2,1,0:T(8,128)(2,1)S(1)} %get-tuple-element.57.sides, ...), custom_call_target="tpu_custom_call" | custom-call | flops 1698693120 | bytes 1474560 | tf_op jit(solution)/shard_map/pallas_call | solution.py:121
  85.7 4.5 %shard_map.64.rest_0_ = bf16[90,45,256]{2,1,0:T(8,128)(2,1)} custom-call(s32[2]{0:T(128)S(1)} %get-tuple-element.39.taps, bf16[90,45,256]{2,1,0:T(8,128)(2,1)S(1)} %get-tuple-element.40.field, bf16[2,45,256]{2,1,0:T(8,128)(2,1)S(1)} %get-tuple-element.69.ends, bf16[2,92,256]{2,1,0:T(8,128)(2,1)S(1)} %get-tuple-element.57.sides, ...), custom_call_target="tpu_custom_call", output_to_operand_aliasing={{}: (5, {})} | custom-call | flops 1698693120 | bytes 1474560 | tf_op jit(solution)/shard_map/pallas_call | solution.py:121
  90.1 2.8 %shard_map.65.rest_0_ = bf16[90,45,256]{2,1,0:T(8,128)(2,1)} custom-call(s32[2]{0:T(128)S(1)} %get-tuple-element.39.taps, bf16[90,45,256]{2,1,0:T(8,128)(2,1)S(1)} %get-tuple-element.40.field, bf16[2,45,256]{2,1,0:T(8,128)(2,1)S(1)} %get-tuple-element.69.ends, bf16[2,92,256]{2,1,0:T(8,128)(2,1)S(1)} %get-tuple-element.57.sides, ...), custom_call_target="tpu_custom_call", output_to_operand_aliasing={{}: (5, {})} | custom-call | flops 849346560 | bytes 737280 | tf_op jit(solution)/shard_map/pallas_call | solution.py:121
  93.0 3.0 %shard_map.66 = bf16[90,45,256]{2,1,0:T(8,128)(2,1)} custom-call(s32[2]{0:T(128)S(1)} %get-tuple-element.39.taps, bf16[90,45,256]{2,1,0:T(8,128)(2,1)S(1)} %get-tuple-element.40.field, bf16[2,45,256]{2,1,0:T(8,128)(2,1)S(1)} %get-tuple-element.69.ends, bf16[2,92,256]{2,1,0:T(8,128)(2,1)S(1)} %get-tuple-element.57.sides, ...), custom_call_target="tpu_custom_call", output_to_operand_aliasing={{}: (5, {})} | custom-call | flops 849346560 | bytes 737280 | tf_op jit(solution)/shard_map/pallas_call | solution.py:121
  96.3 1.9 %shard_map.72 = f32[2304,256]{1,0:T(8,128)} custom-call(s32[16]{0:T(128)S(1)} %stack.176.where, f32[8,144,256]{2,1,0:T(8,128)S(1)} %bitcast.98, f32[8,144,256]{2,1,0:T(8,128)S(1)} %bitcast.99), custom_call_target="tpu_custom_call" | custom-call | tf_op jit(solution)/shard_map/pallas_call | solution.py:473
  (53 shorter events, 2.5 us)
Async XLA Ops:
  1.0 1.6 %copy-start = (bf16[90,45,256]{2,1,0:T(8,128)(2,1)S(1)}, bf16[90,45,256]{2,1,0:T(8,128)(2,1)}, u32[]{:S(2)}) copy-start(bf16[90,45,256]{2,1,0:T(8,128)(2,1)} %cotangent) | copy-start | bytes 6220804
  2.6 1.6 %copy-start.2 = (bf16[90,45,256]{2,1,0:T(8,128)(2,1)S(1)}, bf16[90,45,256]{2,1,0:T(8,128)(2,1)}, u32[]{:S(2)}) copy-start(bf16[90,45,256]{2,1,0:T(8,128)(2,1)} %inputs) | copy-start | bytes 6220804
  4.3 5.3 %copy-start.1 = (bf16[90,45,256]{2,1,0:T(8,128)(2,1)S(1)}, bf16[90,45,256]{2,1,0:T(8,128)(2,1)}, u32[]{:S(2)}) copy-start(bf16[90,45,256]{2,1,0:T(8,128)(2,1)} %cotangent) | copy-start | bytes 6220804
  4.3 5.3 %copy-start.3 = (bf16[90,45,256]{2,1,0:T(8,128)(2,1)S(1)}, bf16[90,45,256]{2,1,0:T(8,128)(2,1)}, u32[]{:S(2)}) copy-start(bf16[90,45,256]{2,1,0:T(8,128)(2,1)} %inputs) | copy-start | bytes 6220804
  5.0 15.5 %collective-permute-start = (bf16[2,45,256]{2,1,0:T(8,128)(2,1)S(1)}, bf16[2,45,256]{2,1,0:T(8,128)(2,1)S(1)}, u32[]{:S(2)}, u32[]{:S(2)}) collective-permute-start(bf16[2,45,256]{2,1,0:T(8,128)(2,1)S(1)} %get-tuple-element.34), channel_id=1, source_target_pairs={{0,4},{1,5},{2,6},{3,7},{4,0},{5,1},{6,2},{7,3},{8,16},{9,17},{10,... | collective-permute-start | bytes 138248 | tf_op jit(solution)/shard_map/ppermute | solution.py:504
  9.1 11.3 %collective-permute-start.1 = (bf16[2,45,256]{2,1,0:T(8,128)(2,1)S(1)}, bf16[2,45,256]{2,1,0:T(8,128)(2,1)S(1)}, u32[]{:S(2)}, u32[]{:S(2)}) collective-permute-start(bf16[2,45,256]{2,1,0:T(8,128)(2,1)S(1)} %get-tuple-element.35), channel_id=1, source_target_pairs={{0,8},{8,0},{16,24},{24,16},{1,9},{9,1},{17,25},{25,17},{2,10},{10... | collective-permute-start | bytes 138248 | tf_op jit(solution)/shard_map/ppermute | solution.py:486
  20.7 6.6 %collective-permute-start.2 = (bf16[2,92,256]{2,1,0:T(8,128)(2,1)S(1)}, bf16[2,92,256]{2,1,0:T(8,128)(2,1)S(1)}, u32[]{:S(2)}, u32[]{:S(2)}) collective-permute-start(bf16[2,92,256]{2,1,0:T(8,128)(2,1)S(1)} %get-tuple-element.62), channel_id=1, source_target_pairs={{0,7},{1,2},{2,1},{3,4},{4,3},{5,6},{6,5},{7,0},{8,15},{9,10},{10,... | collective-permute-start | bytes 282632 | tf_op jit(solution)/shard_map/ppermute | solution.py:491
  23.2 4.1 %collective-permute-start.3 = (bf16[2,92,256]{2,1,0:T(8,128)(2,1)S(1)}, bf16[2,92,256]{2,1,0:T(8,128)(2,1)S(1)}, u32[]{:S(2)}, u32[]{:S(2)}) collective-permute-start(bf16[2,92,256]{2,1,0:T(8,128)(2,1)S(1)} %get-tuple-element.61), channel_id=1, source_target_pairs={{0,1},{1,0},{2,3},{3,2},{4,5},{5,4},{6,7},{7,6},{8,9},{9,8},{10,11... | collective-permute-start | bytes 282632 | tf_op jit(solution)/shard_map/ppermute | solution.py:486
  29.5 2.9 %collective-permute-start.4 = (f32[1152,256]{1,0:T(8,128)S(1)}, f32[1152,256]{1,0:T(8,128)S(1)}, u32[]{:S(2)}, u32[]{:S(2)}) collective-permute-start(f32[1152,256]{1,0:T(8,128)S(1)} %get-tuple-element.48), channel_id=1, source_target_pairs={{0,1},{1,0},{2,3},{3,2},{4,5},{5,4},{6,7},{7,6},{8,9},{9,8},{10,11... | collective-permute-start | bytes 3538952 | tf_op jit(solution)/shard_map/ppermute | solution.py:486
  32.4 23.6 %copy-start.4 = (bf16[3,3,256,256]{3,2,1,0:T(8,128)(2,1)S(1)}, bf16[3,3,256,256]{3,2,1,0:T(8,128)(2,1)}, u32[]{:S(2)}) copy-start(bf16[3,3,256,256]{3,2,1,0:T(8,128)(2,1)} %kernel) | copy-start | bytes 3538948
  33.1 9.9 %collective-permute-start.5 = (f32[288,256]{1,0:T(8,128)S(1)}, f32[288,256]{1,0:T(8,128)S(1)}, u32[]{:S(2)}, u32[]{:S(2)}) collective-permute-start(f32[288,256]{1,0:T(8,128)S(1)} %get-tuple-element.50), channel_id=1, source_target_pairs={{0,8},{8,0},{16,24},{24,16},{1,9},{9,1},{17,25},{25,17},{2,10},{10... | collective-permute-start | bytes 884744 | tf_op jit(solution)/shard_map/ppermute | solution.py:486
  34.1 14.4 %collective-permute-start.6 = (f32[288,256]{1,0:T(8,128)S(1)}, f32[288,256]{1,0:T(8,128)S(1)}, u32[]{:S(2)}, u32[]{:S(2)}) collective-permute-start(f32[288,256]{1,0:T(8,128)S(1)} %get-tuple-element.51), channel_id=1, source_target_pairs={{0,16},{8,24},{16,0},{24,8},{1,17},{9,25},{17,1},{25,9},{2,18},{10... | collective-permute-start | bytes 884744 | tf_op jit(solution)/shard_map/ppermute | solution.py:486
  35.9 14.0 %collective-permute-start.7 = (f32[288,256]{1,0:T(8,128)S(1)}, f32[288,256]{1,0:T(8,128)S(1)}, u32[]{:S(2)}, u32[]{:S(2)}) collective-permute-start(f32[288,256]{1,0:T(8,128)S(1)} %get-tuple-element.52), channel_id=1, source_target_pairs={{0,24},{8,16},{16,8},{24,0},{1,25},{9,17},{17,9},{25,1},{2,26},{10... | collective-permute-start | bytes 884744 | tf_op jit(solution)/shard_map/ppermute | solution.py:486
  50.6 5.2 %collective-permute-start.8 = (f32[144,256]{1,0:T(8,128)S(1)}, f32[144,256]{1,0:T(8,128)S(1)}, u32[]{:S(2)}, u32[]{:S(2)}) collective-permute-start(f32[144,256]{1,0:T(8,128)S(1)} %get-tuple-element.54), channel_id=1, source_target_pairs={{0,2},{1,3},{2,0},{3,1},{4,6},{5,7},{6,4},{7,5},{8,10},{9,11},{10,... | collective-permute-start | bytes 442376 | tf_op jit(solution)/shard_map/ppermute | solution.py:486
  55.8 7.7 %collective-permute-start.9 = (f32[144,256]{1,0:T(8,128)S(1)}, f32[144,256]{1,0:T(8,128)S(1)}, u32[]{:S(2)}, u32[]{:S(2)}) collective-permute-start(f32[144,256]{1,0:T(8,128)S(1)} %add.107.first), channel_id=1, source_target_pairs={{0,4},{1,5},{2,6},{3,7},{4,0},{5,1},{6,2},{7,3},{8,12},{9,13},{10,... | collective-permute-start | bytes 442376 | tf_op jit(solution)/shard_map/ppermute | solution.py:486
  63.7 4.5 %collective-permute-start.10 = (f16[160,256]{1,0:T(8,128)(2,1)S(1)}, f16[160,256]{1,0:T(8,128)(2,1)S(1)}, u32[]{:S(2)}, u32[]{:S(2)}) collective-permute-start(f16[160,256]{1,0:T(8,128)(2,1)S(1)} %convert_element_type.15), channel_id=1, source_target_pairs={{0,2},{1,3},{2,0},{3,1},{4,6},{5,7},{6,4},{7,5},{8,10},{9,11},{10,... | collective-permute-start | bytes 245768 | tf_op jit(solution)/shard_map/ppermute | solution.py:486
  68.2 17.1 %collective-permute-start.11 = (f16[2,160,256]{2,1,0:T(8,128)(2,1)S(1)}, f16[2,160,256]{2,1,0:T(8,128)(2,1)S(1)}, u32[]{:S(2)}, u32[]{:S(2)}) collective-permute-start(f16[2,160,256]{2,1,0:T(8,128)(2,1)S(1)} %get-tuple-element.68), channel_id=1, source_target_pairs={{0,8},{8,0},{16,24},{24,16},{1,9},{9,1},{17,25},{25,17},{2,10},{10... | collective-permute-start | bytes 491528 | tf_op jit(solution)/shard_map/ppermute | solution.py:486
  69.4 16.0 %collective-permute-start.12 = (f16[2,160,256]{2,1,0:T(8,128)(2,1)S(1)}, f16[2,160,256]{2,1,0:T(8,128)(2,1)S(1)}, u32[]{:S(2)}, u32[]{:S(2)}) collective-permute-start(f16[2,160,256]{2,1,0:T(8,128)(2,1)S(1)} %get-tuple-element.68), channel_id=1, source_target_pairs={{0,16},{8,24},{16,0},{24,8},{1,17},{9,25},{17,1},{25,9},{2,18},{10... | collective-permute-start | bytes 491528 | tf_op jit(solution)/shard_map/ppermute | solution.py:486
  70.3 15.0 %collective-permute-start.13 = (f16[2,160,256]{2,1,0:T(8,128)(2,1)S(1)}, f16[2,160,256]{2,1,0:T(8,128)(2,1)S(1)}, u32[]{:S(2)}, u32[]{:S(2)}) collective-permute-start(f16[2,160,256]{2,1,0:T(8,128)(2,1)S(1)} %get-tuple-element.68), channel_id=1, source_target_pairs={{0,24},{8,16},{16,8},{24,0},{1,25},{9,17},{17,9},{25,1},{2,26},{10... | collective-permute-start | bytes 491528 | tf_op jit(solution)/shard_map/ppermute | solution.py:486
  85.6 10.6 %collective-permute-start.14 = (f16[4,2,160,256]{3,2,1,0:T(8,128)(2,1)S(1)}, f16[4,2,160,256]{3,2,1,0:T(8,128)(2,1)S(1)}, u32[]{:S(2)}, u32[]{:S(2)}) collective-permute-start(f16[4,2,160,256]{3,2,1,0:T(8,128)(2,1)S(1)} %pad_maximum_fusion), channel_id=1, source_target_pairs={{0,1},{1,0},{2,3},{3,2},{4,5},{5,4},{6,7},{7,6},{8,9},{9,8},{10,11... | collective-permute-start | bytes 1966088 | tf_op jit(solution)/shard_map/ppermute | solution.py:486

commit v3 on v2

--- a/solution.py
+++ b/solution.py
@@ -18,6 +18,10 @@
 
 def padded_width(cols):
     return -(-(cols + 3) // 16) * 16
+
+
+def in_hbm(value):
+    return pltpu.with_memory_space_constraint(value, pltpu.HBM)
 
 
 def params(mib):
@@ -64,41 +68,48 @@
     return max(n for n in range(1, 6) if rows % n == 0)
 
 
-def conv_rows(taps, window, weights, result, out, sem, cols, first, rows, total):
+def conv_rows(taps, window, weights, result, cols, first, rows, total):
     width = weights.shape[-1]
     wide = padded_width(cols)
     step = block_rows(rows)
 
-    def rows_of(start, count, which):
-        acc = None
-        for a in range(3):
-            at = start + a
-            at = at * wide if isinstance(at, int) else pl.multiple_of(at * wide, 16)
-            term = jnp.dot(window[pl.ds(at, count * wide), :], weights[which[a]], preferred_element_type=F32)
-            acc = term if acc is None else acc + term
-        return acc.reshape(count, wide, width)[:, :cols].astype(BF16)
-
-    def write(at):
-        return pltpu.make_async_copy(result.at[pl.ds(at, step)], out.at[pl.ds(first + at, step)], sem)
+    def term(slot, count, which):
+        at = slot * wide if isinstance(slot, int) else pl.multiple_of(slot * wide, 16)
+        return jnp.dot(window[pl.ds(at, count * wide), :], weights[which], preferred_element_type=F32)
+
+    def block(i, top=0, bottom=2):
+        start = i * step
+        if isinstance(top, int):
+            value = term(start, step, 0)
+        else:
+            value = jnp.concatenate([term(start, 1, top), term(start + 1, step - 1, 0)], 0)
+        value = value + term(start + 1, step, 1)
+        if isinstance(bottom, int):
+            value = value + term(start + 2, step, 2)
+        else:
+            value = value + jnp.concatenate(
+                [term(start + 2, step - 1, 2), term(start + step + 1, 1, bottom)], 0
+            )
+        result[pl.ds(start, step)] = value.reshape(step, wide, width)[:, :cols].astype(BF16)
 
     count = rows // step
-    low = int(first == 0 and taps is not None)
-    high = count - int(first + rows == total and taps is not None)
-
-    @pl.loop(low, high)
-    def _(i):
-        result[pl.ds(i * step, step)] = rows_of(i * step, step, (0, 1, 2))
-        write(i * step).start()
-
+    poles = taps is not None and step > 1
+    low = int(first == 0 and poles)
+    high = count - int(first + rows == total and poles)
+    group = 3
+    trips = (high - low) // group
+
+    @pl.loop(0, trips)
+    def _(j):
+        for u in range(group):
+            block(low + j * group + u)
+
+    for i in range(low + trips * group, high):
+        block(i)
     if low:
-        result[0:step] = rows_of(0, step, (0, 1, 2))
-        result[0:1] = rows_of(0, 1, (taps[0], 1, 2))
-        write(0).start()
+        block(0, top=taps[0])
     if high < count:
-        result[rows - step : rows] = rows_of(rows - step, step, (0, 1, 2))
-        result[rows - 1 : rows] = rows_of(rows - 1, 1, (0, 1, taps[1]))
-        write(rows - step).start()
-    pltpu.make_async_copy(result, out.at[pl.ds(first, rows)], sem).wait()
+        block(count - 1, bottom=taps[1])
 
 
 def conv_cost(rows, cols, width):
@@ -108,31 +119,22 @@
     )
 
 
-def backward(taps, field, ends, sides, weights, first, rows, out=None):
+def prepare(field, ends, sides):
     total, cols, width = field.shape
     wide = padded_width(cols)
-    more = [] if out is None else [out]
-
-    def body(taps, field, ends, sides, weights, *rest):
-        out, window, side_rows, result, sem = rest[-5:]
-        fill_window(field, ends, sides, side_rows, window, first, rows)
-        conv_rows(taps, window, weights, result, out, sem, cols, first, rows, total)
-
-    return pl.pallas_call(
-        body,
-        out_shape=jax.ShapeDtypeStruct((total, cols, width), BF16),
-        in_specs=[SMEM, VMEM, VMEM, VMEM, VMEM] + [HBM] * len(more),
-        out_specs=HBM,
-        scratch_shapes=[
-            pltpu.VMEM(((rows + 2) * wide, 3 * width), BF16),
-            pltpu.VMEM((2, total + 2, width), F32),
-            pltpu.VMEM((rows, cols, width), BF16),
-            pltpu.SemaphoreType.DMA,
-        ],
-        input_output_aliases={5: 0} if more else {},
-        compiler_params=params(20),
-        cost_estimate=conv_cost(rows, cols, width),
-    )(taps, field, ends, sides, weights, *more)
+
+    def body(field, ends, sides, window, side_rows):
+        fill_window(field, ends, sides, side_rows, window, 0, total)
+
+    return pl.pallas_call(
+        body,
+        out_shape=jax.ShapeDtypeStruct(((total + 2) * wide, 3 * width), BF16),
+        in_specs=[VMEM] * 3,
+        out_specs=VMEM,
+        scratch_shapes=[pltpu.VMEM((2, total + 2, width), F32)],
+        compiler_params=params(8),
+        cost_estimate=pl.CostEstimate(flops=0, bytes_accessed=8 * total * wide * width, transcendentals=0),
+    )(field, ends, sides)
 
 
 def patch(window, ends, sides):
@@ -168,59 +170,74 @@
     )(window, ends, sides)
 
 
-def forward(window, weights, shape, first, rows, out=None):
+class Flush:
+    def __init__(self):
+        self.piece = self.first = self.name = None
+        self.outputs = {}
+
+    def operands(self):
+        if self.piece is None:
+            return []
+        known = self.outputs.get(self.name)
+        return [self.piece] if known is None else [self.piece, known]
+
+    def specs(self):
+        return [VMEM, HBM][: len(self.operands())]
+
+    def shapes(self, shape):
+        return [] if self.piece is None else [jax.ShapeDtypeStruct(shape, BF16)]
+
+    def aliases(self, operand, output):
+        return {operand + 1: output} if len(self.operands()) == 2 else {}
+
+    def scratch(self):
+        return [] if self.piece is None else [pltpu.SemaphoreType.DMA]
+
+    def copy(self, piece, out, sem):
+        return pltpu.make_async_copy(piece, out.at[pl.ds(self.first, self.piece.shape[0])], sem)
+
+
+def conv(taps, window, weights, shape, first, rows, name, flush):
     total, cols, width = shape
     wide = padded_width(cols)
-    more = [] if out is None else [out]
-
-    def body(window, weights, *rest):
-        out, result, sem = rest[-3:]
+    flags = [] if taps is None else [taps]
+    more = flush.operands()
+    inputs = len(flags) + 2
+
+    def body(*refs):
+        taps = refs[0] if flags else None
+        window, weights = refs[len(flags) : inputs]
+        result = refs[inputs + len(more)]
+        copy = None
+        if more:
+            copy = flush.copy(refs[inputs], refs[-2], refs[-1])
+            copy.start()
         view = window.at[first * wide : (first + rows + 2) * wide]
-        conv_rows(None, view, weights, result, out, sem, cols, first, rows, total)
-
-    return pl.pallas_call(
-        body,
-        out_shape=jax.ShapeDtypeStruct(shape, BF16),
-        in_specs=[VMEM, VMEM] + [HBM] * len(more),
-        out_specs=HBM,
-        scratch_shapes=[pltpu.VMEM((rows, cols, width), BF16), pltpu.SemaphoreType.DMA],
-        input_output_aliases={2: 0} if more else {},
+        conv_rows(taps, view, weights, result, cols, first, rows, total)
+        if copy is not None:
+            copy.wait()
+
+    results = pl.pallas_call(
+        body,
+        out_shape=[jax.ShapeDtypeStruct((rows, cols, width), BF16)] + flush.shapes(shape),
+        in_specs=[SMEM] * len(flags) + [VMEM] * 2 + flush.specs(),
+        out_specs=[VMEM] + [HBM] * bool(more),
+        scratch_shapes=flush.scratch(),
+        input_output_aliases=flush.aliases(inputs, 1),
         compiler_params=params(8),
         cost_estimate=conv_cost(rows, cols, width),
-    )(window, weights, *more)
+    )(*flags, window, weights, *more)
+    if more:
+        flush.outputs[flush.name] = results[1]
+    flush.piece, flush.first, flush.name = results[0], first, name
 
 
 def turn_group(wide):
     return 128 // math.gcd(128, wide)
 
 
-def row_messages(rows, inputs, cotangent):
-    _, cols, width = inputs.shape
-
-    def body(rows, inputs, cotangent, near, far, sem):
-        copies = [
-            pltpu.make_async_copy(field.at[rows[k]], out.at[j], sem.at[2 * k + j])
-            for k, out in enumerate((near, far))
-            for j, field in enumerate((inputs, cotangent))
-        ]
-        for copy in copies:
-            copy.start()
-        for copy in copies:
-            copy.wait()
-
-    shape = jax.ShapeDtypeStruct((2, cols, width), BF16)
-    return pl.pallas_call(
-        body,
-        out_shape=(shape, shape),
-        in_specs=[SMEM, HBM, HBM],
-        out_specs=(VMEM, VMEM),
-        scratch_shapes=[pltpu.SemaphoreType.DMA((4,))],
-        compiler_params=params(8),
-    )(rows, inputs, cotangent)
-
-
 def fetch_chunk(total):
-    return max(n for n in range(1, 33) if total % n == 0)
+    return max(n for n in range(1, 19) if total % n == 0)
 
 
 def begin_kernel(field_hbm, cot_hbm, columns, window, turned, taps, cot, field, column_rows, sems):
@@ -302,7 +319,7 @@
             pltpu.VMEM((4, total, width), F32),
             pltpu.SemaphoreType.DMA((total // fetch_chunk(total), 2)),
         ],
-        compiler_params=params(20),
+        compiler_params=params(12),
         cost_estimate=pl.CostEstimate(
             flops=8 * total * wide * width * width, bytes_accessed=4 * total * wide * width, transcendentals=0
         ),
@@ -346,7 +363,7 @@
     )(window, turned)
 
 
-def edge_kernel(half, middle, outer, ends, sides, rows, columns, send, keep, side_rows):
+def edge_kernel(half, middle, outer, ends, sides, rows, columns, send, every, side_rows):
     _, cols, width = ends.shape
     wide = padded_width(cols)
     total = columns.shape[1]
@@ -377,28 +394,19 @@
                 (((0,), (0,)), ((), ())),
                 preferred_element_type=F32,
             )
-        for part in range(2):
-            start = tap * width + part * width // 2
-            which, start = divmod(start, size)
-            piece = value[part * width // 2 : (part + 1) * width // 2]
-            at = slice(start, start + width // 2)
-
-            @pl.when(half[0] == which)
-            def _():
-                keep[at] = piece
-
-            @pl.when(half[0] != which)
-            def _():
-                send[at] = piece
+        every[tap * width : (tap + 1) * width] = value
+    send[...] = every[pl.ds(pl.multiple_of((1 - half[0]) * size, 8), size)]
 
 
 def with_edges(half, middle, outer, ends, sides, rows, columns):
     _, _, width = ends.shape
     total = columns.shape[1]
-    shape = jax.ShapeDtypeStruct((9 * width // 2, width), F32)
     return pl.pallas_call(
         edge_kernel,
-        out_shape=(shape, shape),
+        out_shape=(
+            jax.ShapeDtypeStruct((9 * width // 2, width), F32),
+            jax.ShapeDtypeStruct((9 * width, width), F32),
+        ),
         in_specs=[SMEM] + [VMEM] * 6,
         out_specs=(VMEM, VMEM),
         scratch_shapes=[pltpu.VMEM((2, total + 2, width), F32)],
@@ -409,31 +417,53 @@
     )(half, middle, outer, ends, sides, rows, columns)
 
 
-def add_blocks(places, terms, blocks, scale=None):
-    rows, width = terms[0].shape
-    size = rows // blocks
-    count = places.shape[0]
+def add_blocks(places, terms, sizes):
+    width = terms[0].shape[1]
+    count = len(sizes)
 
     def body(where, *refs):
         sources, outs = refs[: len(terms)], refs[len(terms) :]
-        for k in range(count):
-            at = pl.ds(pl.multiple_of(where[k] * size, 8), size)
-            value = sources[0][at]
-            for source in sources[1:]:
-                value = value + source[at]
-            outs[k][...] = value if scale is None else value * scale
-
-    shape = jax.ShapeDtypeStruct((size, width), F32)
-    return pl.pallas_call(
-        body,
-        out_shape=(shape,) * count,
+        for k, size in enumerate(sizes):
+            value = None
+            for t, source in enumerate(sources):
+                part = source[pl.ds(pl.multiple_of(where[t * count + k], 8), size)]
+                value = part if value is None else value + part
+            outs[k][...] = value
+
+    return pl.pallas_call(
+        body,
+        out_shape=tuple(jax.ShapeDtypeStruct((size, width), F32) for size in sizes),
         in_specs=[SMEM] + [VMEM] * len(terms),
         out_specs=(VMEM,) * count,
         compiler_params=params(8),
         cost_estimate=pl.CostEstimate(
-            flops=rows * width, bytes_accessed=4 * rows * width * (len(terms) + 1), transcendentals=0
+            flops=sum(sizes) * width, bytes_accessed=4 * sum(sizes) * width * (len(terms) + 1), transcendentals=0
         ),
     )(places, *terms)
+
+
+def join_sums(upper, lower):
+    above, width = upper[0].shape
+    below = lower[0].shape[0]
+
+    def body(*refs):
+        out = refs[-1]
+        for at, size, sources in ((0, above, refs[: len(upper)]), (above, below, refs[len(upper) : -1])):
+            value = sources[0][...]
+            for source in sources[1:]:
+                value = value + source[...]
+            out[at : at + size] = value
+
+    return pl.pallas_call(
+        body,
+        out_shape=jax.ShapeDtypeStruct((above + below, width), F32),
+        in_specs=[VMEM] * (len(upper) + len(lower)),
+        out_specs=VMEM,
+        compiler_params=params(8),
+        cost_estimate=pl.CostEstimate(
+            flops=4 * (above + below) * width, bytes_accessed=16 * (above + below) * width, transcendentals=0
+        ),
+    )(*upper, *lower)
 
 
 def last_sum(terms, scale):
@@ -444,11 +474,11 @@
         top = jnp.max(jnp.max(jnp.abs(value), axis=1, keepdims=True), axis=0, keepdims=True)
         exponent = jnp.ceil(jnp.log2(jnp.maximum(top, 1e-30)))
         out[:rows] = value * jnp.exp2(-exponent)
-        out[rows:] = jnp.broadcast_to(exponent, (16, width))
-
-    return pl.pallas_call(
-        body,
-        out_shape=jax.ShapeDtypeStruct((rows + 16, width), F32),
+        out[rows:] = jnp.broadcast_to(exponent, (8, width))
+
+    return pl.pallas_call(
+        body,
+        out_shape=jax.ShapeDtypeStruct((rows + 8, width), F32),
         in_specs=[VMEM] * 2,
         out_specs=VMEM,
         compiler_params=params(8),
@@ -457,28 +487,44 @@
 
 
 def decode(coded):
-    return coded[..., :-16, :].astype(F32) * jnp.exp2(coded[..., -1:, :].astype(F32))
-
-
-def finish(places, own, other):
-    blocks, size, width = own.shape
-
-    def body(where, own, other, out, sem):
-        for k in range(2 * blocks):
-            source = own if k < blocks else other
-            at = pl.multiple_of(where[k] * size, 8)
-            pltpu.make_async_copy(source.at[k % blocks], out.at[pl.ds(at, size)], sem).start()
-        pltpu.make_async_copy(out, out, sem).wait()
-
-    out = pl.pallas_call(
-        body,
-        out_shape=jax.ShapeDtypeStruct((2 * blocks * size, width), F32),
-        in_specs=[SMEM, VMEM, VMEM],
-        out_specs=HBM,
-        scratch_shapes=[pltpu.SemaphoreType.DMA],
-        compiler_params=params(8),
-    )(places, own, other)
-    return out.reshape(3, 3, width, width)
+    return coded[..., :-8, :].astype(F32) * jnp.exp2(coded[..., -1:, :].astype(F32))
+
+
+def put_blocks(places, blocks, cuts, total, out=None, flush=None, shape=None):
+    count, _, width = blocks.shape
+    more = [] if out is None else [out]
+    late = [] if flush is None else flush.operands()
+    inputs = 2 + len(more)
+
+    def body(where, blocks, *rest):
+        refs = rest[len(more) + len(late) :]
+        out, sem = refs[0], refs[-1]
+        copy = None
+        if late:
+            copy = flush.copy(rest[len(more)], refs[1], refs[2])
+            copy.start()
+        for k in range(count):
+            start = 0
+            for j, size in enumerate(cuts):
+                at = pl.multiple_of(where[2 * k + j], 8)
+                pltpu.make_async_copy(blocks.at[k, pl.ds(start, size)], out.at[pl.ds(at, size)], sem).start()
+                start += size
+        pltpu.make_async_copy(blocks, blocks, sem).wait()
+        if copy is not None:
+            copy.wait()
+
+    results = pl.pallas_call(
+        body,
+        out_shape=[jax.ShapeDtypeStruct((total, width), F32)] + (flush.shapes(shape) if late else []),
+        in_specs=[SMEM, VMEM] + [HBM] * len(more) + (flush.specs() if late else []),
+        out_specs=[HBM] * (1 + bool(late)),
+        scratch_shapes=(flush.scratch() if late else []) + [pltpu.SemaphoreType.DMA],
+        input_output_aliases={**({2: 0} if more else {}), **(flush.aliases(inputs, 1) if late else {})},
+        compiler_params=params(8),
+    )(places, blocks, *more, *late)
+    if late:
+        flush.outputs[flush.name] = results[1]
+    return results[0]
 
 
 def swap(value, axis, mask):
@@ -514,30 +560,52 @@
 
     mine, place = sector & 1, (sector >> 1) & 1
     odd = band & 1
+    half_rows = 9 * width // 2
+    unit = 16 * bands
+    upper = (half_rows // unit + 1) // 2 * unit
+    lower = half_rows - upper
+    upper_part, lower_part = upper // bands, lower // 2
+    upper_end, lower_end = upper_part // 2, lower_part // bands
+    first_sizes = [upper_part] * bands + [lower_part] * 2
+    first_rows = [(band ^ m) * upper_part for m in range(bands)]
+    first_rows += [upper + p * lower_part for p in (place, 1 - place)]
+
+    def homes(h):
+        return vector(
+            *[
+                h * half_rows + row
+                for m in range(bands)
+                for p in (place, 1 - place)
+                for row in (
+                    (band ^ m) * upper_part + p * upper_end,
+                    upper + p * lower_part + (band ^ m) * lower_end,
+                )
+            ]
+        )
+
     facts = dict(
         even_band=odd == 0,
         even_sector=mine == 0,
         half=vector(mine),
-        rows=vector((1 - odd) * (rows - 1), odd * (rows - 1)),
-        lat=vector(*[band ^ m for m in range(bands)]),
-        lon=vector(place, 1 - place),
+        near_row=(1 - odd) * (rows - 1),
+        far_row=odd * (rows - 1),
+        first=vector(*[mine * half_rows + row for row in first_rows], *first_rows),
+        upper=vector(*[p * upper_end for _ in range(bands) for p in (place, 1 - place)]),
+        lower=vector(*[(band ^ m) * lower_end for _ in range(2) for m in range(bands)]),
         poles=vector(jnp.where(band == 0, 2, 0), jnp.where(band == bands - 1, 0, 2)),
-        last=vector(
-            *[
-                (h * bands + (band ^ m)) * 2 + p
-                for h in (mine, 1 - mine)
-                for m in range(bands)
-                for p in (place, 1 - place)
-            ]
-        ),
+        own=homes(mine),
+        other=homes(1 - mine),
     )
     inputs, kernel, cotangent, facts = lax.optimization_barrier((inputs, kernel, cotangent, facts))
     even_band, even_sector, half = facts["even_band"], facts["even_sector"], facts["half"]
 
-    near, far = row_messages(facts["rows"], inputs, cotangent)
+    near, far = (
+        jnp.stack([lax.dynamic_index_in_dim(field, facts[name], 0, False) for field in (inputs, cotangent)])
+        for name in ("near_row", "far_row")
+    )
     near = swap(near, "lat", 1)
     far = swap_rows(far)
-    columns, window, turned, middle, cot = begin(inputs, cotangent)
+    columns, window, turned, middle, cot = begin(in_hbm(inputs), in_hbm(cotangent))
     ends = jnp.stack([jnp.where(even_band, far, near), jnp.where(even_band, near, far)], 1)
 
     def side(place):
@@ -556,31 +624,39 @@
     sides = jnp.stack([jnp.where(even_sector, far, near), jnp.where(even_sector, near, far)], 1)
 
     edge_rows = jnp.stack([cotangent[0], cotangent[-1]])
-    send, keep = with_edges(half, middle, outer, ends[0], sides[0], edge_rows, columns[2:])
+    send, every = with_edges(half, middle, outer, ends[0], sides[0], edge_rows, columns[2:])
 
     weights = kernel.reshape(3, 3 * width, width)
     flipped = flip(kernel)
     window = patch(window, ends[0], sides[0])
-    outputs = input_grad = None
-    for start, count in pieces(rows, FORWARD):
-        outputs = forward(window, weights, inputs.shape, start, count, outputs)
-    for start, count in pieces(rows, BACKWARD):
-        input_grad = backward(facts["poles"], cot, ends[1], sides[1], flipped, start, count, input_grad)
+    cot_window = prepare(cot, ends[1], sides[1])
+    flush = Flush()
+    for name, (start, count) in pieces(rows):
+        if name.startswith("forward"):
+            conv(None, window, weights, inputs.shape, start, count, "outputs", flush)
+        else:
+            conv(facts["poles"], cot_window, flipped, inputs.shape, start, count, "input_grad", flush)
 
     got = swap(send, "lon", 1)
-    parts = add_blocks(facts["lat"], [keep, got], bands)
+    *parts, low_keep, low_send = add_blocks(facts["first"], [every, got], first_sizes)
+    low_got = swap(low_send, "lon", 2)
     got = []
     for m in range(1, bands):
         got.append(swap(parts[m], "lat", m))
-    keep, send = add_blocks(facts["lon"], [parts[0], *got], 2)
+    lows = add_blocks(facts["lower"], [low_keep, low_got], [lower_end] * bands)
+    keep, send = add_blocks(facts["upper"], [parts[0], *got], [upper_end] * 2)
+    low_got = []
     got = swap(send, "lon", 2)
+    for m in range(1, bands):
+        low_got.append(swap(lows[m], "lat", m))
+    value = join_sums([keep, got], [lows[0], *low_got])
     factor = 1.0 / math.sqrt(rows * cols * bands * sectors)
     mask = 4
-    terms = [keep, got]
     while mask < sectors:
-        value = terms[0] + terms[1]
         terms = [value, swap(value, "lon", mask)]
         mask *= 2
+        if mask < sectors:
+            value = terms[0] + terms[1]
 
     coded = last_sum(terms, factor).astype(HALF)
     got = swap(coded, "lon", 2)
@@ -590,19 +666,22 @@
         got.append(swap(coded, "lat", m))
     coded = jnp.stack([coded, *got])
     got = swap(coded, "lon", 1)
-    own, other = (decode(c).reshape(2 * bands, -1, width) for c in (coded, got))
-    kernel_grad = finish(facts["last"], own, other)
-    return (outputs, input_grad, kernel_grad)
-
-
-FORWARD = (0, 90)
-BACKWARD = (0, 30, 60, 75, 90)
-
-
-def pieces(rows, cuts):
-    if cuts[-1] != rows:
-        cuts = (0, rows)
-    return [(low, high - low) for low, high in zip(cuts, cuts[1:])]
+    whole, cuts = 9 * width, (upper_end, lower_end)
+    kernel_grad = put_blocks(facts["own"], decode(coded).reshape(2 * bands, -1, width), cuts, whole, None, flush, inputs.shape)
+    kernel_grad = put_blocks(facts["other"], decode(got).reshape(2 * bands, -1, width), cuts, whole, kernel_grad)
+    return (flush.outputs["outputs"], flush.outputs["input_grad"], kernel_grad.reshape(3, 3, width, width))
+
+
+FORWARD = (0, 45, 90)
+BACKWARD = (0, 45, 60, 90)
+
+
+def pieces(rows):
+    for name, cuts in (("forward", FORWARD), ("backward", BACKWARD)):
+        if cuts[-1] != rows:
+            cuts = tuple(k * rows // (len(cuts) - 1) for k in range(len(cuts)))
+        for k, (low, high) in enumerate(zip(cuts, cuts[1:])):
+            yield f"{name}_{k}", (low, high - low)
 
 
 def solution(mesh):

time: 98.4 us -> 77.8 us (0.79)
  waiting for transfers between devices: 35.5 us -> 20.9 us
  Pallas kernels: 42.3 us -> 32.9 us
  starting transfers between devices: 15 us -> 20.4 us
  local copies, waits for them, and re-layouts: 3.41 us -> 1.37 us
    ppermute x13 -> x17, waiting for transfers between devices: 31.4 us -> 16.8 us  [swap(): return lax.ppermute(value, axis, [(i, i ^ mask) for i in range(count)])]
    pallas_call x11 -> x14, Pallas kernels: 30.2 us -> 21.4 us  [the longest x5 14.1 us: conv(): pl.pallas_call(body, out_shape=[jax.ShapeDtypeStruct((rows, cols, width),...]
    ppermute x13 -> x17, starting transfers between devices: 8.34 us -> 13.7 us  [swap(): return lax.ppermute(value, axis, [(i, i ^ mask) for i in range(count)])]
    unnamed x12 -> x4, local copies, waits for them, and re-layouts: 3.27 us -> 0.02 us
  transfers between devices with their start and end apart: 15 -> 19, of which waited for: 8 -> 7; matrix products, arithmetic and copies ran while one was open for 0% -> 0% of each run, Pallas kernels for 37% -> 39%
where the time goes in v3:
time: 77.8 us; the launch traced here: 77.6 us
  Pallas kernels  32.9 us (42%)
  waiting for transfers between devices  20.9 us (27%)
  starting transfers between devices  20.4 us (26%)
  local copies, waits for them, and re-layouts  1.37 us (2%)
  between operations  1.34 us (2%)
  other arithmetic  0.8 us (1%)
    ppermute x17, waiting for transfers between devices, swap(): return lax.ppermute(value, axis, [(i, i ^ mask) for i in range(count)])  16.8 us
    pallas_call x5, Pallas kernels, conv(): pl.pallas_call(body, out_shape=[jax.ShapeDtypeStruct((rows, cols, width),...  14.1 us
    ppermute x17, starting transfers between devices, swap(): return lax.ppermute(value, axis, [(i, i ^ mask) for i in range(count)])  13.7 us
    pallas_call x1, Pallas kernels, begin(): pl.pallas_call(begin_kernel, out_shape=(jax.ShapeDtypeStruct((4, total, w...  6.41 us
    ppermute x1, starting transfers between devices, swap_rows(): return lax.ppermute(value, ('lat', 'lon'), pairs)  4.13 us
    ppermute x1, waiting for transfers between devices, swap_next(): lax.ppermute(value, axis, [(i, (i + (1 if i % 2 else -1)) % count) for i...  4.04 us
    pallas_call x1, Pallas kernels, outer_taps(): pl.pallas_call(body, out_shape=jax.ShapeDtypeStruct((6, width, width), F3...  3.74 us
    pallas_call x2, Pallas kernels, put_blocks(): pl.pallas_call(body, out_shape=[jax.ShapeDtypeStruct((total, width), F32)...  3.36 us
  transfers between devices with their start and end apart: 19, of which 7 were waited for; matrix products, arithmetic and copies ran while one was open for 0% of the time, Pallas kernels for 39%

profile of v3, /device:TPU:0, one launch (start us, length us, event | category | flops | bytes accessed | tf_op | source)
XLA Modules:
  0.0 77.6 jit_solution(6628989493559412036)
XLA Ops:
  1.3 0.8 %constant_dynamic-slice_fusion.1 = (bf16[1,45,256]{2,1,0:T(8,128)(2,1)S(1)}, bf16[1,45,256]{2,1,0:T(8,128)(2,1)S(1)}, bf16[1,45,256]{2,1,0:T(8,128)(2,1)S(1)}, b...) fusion(bf16[90,45,256]{2,1,0:T(8,128)(2,1)} %field_hbm, ...), kind=kLoop, calls=%fused_computation.54 | loop fusion | bytes 276488 | tf_op jit(solution)/shard_map/jit(dynamic_index_in_dim)/dynamic_slice | solution.py:603
  2.1 4.1 %collective-permute-start = (bf16[2,45,256]{2,1,0:T(8,128)(2,1)S(1)}, bf16[2,45,256]{2,1,0:T(8,128)(2,1)S(1)}, u32[]{:S(2)}, u32[]{:S(2)}) collective-permute-start(bf16[2,45,256]{2,1,0:T(8,128)(2,1)S(1)} %pad_maximum_fusion.6), channel_id=1, source_target_pairs={{0,4},{1,5},{2,6},{3,7},{4,0},{5,1},{6,2},{7,3},{8,16},{9,17},{10,... | collective-permute-start | bytes 138248 | tf_op jit(solution)/shard_map/ppermute | solution.py:550
  6.7 6.4 %shard_map.58 = (bf16[4,90,256]{2,1,0:T(8,128)(2,1)S(1)}, bf16[4416,768]{1,0:T(8,128)(2,1)S(1)}, bf16[256,4608]{1,0:T(8,128)(2,1)S(1)}, f32[3,256,256]{2,1,0:T(8,128)S(1)}, bf16[90,45,256]{2,1,0:T(8,128)(2,1)S(1)}) custom-call(bf16[90,45,256]{2,1,0:T(8,128)(2,1)} %field_hbm, bf16[90,45,256]{2,1,0:T(8,128)(2,1)} %cot_hbm), custom_call_target="tpu_custom_call" | custom-call | flops 2264924160 | bytes 4423680 | tf_op jit(solution)/shard_map/pallas_call | solution.py:306
  13.2 3.7 %shard_map.65.outer = f32[6,256,256]{2,1,0:T(8,128)S(1)} custom-call(bf16[4416,768]{1,0:T(8,128)(2,1)S(1)} %get-tuple-element.56.old.window, bf16[256,4608]{1,0:T(8,128)(2,1)S(1)} %get-tuple-element.65.turned), custom_call_target="tpu_custom_call" | custom-call | flops 3397386240 | bytes 4423680 | tf_op jit(solution)/shard_map/pallas_call | solution.py:354
  17.2 2.5 %collective-permute-start.2 = (bf16[2,92,256]{2,1,0:T(8,128)(2,1)S(1)}, bf16[2,92,256]{2,1,0:T(8,128)(2,1)S(1)}, u32[]{:S(2)}, u32[]{:S(2)}) collective-permute-start(bf16[2,92,256]{2,1,0:T(8,128)(2,1)S(1)} %get-tuple-element.100), channel_id=1, source_target_pairs={{0,7},{1,2},{2,1},{3,4},{4,3},{5,6},{6,5},{7,0},{8,15},{9,10},{10,... | collective-permute-start | bytes 282632 | tf_op jit(solution)/shard_map/ppermute | solution.py:537
  19.8 4.0 %collective-permute-done.2 = bf16[2,92,256]{2,1,0:T(8,128)(2,1)S(1)} collective-permute-done((bf16[2,92,256]{2,1,0:T(8,128)(2,1)S(1)}, bf16[2,92,256]{2,1,0:T(8,128)(2,1)S(1)}, u32[]{:S(2)}, u32[]{:S(2)}) %collective-permute-start.2) | collective-permute-done | bytes 94240 | tf_op jit(solution)/shard_map/ppermute | solution.py:537
  24.5 2.8 %collective-permute-done.4.refs_1_ = f32[1152,256]{1,0:T(8,128)S(1)} collective-permute-done((f32[1152,256]{1,0:T(8,128)S(1)}, f32[1152,256]{1,0:T(8,128)S(1)}, u32[]{:S(2)}, u32[]{:S(2)}) %collective-permute-start.4) | collective-permute-done | bytes 1179680 | tf_op jit(solution)/shard_map/ppermute | solution.py:532
  27.4 0.7 shard_map.67
  28.1 1.6 %collective-permute-start.5 = (f32[144,256]{1,0:T(8,128)S(1)}, f32[144,256]{1,0:T(8,128)S(1)}, u32[]{:S(2)}, u32[]{:S(2)}) collective-permute-start(f32[144,256]{1,0:T(8,128)S(1)} %get-tuple-element.69), channel_id=1, source_target_pairs={{0,8},{8,0},{16,24},{24,16},{1,9},{9,1},{17,25},{25,17},{2,10},{10... | collective-permute-start | bytes 442376 | tf_op jit(solution)/shard_map/ppermute | solution.py:532
  29.7 1.2 %collective-permute-start.6 = (f32[144,256]{1,0:T(8,128)S(1)}, f32[144,256]{1,0:T(8,128)S(1)}, u32[]{:S(2)}, u32[]{:S(2)}) collective-permute-start(f32[144,256]{1,0:T(8,128)S(1)} %get-tuple-element.70), channel_id=1, source_target_pairs={{0,16},{8,24},{16,0},{24,8},{1,17},{9,25},{17,1},{25,9},{2,18},{10... | collective-permute-start | bytes 442376 | tf_op jit(solution)/shard_map/ppermute | solution.py:532
  30.9 0.8 %collective-permute-start.7 = (f32[144,256]{1,0:T(8,128)S(1)}, f32[144,256]{1,0:T(8,128)S(1)}, u32[]{:S(2)}, u32[]{:S(2)}) collective-permute-start(f32[144,256]{1,0:T(8,128)S(1)} %get-tuple-element.71), channel_id=1, source_target_pairs={{0,24},{8,16},{16,8},{24,0},{1,25},{9,17},{17,9},{25,1},{2,26},{10... | collective-permute-start | bytes 442376 | tf_op jit(solution)/shard_map/ppermute | solution.py:532
  32.0 1.0 %shard_map.61.refs_0_ = bf16[4416,768]{1,0:T(8,128)(2,1)S(1)} custom-call(bf16[4416,768]{1,0:T(8,128)(2,1)S(1)} %get-tuple-element.56.old.window, bf16[2,45,256]{2,1,0:T(8,128)(2,1)S(1)} %get-tuple-element.107.ends, bf16[2,92,256]{2,1,0:T(8,128)(2,1)S(1)} %get-tuple-element.95.sides), custom_call_target="tpu_custom_call", output_to_operand_aliasing={{}: (0, {})} | custom-call | bytes 5898240 | tf_op jit(solution)/shard_map/pallas_call | solution.py:161
  33.0 1.9 %collective-permute-done.5.refs_1_ = f32[144,256]{1,0:T(8,128)S(1)} collective-permute-done((f32[144,256]{1,0:T(8,128)S(1)}, f32[144,256]{1,0:T(8,128)S(1)}, u32[]{:S(2)}, u32[]{:S(2)}) %collective-permute-start.5) | collective-permute-done | bytes 147488 | tf_op jit(solution)/shard_map/ppermute | solution.py:532
  34.9 2.3 %collective-permute-done.6.refs_2_ = f32[144,256]{1,0:T(8,128)S(1)} collective-permute-done((f32[144,256]{1,0:T(8,128)S(1)}, f32[144,256]{1,0:T(8,128)S(1)}, u32[]{:S(2)}, u32[]{:S(2)}) %collective-permute-start.6) | collective-permute-done | bytes 147488 | tf_op jit(solution)/shard_map/ppermute | solution.py:532
  37.2 1.4 %collective-permute-done.7.refs_3_ = f32[144,256]{1,0:T(8,128)S(1)} collective-permute-done((f32[144,256]{1,0:T(8,128)S(1)}, f32[144,256]{1,0:T(8,128)S(1)}, u32[]{:S(2)}, u32[]{:S(2)}) %collective-permute-start.7) | collective-permute-done | bytes 147488 | tf_op jit(solution)/shard_map/ppermute | solution.py:532
  39.2 1.7 %collective-permute-start.8 = (f32[72,256]{1,0:T(8,128)S(1)}, f32[72,256]{1,0:T(8,128)S(1)}, u32[]{:S(2)}, u32[]{:S(2)}) collective-permute-start(f32[72,256]{1,0:T(8,128)S(1)} %get-tuple-element.73), channel_id=1, source_target_pairs={{0,2},{1,3},{2,0},{3,1},{4,6},{5,7},{6,4},{7,5},{8,10},{9,11},{10,... | collective-permute-start | bytes 221192 | tf_op jit(solution)/shard_map/ppermute | solution.py:532
  41.5 0.9 %collective-permute-start.10 = (f32[72,256]{1,0:T(8,128)S(1)}, f32[72,256]{1,0:T(8,128)S(1)}, u32[]{:S(2)}, u32[]{:S(2)}) collective-permute-start(f32[72,256]{1,0:T(8,128)S(1)} %get-tuple-element.78), channel_id=1, source_target_pairs={{0,8},{8,0},{16,24},{24,16},{1,9},{9,1},{17,25},{25,17},{2,10},{10... | collective-permute-start | bytes 221192 | tf_op jit(solution)/shard_map/ppermute | solution.py:532
  42.3 1.5 %collective-permute-start.11 = (f32[72,256]{1,0:T(8,128)S(1)}, f32[72,256]{1,0:T(8,128)S(1)}, u32[]{:S(2)}, u32[]{:S(2)}) collective-permute-start(f32[72,256]{1,0:T(8,128)S(1)} %get-tuple-element.79), channel_id=1, source_target_pairs={{0,16},{8,24},{16,0},{24,8},{1,17},{9,25},{17,1},{25,9},{2,18},{10... | collective-permute-start | bytes 221192 | tf_op jit(solution)/shard_map/ppermute | solution.py:532
  43.9 1.2 %collective-permute-start.12 = (f32[72,256]{1,0:T(8,128)S(1)}, f32[72,256]{1,0:T(8,128)S(1)}, u32[]{:S(2)}, u32[]{:S(2)}) collective-permute-start(f32[72,256]{1,0:T(8,128)S(1)} %get-tuple-element.80), channel_id=1, source_target_pairs={{0,24},{8,16},{16,8},{24,0},{1,25},{9,17},{17,9},{25,1},{2,26},{10... | collective-permute-start | bytes 221192 | tf_op jit(solution)/shard_map/ppermute | solution.py:532
  45.0 3.1 %shard_map.62.refs_2_ = bf16[45,45,256]{2,1,0:T(8,128)(2,1)S(1)} custom-call(bf16[4416,768]{1,0:T(8,128)(2,1)S(1)} %shard_map.61.refs_0_, bf16[3,768,256]{2,1,0:T(8,128)(2,1)S(1)} %bitcast.126), custom_call_target="tpu_custom_call" | custom-call | flops 2548039680 | bytes 2211840 | tf_op jit(solution)/shard_map/pallas_call | solution.py:220
  48.1 1.4 %shard_map.59.refs_1_ = bf16[4416,768]{1,0:T(8,128)(2,1)S(1)} custom-call(bf16[90,45,256]{2,1,0:T(8,128)(2,1)S(1)} %get-tuple-element.49.field, bf16[2,45,256]{2,1,0:T(8,128)(2,1)S(1)} %get-tuple-element.108.ends, bf16[2,92,256]{2,1,0:T(8,128)(2,1)S(1)} %get-tuple-element.96.sides), custom_call_target="tpu_custom_call" | custom-call | bytes 8847360 | tf_op jit(solution)/shard_map/pallas_call | solution.py:129
  50.2 3.1 %shard_map.63 = (bf16[45,45,256]{2,1,0:T(8,128)(2,1)S(1)}, bf16[90,45,256]{2,1,0:T(8,128)(2,1)}) custom-call(bf16[4416,768]{1,0:T(8,128)(2,1)S(1)} %shard_map.61.refs_0_, bf16[3,768,256]{2,1,0:T(8,128)(2,1)S(1)} %bitcast.127, bf16[45,45,256]{2,1,0:T(8,128)(2,1)S(1)} %shard_map.62.refs_2_), custom_call_target="tpu_custom_call" | custom-call | flops 2548039680 | bytes 2211840 | tf_op jit(solution)/shard_map/pallas_call | solution.py:220
  53.3 4.0 %collective-permute-done.13.second = f32[144,256]{1,0:T(8,128)S(1)} collective-permute-done((f32[144,256]{1,0:T(8,128)S(1)}, f32[144,256]{1,0:T(8,128)S(1)}, u32[]{:S(2)}, u32[]{:S(2)}) %collective-permute-start.13) | collective-permute-done | bytes 147488 | tf_op jit(solution)/shard_map/ppermute | solution.py:532
  57.6 4.4 %collective-permute-done.14 = f16[152,256]{1,0:T(8,128)(2,1)S(1)} collective-permute-done((f16[152,256]{1,0:T(8,128)(2,1)S(1)}, f16[152,256]{1,0:T(8,128)(2,1)S(1)}, u32[]{:S(2)}, u32[]{:S(2)}) %collective-permute-start.14) | collective-permute-done | bytes 77856 | tf_op jit(solution)/shard_map/ppermute | solution.py:532
  62.0 0.9 %collective-permute-start.15 = (f16[2,152,256]{2,1,0:T(8,128)(2,1)S(1)}, f16[2,152,256]{2,1,0:T(8,128)(2,1)S(1)}, u32[]{:S(2)}, u32[]{:S(2)}) collective-permute-start(f16[2,152,256]{2,1,0:T(8,128)(2,1)S(1)} %get-tuple-element.106), channel_id=1, source_target_pairs={{0,8},{8,0},{16,24},{24,16},{1,9},{9,1},{17,25},{25,17},{2,10},{10... | collective-permute-start | bytes 466952 | tf_op jit(solution)/shard_map/ppermute | solution.py:532
  62.9 1.2 %collective-permute-start.16 = (f16[2,152,256]{2,1,0:T(8,128)(2,1)S(1)}, f16[2,152,256]{2,1,0:T(8,128)(2,1)S(1)}, u32[]{:S(2)}, u32[]{:S(2)}) collective-permute-start(f16[2,152,256]{2,1,0:T(8,128)(2,1)S(1)} %get-tuple-element.106), channel_id=1, source_target_pairs={{0,16},{8,24},{16,0},{24,8},{1,17},{9,25},{17,1},{25,9},{2,18},{10... | collective-permute-start | bytes 466952 | tf_op jit(solution)/shard_map/ppermute | solution.py:532
  64.2 1.4 %collective-permute-start.17 = (f16[2,152,256]{2,1,0:T(8,128)(2,1)S(1)}, f16[2,152,256]{2,1,0:T(8,128)(2,1)S(1)}, u32[]{:S(2)}, u32[]{:S(2)}) collective-permute-start(f16[2,152,256]{2,1,0:T(8,128)(2,1)S(1)} %get-tuple-element.106), channel_id=1, source_target_pairs={{0,24},{8,16},{16,8},{24,0},{1,25},{9,17},{17,9},{25,1},{2,26},{10... | collective-permute-start | bytes 466952 | tf_op jit(solution)/shard_map/ppermute | solution.py:532
  65.6 3.8 %shard_map.64 = (bf16[45,45,256]{2,1,0:T(8,128)(2,1)S(1)}, bf16[90,45,256]{2,1,0:T(8,128)(2,1)}) custom-call(s32[2]{0:T(128)S(1)} %pad_add_fusion.refs_0_, bf16[4416,768]{1,0:T(8,128)(2,1)S(1)} %shard_map.59.refs_1_, bf16[3,768,256]{2,1,0:T(8,128)(2,1)S(1)} %shard_map.60.refs_2_, ...), custom_call_target="tpu_custom_call", output_to_operand_aliasing={{1}: (4, {})} | custom-call | flops 2548039680 | bytes 2211840 | tf_op jit(solution)/shard_map/pallas_call | solution.py:220
  69.4 1.6 %shard_map.72 = (bf16[15,45,256]{2,1,0:T(8,128)(2,1)S(1)}, bf16[90,45,256]{2,1,0:T(8,128)(2,1)}) custom-call(s32[2]{0:T(128)S(1)} %pad_add_fusion.refs_0_, bf16[4416,768]{1,0:T(8,128)(2,1)S(1)} %shard_map.59.refs_1_, bf16[3,768,256]{2,1,0:T(8,128)(2,1)S(1)} %shard_map.60.refs_2_, bf16[45,45,256]{2,1,0:T(8,128)(2,1)S(1)} %get-tuple-element.81.refs_3_), custom_call_target="tpu_custom_call" | custom-call | flops 849346560 | bytes 737280 | tf_op jit(solution)/shard_map/pallas_call | solution.py:220
  71.3 2.4 %shard_map.73 = (bf16[30,45,256]{2,1,0:T(8,128)(2,1)S(1)}, bf16[90,45,256]{2,1,0:T(8,128)(2,1)}) custom-call(s32[2]{0:T(128)S(1)} %pad_add_fusion.refs_0_, bf16[4416,768]{1,0:T(8,128)(2,1)S(1)} %shard_map.59.refs_1_, bf16[3,768,256]{2,1,0:T(8,128)(2,1)S(1)} %shard_map.60.refs_2_, ...), custom_call_target="tpu_custom_call", output_to_operand_aliasing={{1}: (4, {})} | custom-call | flops 1698693120 | bytes 1474560 | tf_op jit(solution)/shard_map/pallas_call | solution.py:220
  73.9 1.8 %shard_map.74 = (f32[2304,256]{1,0:T(8,128)}, bf16[90,45,256]{2,1,0:T(8,128)(2,1)}) custom-call(s32[16]{0:T(128)S(1)} %stack.312.where, f32[8,144,256]{2,1,0:T(8,128)S(1)} %bitcast.124, bf16[30,45,256]{2,1,0:T(8,128)(2,1)S(1)} %get-tuple-element.84.rest_0_, bf16[90,45,256]{2,1,0:T(8,128)(2,1)} %get-tuple-element.85.rest_1_), custom_call_target="tpu_custom_call", output_to_operand_aliasing={{1}: (3, {})} | custom-call | tf_op jit(solution)/shard_map/pallas_call | solution.py:516
  75.9 1.6 %shard_map.75 = f32[2304,256]{1,0:T(8,128)} custom-call(s32[16]{0:T(128)S(1)} %stack.295.where, f32[8,144,256]{2,1,0:T(8,128)S(1)} %bitcast.125, f32[2304,256]{1,0:T(8,128)} %get-tuple-element.88.rest_0_), custom_call_target="tpu_custom_call", output_to_operand_aliasing={{}: (2, {})} | custom-call | tf_op jit(solution)/shard_map/pallas_call | solution.py:516
  (59 shorter events, 5.0 us)
Async XLA Ops:
  2.1 14.8 %collective-permute-start = (bf16[2,45,256]{2,1,0:T(8,128)(2,1)S(1)}, bf16[2,45,256]{2,1,0:T(8,128)(2,1)S(1)}, u32[]{:S(2)}, u32[]{:S(2)}) collective-permute-start(bf16[2,45,256]{2,1,0:T(8,128)(2,1)S(1)} %pad_maximum_fusion.6), channel_id=1, source_target_pairs={{0,4},{1,5},{2,6},{3,7},{4,0},{5,1},{6,2},{7,3},{8,16},{9,17},{10,... | collective-permute-start | bytes 138248 | tf_op jit(solution)/shard_map/ppermute | solution.py:550
  6.3 10.7 %collective-permute-start.1 = (bf16[2,45,256]{2,1,0:T(8,128)(2,1)S(1)}, bf16[2,45,256]{2,1,0:T(8,128)(2,1)S(1)}, u32[]{:S(2)}, u32[]{:S(2)}) collective-permute-start(bf16[2,45,256]{2,1,0:T(8,128)(2,1)S(1)} %pad_maximum_fusion.7), channel_id=1, source_target_pairs={{0,8},{8,0},{16,24},{24,16},{1,9},{9,1},{17,25},{25,17},{2,10},{10... | collective-permute-start | bytes 138248 | tf_op jit(solution)/shard_map/ppermute | solution.py:532
  17.2 6.6 %collective-permute-start.2 = (bf16[2,92,256]{2,1,0:T(8,128)(2,1)S(1)}, bf16[2,92,256]{2,1,0:T(8,128)(2,1)S(1)}, u32[]{:S(2)}, u32[]{:S(2)}) collective-permute-start(bf16[2,92,256]{2,1,0:T(8,128)(2,1)S(1)} %get-tuple-element.100), channel_id=1, source_target_pairs={{0,7},{1,2},{2,1},{3,4},{4,3},{5,6},{6,5},{7,0},{8,15},{9,10},{10,... | collective-permute-start | bytes 282632 | tf_op jit(solution)/shard_map/ppermute | solution.py:537
  19.7 4.1 %collective-permute-start.3 = (bf16[2,92,256]{2,1,0:T(8,128)(2,1)S(1)}, bf16[2,92,256]{2,1,0:T(8,128)(2,1)S(1)}, u32[]{:S(2)}, u32[]{:S(2)}) collective-permute-start(bf16[2,92,256]{2,1,0:T(8,128)(2,1)S(1)} %get-tuple-element.99), channel_id=1, source_target_pairs={{0,1},{1,0},{2,3},{3,2},{4,5},{5,4},{6,7},{7,6},{8,9},{9,8},{10,11... | collective-permute-start | bytes 282632 | tf_op jit(solution)/shard_map/ppermute | solution.py:532
  24.4 7.2 %copy-start = (bf16[3,3,256,256]{3,2,1,0:T(8,128)(2,1)S(1)}, bf16[3,3,256,256]{3,2,1,0:T(8,128)(2,1)}, u32[]{:S(2)}) copy-start(bf16[3,3,256,256]{3,2,1,0:T(8,128)(2,1)} %kernel) | copy-start | bytes 3538948
  24.4 2.9 %collective-permute-start.4 = (f32[1152,256]{1,0:T(8,128)S(1)}, f32[1152,256]{1,0:T(8,128)S(1)}, u32[]{:S(2)}, u32[]{:S(2)}) collective-permute-start(f32[1152,256]{1,0:T(8,128)S(1)} %get-tuple-element.67), channel_id=1, source_target_pairs={{0,1},{1,0},{2,3},{3,2},{4,5},{5,4},{6,7},{7,6},{8,9},{9,8},{10,11... | collective-permute-start | bytes 3538952 | tf_op jit(solution)/shard_map/ppermute | solution.py:532
  28.0 12.9 %collective-permute-start.9 = (f32[288,256]{1,0:T(8,128)S(1)}, f32[288,256]{1,0:T(8,128)S(1)}, u32[]{:S(2)}, u32[]{:S(2)}) collective-permute-start(f32[288,256]{1,0:T(8,128)S(1)} %get-tuple-element.76), channel_id=1, source_target_pairs={{0,2},{1,3},{2,0},{3,1},{4,6},{5,7},{6,4},{7,5},{8,10},{9,11},{10,... | collective-permute-start | bytes 884744 | tf_op jit(solution)/shard_map/ppermute | solution.py:532
  28.1 6.8 %collective-permute-start.5 = (f32[144,256]{1,0:T(8,128)S(1)}, f32[144,256]{1,0:T(8,128)S(1)}, u32[]{:S(2)}, u32[]{:S(2)}) collective-permute-start(f32[144,256]{1,0:T(8,128)S(1)} %get-tuple-element.69), channel_id=1, source_target_pairs={{0,8},{8,0},{16,24},{24,16},{1,9},{9,1},{17,25},{25,17},{2,10},{10... | collective-permute-start | bytes 442376 | tf_op jit(solution)/shard_map/ppermute | solution.py:532
  29.7 7.5 %collective-permute-start.6 = (f32[144,256]{1,0:T(8,128)S(1)}, f32[144,256]{1,0:T(8,128)S(1)}, u32[]{:S(2)}, u32[]{:S(2)}) collective-permute-start(f32[144,256]{1,0:T(8,128)S(1)} %get-tuple-element.70), channel_id=1, source_target_pairs={{0,16},{8,24},{16,0},{24,8},{1,17},{9,25},{17,1},{25,9},{2,18},{10... | collective-permute-start | bytes 442376 | tf_op jit(solution)/shard_map/ppermute | solution.py:532
  30.9 7.7 %collective-permute-start.7 = (f32[144,256]{1,0:T(8,128)S(1)}, f32[144,256]{1,0:T(8,128)S(1)}, u32[]{:S(2)}, u32[]{:S(2)}) collective-permute-start(f32[144,256]{1,0:T(8,128)S(1)} %get-tuple-element.71), channel_id=1, source_target_pairs={{0,24},{8,16},{16,8},{24,0},{1,25},{9,17},{17,9},{25,1},{2,26},{10... | collective-permute-start | bytes 442376 | tf_op jit(solution)/shard_map/ppermute | solution.py:532
  39.2 10.4 %collective-permute-start.8 = (f32[72,256]{1,0:T(8,128)S(1)}, f32[72,256]{1,0:T(8,128)S(1)}, u32[]{:S(2)}, u32[]{:S(2)}) collective-permute-start(f32[72,256]{1,0:T(8,128)S(1)} %get-tuple-element.73), channel_id=1, source_target_pairs={{0,2},{1,3},{2,0},{3,1},{4,6},{5,7},{6,4},{7,5},{8,10},{9,11},{10,... | collective-permute-start | bytes 221192 | tf_op jit(solution)/shard_map/ppermute | solution.py:532
  41.5 8.0 %collective-permute-start.10 = (f32[72,256]{1,0:T(8,128)S(1)}, f32[72,256]{1,0:T(8,128)S(1)}, u32[]{:S(2)}, u32[]{:S(2)}) collective-permute-start(f32[72,256]{1,0:T(8,128)S(1)} %get-tuple-element.78), channel_id=1, source_target_pairs={{0,8},{8,0},{16,24},{24,16},{1,9},{9,1},{17,25},{25,17},{2,10},{10... | collective-permute-start | bytes 221192 | tf_op jit(solution)/shard_map/ppermute | solution.py:532
  42.3 7.2 %collective-permute-start.11 = (f32[72,256]{1,0:T(8,128)S(1)}, f32[72,256]{1,0:T(8,128)S(1)}, u32[]{:S(2)}, u32[]{:S(2)}) collective-permute-start(f32[72,256]{1,0:T(8,128)S(1)} %get-tuple-element.79), channel_id=1, source_target_pairs={{0,16},{8,24},{16,0},{24,8},{1,17},{9,25},{17,1},{25,9},{2,18},{10... | collective-permute-start | bytes 221192 | tf_op jit(solution)/shard_map/ppermute | solution.py:532
  43.9 5.7 %collective-permute-start.12 = (f32[72,256]{1,0:T(8,128)S(1)}, f32[72,256]{1,0:T(8,128)S(1)}, u32[]{:S(2)}, u32[]{:S(2)}) collective-permute-start(f32[72,256]{1,0:T(8,128)S(1)} %get-tuple-element.80), channel_id=1, source_target_pairs={{0,24},{8,16},{16,8},{24,0},{1,25},{9,17},{17,9},{25,1},{2,26},{10... | collective-permute-start | bytes 221192 | tf_op jit(solution)/shard_map/ppermute | solution.py:532
  49.6 7.8 %collective-permute-start.13 = (f32[144,256]{1,0:T(8,128)S(1)}, f32[144,256]{1,0:T(8,128)S(1)}, u32[]{:S(2)}, u32[]{:S(2)}) collective-permute-start(f32[144,256]{1,0:T(8,128)S(1)} %shard_map.70.first), channel_id=1, source_target_pairs={{0,4},{1,5},{2,6},{3,7},{4,0},{5,1},{6,2},{7,3},{8,12},{9,13},{10,... | collective-permute-start | bytes 442376 | tf_op jit(solution)/shard_map/ppermute | solution.py:532
  57.5 4.5 %collective-permute-start.14 = (f16[152,256]{1,0:T(8,128)(2,1)S(1)}, f16[152,256]{1,0:T(8,128)(2,1)S(1)}, u32[]{:S(2)}, u32[]{:S(2)}) collective-permute-start(f16[152,256]{1,0:T(8,128)(2,1)S(1)} %convert_element_type.15), channel_id=1, source_target_pairs={{0,2},{1,3},{2,0},{3,1},{4,6},{5,7},{6,4},{7,5},{8,10},{9,11},{10,... | collective-permute-start | bytes 233480 | tf_op jit(solution)/shard_map/ppermute | solution.py:532
  62.0 9.0 %collective-permute-start.15 = (f16[2,152,256]{2,1,0:T(8,128)(2,1)S(1)}, f16[2,152,256]{2,1,0:T(8,128)(2,1)S(1)}, u32[]{:S(2)}, u32[]{:S(2)}) collective-permute-start(f16[2,152,256]{2,1,0:T(8,128)(2,1)S(1)} %get-tuple-element.106), channel_id=1, source_target_pairs={{0,8},{8,0},{16,24},{24,16},{1,9},{9,1},{17,25},{25,17},{2,10},{10... | collective-permute-start | bytes 466952 | tf_op jit(solution)/shard_map/ppermute | solution.py:532
  62.9 8.1 %collective-permute-start.16 = (f16[2,152,256]{2,1,0:T(8,128)(2,1)S(1)}, f16[2,152,256]{2,1,0:T(8,128)(2,1)S(1)}, u32[]{:S(2)}, u32[]{:S(2)}) collective-permute-start(f16[2,152,256]{2,1,0:T(8,128)(2,1)S(1)} %get-tuple-element.106), channel_id=1, source_target_pairs={{0,16},{8,24},{16,0},{24,8},{1,17},{9,25},{17,1},{25,9},{2,18},{10... | collective-permute-start | bytes 466952 | tf_op jit(solution)/shard_map/ppermute | solution.py:532
  64.2 6.9 %collective-permute-start.17 = (f16[2,152,256]{2,1,0:T(8,128)(2,1)S(1)}, f16[2,152,256]{2,1,0:T(8,128)(2,1)S(1)}, u32[]{:S(2)}, u32[]{:S(2)}) collective-permute-start(f16[2,152,256]{2,1,0:T(8,128)(2,1)S(1)} %get-tuple-element.106), channel_id=1, source_target_pairs={{0,24},{8,16},{16,8},{24,0},{1,25},{9,17},{17,9},{25,1},{2,26},{10... | collective-permute-start | bytes 466952 | tf_op jit(solution)/shard_map/ppermute | solution.py:532
  71.3 4.5 %collective-permute-start.18 = (f16[4,2,152,256]{3,2,1,0:T(8,128)(2,1)S(1)}, f16[4,2,152,256]{3,2,1,0:T(8,128)(2,1)S(1)}, u32[]{:S(2)}, u32[]{:S(2)}) collective-permute-start(f16[4,2,152,256]{3,2,1,0:T(8,128)(2,1)S(1)} %pad_maximum_fusion), channel_id=1, source_target_pairs={{0,1},{1,0},{2,3},{3,2},{4,5},{5,4},{6,7},{7,6},{8,9},{9,8},{10,11... | collective-permute-start | bytes 1867784 | tf_op jit(solution)/shard_map/ppermute | solution.py:532

commit v4 on v3

--- a/solution.py
+++ b/solution.py
@@ -236,65 +236,78 @@
     return 128 // math.gcd(128, wide)
 
 
-def fetch_chunk(total):
-    return max(n for n in range(1, 19) if total % n == 0)
-
-
-def begin_kernel(field_hbm, cot_hbm, columns, window, turned, taps, cot, field, column_rows, sems):
+def begin_kernel(field_hbm, cot_hbm, columns, window, turned, sums, cot, field, column_rows, sems):
     total, cols, width = field.shape
     wide = padded_width(cols)
-    part = fetch_chunk(total)
-    copies = [
-        pltpu.make_async_copy(source.at[pl.ds(at, part)], target.at[pl.ds(at, part)], sems.at[at // part, j])
-        for at in range(0, total, part)
-        for j, (source, target) in enumerate(((cot_hbm, cot), (field_hbm, field)))
-    ]
-    for copy in copies:
-        copy.start()
+    part = 2 * turn_group(wide)
+    chunks = -(-total // part)
+    sizes = [min(part, total - at) for at in range(0, total, part)]
+
+    def copies(i, size):
+        at = i * part
+        return [
+            pltpu.make_async_copy(source.at[pl.ds(at, size)], target.at[pl.ds(at, size)], sems.at[i, j])
+            for j, (source, target) in enumerate(((field_hbm, field), (cot_hbm, cot)))
+        ]
+
+    for i, size in enumerate(sizes):
+        for copy in copies(i, size):
+            copy.start()
     empty = jnp.zeros((1, width), F32)
     blank = jnp.zeros((wide - cols, width), F32)
-    group = turn_group(wide)
-    span = group * wide
     for k in range(3):
         window[0:wide, k * width : (k + 1) * width] = jnp.zeros((wide, width), BF16)
         window[(total + 1) * wide : (total + 2) * wide, k * width : (k + 1) * width] = jnp.zeros((wide, width), BF16)
-
-    for at in range(0, total, part):
-        copies[2 * (at // part)].wait()
-        copies[2 * (at // part) + 1].wait()
-
-        @pl.loop(at, at + part)
-        def _(r):
-            row, other = field[r], cot[r]
-            start = pl.multiple_of((r + 1) * wide, 16)
-            for tap, piece in enumerate(shifted(row, empty, empty, wide)):
-                window[pl.ds(start, wide), tap * width : (tap + 1) * width] = piece
-            for k, value in enumerate((row, other)):
-                value = value.astype(F32)
-                column_rows[2 * k, pl.ds(r, 1)] = value[0:1]
-                column_rows[2 * k + 1, pl.ds(r, 1)] = value[cols - 1 : cols]
-
+    sums[...] = jnp.zeros_like(sums)
+
+    def lay(i, size):
+        for copy in copies(i, size):
+            copy.wait()
+        step = size if size % 2 else size // 2
+        for low in range(0, size, step):
+            flat = []
+            for u in range(low, low + step):
+                r = i * part + u
+                row, other = field[r], cot[r].astype(F32)
+                start = pl.multiple_of((r + 1) * wide, 16)
+                for tap, piece in enumerate(shifted(row, empty, empty, wide)):
+                    window[pl.ds(start, wide), tap * width : (tap + 1) * width] = piece
+                row = row.astype(F32)
+                for k, value in enumerate((row[0:1], row[cols - 1 : cols], other[0:1], other[cols - 1 : cols])):
+                    column_rows[k, pl.ds(r, 1)] = value
+                flat += [other, blank]
+            value = jnp.concatenate(flat, 0).T.astype(BF16)
+            if step * wide % 128 == 0:
+                at = pl.multiple_of((i * part + low) * wide, 128)
+                turned[:, pl.ds(at, step * wide)] = value
+            else:
+                turned[:, (i * part + low) * wide : (i * part + low + step) * wide] = value
+
+    def multiply(i, size):
+        at = i * part * wide
+        at = at if isinstance(at, int) else pl.multiple_of(at, 128)
+        sums[...] += jnp.dot(
+            turned[:, pl.ds(at, size * wide)],
+            window[pl.ds(at + wide, size * wide), :],
+            preferred_element_type=F32,
+        )
+
+    lay(0, sizes[0])
+
+    @pl.loop(1, chunks - 1)
+    def _(i):
+        lay(i, part)
+        multiply(i - 1, part)
+
+    if chunks > 1:
+        lay(chunks - 1, sizes[-1])
+        multiply(chunks - 2, part)
+    multiply(chunks - 1, sizes[-1])
     columns[...] = column_rows[...].astype(BF16)
 
-    def chunk(start, count):
-        return [part for j in range(count) for part in (cot[start + j].astype(F32), blank)]
-
-    @pl.loop(0, total // group)
-    def _(i):
-        value = jnp.concatenate(chunk(i * group, group), 0)
-        turned[:, pl.ds(pl.multiple_of(i * span, 128), span)] = value.T.astype(BF16)
-
-    rest = total % group
-    if rest:
-        start = total - rest
-        value = jnp.concatenate(chunk(start, rest) + [jnp.zeros((span - rest * wide, width), F32)], 0)
-        turned[:, start * wide : start * wide + span] = value.T.astype(BF16)
-    tap_row(turned, window, taps, total * wide, wide, 0)
-
-
-def tap_row(turned, window, taps, cells, start, slot):
+
+def store_turned(value, taps, slot):
     width = taps.shape[-1]
-    value = jnp.dot(turned[:, :cells], window[start : start + cells, :], preferred_element_type=F32)
     for b in range(3):
         taps[slot + b] = value[:, b * width : (b + 1) * width].T
 
@@ -309,7 +322,7 @@
             jax.ShapeDtypeStruct((4, total, width), BF16),
             jax.ShapeDtypeStruct(((total + 2) * wide, 3 * width), BF16),
             jax.ShapeDtypeStruct((width, -(-total // group) * group * wide), BF16),
-            jax.ShapeDtypeStruct((3, width, width), F32),
+            jax.ShapeDtypeStruct((width, 3 * width), F32),
             jax.ShapeDtypeStruct(cot.shape, BF16),
         ),
         in_specs=[HBM, HBM],
@@ -317,7 +330,7 @@
         scratch_shapes=[
             pltpu.VMEM(field.shape, BF16),
             pltpu.VMEM((4, total, width), F32),
-            pltpu.SemaphoreType.DMA((total // fetch_chunk(total), 2)),
+            pltpu.SemaphoreType.DMA((-(-total // (2 * group)), 2)),
         ],
         compiler_params=params(12),
         cost_estimate=pl.CostEstimate(
@@ -344,26 +357,30 @@
     )(kernel)
 
 
-def outer_taps(window, turned, total, wide):
+def all_taps(window, turned, middle, total, wide):
     width = turned.shape[0]
-
-    def body(window, turned, taps):
-        tap_row(turned, window, taps, total * wide, 0, 0)
-        tap_row(turned, window, taps, total * wide, 2 * wide, 3)
-
-    return pl.pallas_call(
-        body,
-        out_shape=jax.ShapeDtypeStruct((6, width, width), F32),
-        in_specs=[VMEM, VMEM],
+    cells = total * wide
+
+    def body(window, turned, middle, taps):
+        store_turned(middle[...], taps, 3)
+        for slot, start in ((0, 0), (6, 2 * wide)):
+            store_turned(
+                jnp.dot(turned[:, :cells], window[start : start + cells, :], preferred_element_type=F32), taps, slot
+            )
+
+    return pl.pallas_call(
+        body,
+        out_shape=jax.ShapeDtypeStruct((9, width, width), F32),
+        in_specs=[VMEM] * 3,
         out_specs=VMEM,
         compiler_params=params(8),
         cost_estimate=pl.CostEstimate(
             flops=12 * total * wide * width * width, bytes_accessed=4 * total * wide * width, transcendentals=0
         ),
-    )(window, turned)
-
-
-def edge_kernel(half, middle, outer, ends, sides, rows, columns, send, every, side_rows):
+    )(window, turned, middle)
+
+
+def edge_kernel(half, taps, ends, sides, rows, columns, send, every, side_rows):
     _, cols, width = ends.shape
     wide = padded_width(cols)
     total = columns.shape[1]
@@ -386,7 +403,7 @@
         if a != 1:
             left.append(end_parts[a // 2][b])
             right.append(row_parts[a // 2])
-        value = middle[b] if a == 1 else outer[3 * (a // 2) + b]
+        value = taps[tap]
         if left:
             value = value + lax.dot_general(
                 jnp.concatenate(left, 0),
@@ -398,7 +415,7 @@
     send[...] = every[pl.ds(pl.multiple_of((1 - half[0]) * size, 8), size)]
 
 
-def with_edges(half, middle, outer, ends, sides, rows, columns):
+def with_edges(half, taps, ends, sides, rows, columns):
     _, _, width = ends.shape
     total = columns.shape[1]
     return pl.pallas_call(
@@ -407,14 +424,14 @@
             jax.ShapeDtypeStruct((9 * width // 2, width), F32),
             jax.ShapeDtypeStruct((9 * width, width), F32),
         ),
-        in_specs=[SMEM] + [VMEM] * 6,
+        in_specs=[SMEM] + [VMEM] * 5,
         out_specs=(VMEM, VMEM),
         scratch_shapes=[pltpu.VMEM((2, total + 2, width), F32)],
         compiler_params=params(12),
         cost_estimate=pl.CostEstimate(
             flops=16 * 144 * width * width, bytes_accessed=72 * width * width, transcendentals=0
         ),
-    )(half, middle, outer, ends, sides, rows, columns)
+    )(half, taps, ends, sides, rows, columns)
 
 
 def add_blocks(places, terms, sizes):
@@ -562,7 +579,7 @@
     odd = band & 1
     half_rows = 9 * width // 2
     unit = 16 * bands
-    upper = (half_rows // unit + 1) // 2 * unit
+    upper = half_rows * 5 // 8 // unit * unit
     lower = half_rows - upper
     upper_part, lower_part = upper // bands, lower // 2
     upper_end, lower_end = upper_part // 2, lower_part // bands
@@ -570,12 +587,11 @@
     first_rows = [(band ^ m) * upper_part for m in range(bands)]
     first_rows += [upper + p * lower_part for p in (place, 1 - place)]
 
-    def homes(h):
+    def homes(h, p):
         return vector(
             *[
                 h * half_rows + row
                 for m in range(bands)
-                for p in (place, 1 - place)
                 for row in (
                     (band ^ m) * upper_part + p * upper_end,
                     upper + p * lower_part + (band ^ m) * lower_end,
@@ -593,8 +609,8 @@
         upper=vector(*[p * upper_end for _ in range(bands) for p in (place, 1 - place)]),
         lower=vector(*[(band ^ m) * lower_end for _ in range(2) for m in range(bands)]),
         poles=vector(jnp.where(band == 0, 2, 0), jnp.where(band == bands - 1, 0, 2)),
-        own=homes(mine),
-        other=homes(1 - mine),
+        most_homes=jnp.concatenate([homes(mine, place), homes(mine, 1 - place), homes(1 - mine, place)]),
+        last_homes=homes(1 - mine, 1 - place),
     )
     inputs, kernel, cotangent, facts = lax.optimization_barrier((inputs, kernel, cotangent, facts))
     even_band, even_sector, half = facts["even_band"], facts["even_sector"], facts["half"]
@@ -620,11 +636,11 @@
     first, last = side(0), side(1)
     near = swap(jnp.where(even_sector, last, first), "lon", 1)
     far = swap_next(jnp.where(even_sector, first, last), "lon")
-    outer = outer_taps(window, turned, rows, padded_width(cols))
+    outer = all_taps(window, turned, middle, rows, padded_width(cols))
     sides = jnp.stack([jnp.where(even_sector, far, near), jnp.where(even_sector, near, far)], 1)
 
     edge_rows = jnp.stack([cotangent[0], cotangent[-1]])
-    send, every = with_edges(half, middle, outer, ends[0], sides[0], edge_rows, columns[2:])
+    send, every = with_edges(half, outer, ends[0], sides[0], edge_rows, columns[2:])
 
     weights = kernel.reshape(3, 3 * width, width)
     flipped = flip(kernel)
@@ -659,29 +675,41 @@
             value = terms[0] + terms[1]
 
     coded = last_sum(terms, factor).astype(HALF)
-    got = swap(coded, "lon", 2)
-    coded = jnp.stack([coded, got])
-    got = []
-    for m in range(1, bands):
-        got.append(swap(coded, "lat", m))
-    coded = jnp.stack([coded, *got])
-    got = swap(coded, "lon", 1)
+    other = swap(coded, "lon", 2)
     whole, cuts = 9 * width, (upper_end, lower_end)
-    kernel_grad = put_blocks(facts["own"], decode(coded).reshape(2 * bands, -1, width), cuts, whole, None, flush, inputs.shape)
-    kernel_grad = put_blocks(facts["other"], decode(got).reshape(2 * bands, -1, width), cuts, whole, kernel_grad)
+
+    def spread(value):
+        got = []
+        for m in range(1, bands):
+            got.append(swap(value, "lat", m))
+        return [value, *got]
+
+    near = spread(coded)
+    far = spread(other)
+    near = jnp.stack(near)
+    near_other = swap(near, "lon", 1)
+    near_blocks = decode(near)
+    far = jnp.stack(far)
+    far_other = swap(far, "lon", 1)
+    most = jnp.concatenate([near_blocks, decode(far), decode(near_other)])
+    kernel_grad = put_blocks(facts["most_homes"], most, cuts, whole, None, flush, inputs.shape)
+    kernel_grad = put_blocks(facts["last_homes"], decode(far_other), cuts, whole, kernel_grad)
     return (flush.outputs["outputs"], flush.outputs["input_grad"], kernel_grad.reshape(3, 3, width, width))
 
 
-FORWARD = (0, 45, 90)
-BACKWARD = (0, 45, 60, 90)
+PIECES = (
+    ("forward_0", 0, 45),
+    ("forward_1", 45, 75),
+    ("backward_0", 0, 75),
+    ("forward_2", 75, 90),
+    ("backward_1", 75, 90),
+)
 
 
 def pieces(rows):
-    for name, cuts in (("forward", FORWARD), ("backward", BACKWARD)):
-        if cuts[-1] != rows:
-            cuts = tuple(k * rows // (len(cuts) - 1) for k in range(len(cuts)))
-        for k, (low, high) in enumerate(zip(cuts, cuts[1:])):
-            yield f"{name}_{k}", (low, high - low)
+    if max(high for _, _, high in PIECES) != rows:
+        return [("forward_0", (0, rows)), ("backward_0", (0, rows))]
+    return [(name, (low, high - low)) for name, low, high in PIECES]
 
 
 def solution(mesh):

time: 77.8 us -> 78.1 us (level)
  starting transfers between devices: 20.4 us -> 26.8 us
  waiting for transfers between devices: 20.9 us -> 15.7 us
  Pallas kernels: 32.9 us -> 31.7 us
    ppermute x17 -> x21, starting transfers between devices: 13.7 us -> 18.9 us  [swap(): return lax.ppermute(value, axis, [(i, i ^ mask) for i in range(count)])]
    ppermute x17 -> x21, waiting for transfers between devices: 16.8 us -> 13.1 us  [swap(): return lax.ppermute(value, axis, [(i, i ^ mask) for i in range(count)])]
    ppermute x1, waiting for transfers between devices: 4.04 us -> 2.59 us  [swap_next(): lax.ppermute(value, axis, [(i, (i + (1 if i % 2 else -1)) % count) for i...]
    ppermute x1, starting transfers between devices: 2.55 us -> 3.7 us  [swap_next(): lax.ppermute(value, axis, [(i, (i + (1 if i % 2 else -1)) % count) for i...]
    pallas_call x1, Pallas kernels: 6.41 us -> 5.51 us  [begin(): pl.pallas_call(begin_kernel, out_shape=(jax.ShapeDtypeStruct((4, total, w...]
  transfers between devices with their start and end apart: 19 -> 23, of which waited for: 7 -> 11; matrix products, arithmetic and copies ran while one was open for 0% -> 1% of each run, Pallas kernels for 39% -> 37%
where the time goes in v4:
time: 78.1 us; the launch traced here: 77.9 us
  Pallas kernels  31.7 us (41%)
  starting transfers between devices  26.8 us (34%)
  waiting for transfers between devices  15.7 us (20%)
  between operations  1.41 us (2%)
  local copies, waits for them, and re-layouts  1.36 us (2%)
  other arithmetic  0.89 us (1%)
    ppermute x21, starting transfers between devices, swap(): return lax.ppermute(value, axis, [(i, i ^ mask) for i in range(count)])  18.9 us
    pallas_call x5, Pallas kernels, conv(): pl.pallas_call(body, out_shape=[jax.ShapeDtypeStruct((rows, cols, width),...  14 us
    ppermute x21, waiting for transfers between devices, swap(): return lax.ppermute(value, axis, [(i, i ^ mask) for i in range(count)])  13.1 us
    pallas_call x1, Pallas kernels, begin(): pl.pallas_call(begin_kernel, out_shape=(jax.ShapeDtypeStruct((4, total, w...  5.51 us
    ppermute x1, starting transfers between devices, swap_rows(): return lax.ppermute(value, ('lat', 'lon'), pairs)  4.13 us
    pallas_call x1, Pallas kernels, all_taps(): pl.pallas_call(body, out_shape=jax.ShapeDtypeStruct((9, width, width), F3...  3.74 us
    ppermute x1, starting transfers between devices, swap_next(): lax.ppermute(value, axis, [(i, (i + (1 if i % 2 else -1)) % count) for i...  3.7 us
    pallas_call x2, Pallas kernels, put_blocks(): pl.pallas_call(body, out_shape=[jax.ShapeDtypeStruct((total, width), F32)...  3.22 us
  transfers between devices with their start and end apart: 23, of which 11 were waited for; matrix products, arithmetic and copies ran while one was open for 1% of the time, Pallas kernels for 37%

profile of v4, /device:TPU:0, one launch (start us, length us, event | category | flops | bytes accessed | tf_op | source)
XLA Modules:
  0.0 77.9 jit_solution(15413697945256683189)
XLA Ops:
  1.3 0.8 %constant_dynamic-slice_fusion.1 = (bf16[1,45,256]{2,1,0:T(8,128)(2,1)S(1)}, bf16[1,45,256]{2,1,0:T(8,128)(2,1)S(1)}, bf16[1,45,256]{2,1,0:T(8,128)(2,1)S(1)}, b...) fusion(bf16[90,45,256]{2,1,0:T(8,128)(2,1)} %field_hbm, ...), kind=kLoop, calls=%fused_computation.65 | loop fusion | bytes 276488 | tf_op jit(solution)/shard_map/jit(dynamic_index_in_dim)/dynamic_slice | solution.py:619
  2.1 4.1 %collective-permute-start = (bf16[2,45,256]{2,1,0:T(8,128)(2,1)S(1)}, bf16[2,45,256]{2,1,0:T(8,128)(2,1)S(1)}, u32[]{:S(2)}, u32[]{:S(2)}) collective-permute-start(bf16[2,45,256]{2,1,0:T(8,128)(2,1)S(1)} %pad_maximum_fusion.7), channel_id=1, source_target_pairs={{0,4},{1,5},{2,6},{3,7},{4,0},{5,1},{6,2},{7,3},{8,16},{9,17},{10,... | collective-permute-start | bytes 138248 | tf_op jit(solution)/shard_map/ppermute | solution.py:567
  6.7 5.5 %shard_map.58 = (bf16[4,90,256]{2,1,0:T(8,128)(2,1)S(1)}, bf16[4416,768]{1,0:T(8,128)(2,1)S(1)}, bf16[256,4608]{1,0:T(8,128)(2,1)S(1)}, f32[256,768]{1,0:T(8,128)S(1)}, bf16[90,45,256]{2,1,0:T(8,128)(2,1)S(1)}) custom-call(bf16[90,45,256]{2,1,0:T(8,128)(2,1)} %field_hbm, bf16[90,45,256]{2,1,0:T(8,128)(2,1)} %cot_hbm), custom_call_target="tpu_custom_call" | custom-call | flops 2264924160 | bytes 4423680 | tf_op jit(solution)/shard_map/pallas_call | solution.py:319
  12.3 3.7 %shard_map.67.taps = f32[9,256,256]{2,1,0:T(8,128)S(1)} custom-call(bf16[4416,768]{1,0:T(8,128)(2,1)S(1)} %get-tuple-element.56.old.window, bf16[256,4608]{1,0:T(8,128)(2,1)S(1)} %get-tuple-element.67.turned, f32[256,768]{1,0:T(8,128)S(1)} %get-tuple-element.68.middle), custom_call_target="tpu_custom_call" | custom-call | flops 3397386240 | bytes 4423680 | tf_op jit(solution)/shard_map/pallas_call | solution.py:371
  16.4 3.7 %collective-permute-start.2 = (bf16[2,92,256]{2,1,0:T(8,128)(2,1)S(1)}, bf16[2,92,256]{2,1,0:T(8,128)(2,1)S(1)}, u32[]{:S(2)}, u32[]{:S(2)}) collective-permute-start(bf16[2,92,256]{2,1,0:T(8,128)(2,1)S(1)} %get-tuple-element.100), channel_id=1, source_target_pairs={{0,7},{1,2},{2,1},{3,4},{4,3},{5,6},{6,5},{7,0},{8,15},{9,10},{10,... | collective-permute-start | bytes 282632 | tf_op jit(solution)/shard_map/ppermute | solution.py:554
  20.1 2.6 %collective-permute-done.2 = bf16[2,92,256]{2,1,0:T(8,128)(2,1)S(1)} collective-permute-done((bf16[2,92,256]{2,1,0:T(8,128)(2,1)S(1)}, bf16[2,92,256]{2,1,0:T(8,128)(2,1)S(1)}, u32[]{:S(2)}, u32[]{:S(2)}) %collective-permute-start.2) | collective-permute-done | bytes 94240 | tf_op jit(solution)/shard_map/ppermute | solution.py:554
  23.8 1.0 %shard_map.61.refs_0_ = bf16[4416,768]{1,0:T(8,128)(2,1)S(1)} custom-call(bf16[4416,768]{1,0:T(8,128)(2,1)S(1)} %get-tuple-element.56.old.window, bf16[2,45,256]{2,1,0:T(8,128)(2,1)S(1)} %get-tuple-element.105.ends, bf16[2,92,256]{2,1,0:T(8,128)(2,1)S(1)} %get-tuple-element.95.sides), custom_call_target="tpu_custom_call", output_to_operand_aliasing={{}: (0, {})} | custom-call | bytes 5898240 | tf_op jit(solution)/shard_map/pallas_call | solution.py:161
  24.8 1.5 %collective-permute-done.4.refs_1_ = f32[1152,256]{1,0:T(8,128)S(1)} collective-permute-done((f32[1152,256]{1,0:T(8,128)S(1)}, f32[1152,256]{1,0:T(8,128)S(1)}, u32[]{:S(2)}, u32[]{:S(2)}) %collective-permute-start.4) | collective-permute-done | bytes 1179680 | tf_op jit(solution)/shard_map/ppermute | solution.py:549
  26.9 1.7 %collective-permute-start.5 = (f32[176,256]{1,0:T(8,128)S(1)}, f32[176,256]{1,0:T(8,128)S(1)}, u32[]{:S(2)}, u32[]{:S(2)}) collective-permute-start(f32[176,256]{1,0:T(8,128)S(1)} %get-tuple-element.72), channel_id=1, source_target_pairs={{0,8},{8,0},{16,24},{24,16},{1,9},{9,1},{17,25},{25,17},{2,10},{10... | collective-permute-start | bytes 540680 | tf_op jit(solution)/shard_map/ppermute | solution.py:549
  28.6 1.5 %collective-permute-start.6 = (f32[176,256]{1,0:T(8,128)S(1)}, f32[176,256]{1,0:T(8,128)S(1)}, u32[]{:S(2)}, u32[]{:S(2)}) collective-permute-start(f32[176,256]{1,0:T(8,128)S(1)} %get-tuple-element.73), channel_id=1, source_target_pairs={{0,16},{8,24},{16,0},{24,8},{1,17},{9,25},{17,1},{25,9},{2,18},{10... | collective-permute-start | bytes 540680 | tf_op jit(solution)/shard_map/ppermute | solution.py:549
  31.5 3.1 %shard_map.62.refs_2_ = bf16[45,45,256]{2,1,0:T(8,128)(2,1)S(1)} custom-call(bf16[4416,768]{1,0:T(8,128)(2,1)S(1)} %shard_map.61.refs_0_, bf16[3,768,256]{2,1,0:T(8,128)(2,1)S(1)} %bitcast.129), custom_call_target="tpu_custom_call" | custom-call | flops 2548039680 | bytes 2211840 | tf_op jit(solution)/shard_map/pallas_call | solution.py:220
  34.6 1.4 %shard_map.59.refs_1_ = bf16[4416,768]{1,0:T(8,128)(2,1)S(1)} custom-call(bf16[90,45,256]{2,1,0:T(8,128)(2,1)S(1)} %get-tuple-element.49.field, bf16[2,45,256]{2,1,0:T(8,128)(2,1)S(1)} %get-tuple-element.106.ends, bf16[2,92,256]{2,1,0:T(8,128)(2,1)S(1)} %get-tuple-element.96.sides), custom_call_target="tpu_custom_call" | custom-call | bytes 8847360 | tf_op jit(solution)/shard_map/pallas_call | solution.py:129
  36.0 2.1 %shard_map.63 = (bf16[30,45,256]{2,1,0:T(8,128)(2,1)S(1)}, bf16[90,45,256]{2,1,0:T(8,128)(2,1)}) custom-call(bf16[4416,768]{1,0:T(8,128)(2,1)S(1)} %shard_map.61.refs_0_, bf16[3,768,256]{2,1,0:T(8,128)(2,1)S(1)} %bitcast.130, bf16[45,45,256]{2,1,0:T(8,128)(2,1)S(1)} %shard_map.62.refs_2_), custom_call_target="tpu_custom_call" | custom-call | flops 1698693120 | bytes 1474560 | tf_op jit(solution)/shard_map/pallas_call | solution.py:220
  38.1 1.0 %collective-permute-done.7.refs_3_ = f32[176,256]{1,0:T(8,128)S(1)} collective-permute-done((f32[176,256]{1,0:T(8,128)S(1)}, f32[176,256]{1,0:T(8,128)S(1)}, u32[]{:S(2)}, u32[]{:S(2)}) %collective-permute-start.7) | collective-permute-done | bytes 180256 | tf_op jit(solution)/shard_map/ppermute | solution.py:549
  39.7 1.1 %collective-permute-start.8 = (f32[88,256]{1,0:T(8,128)S(1)}, f32[88,256]{1,0:T(8,128)S(1)}, u32[]{:S(2)}, u32[]{:S(2)}) collective-permute-start(f32[88,256]{1,0:T(8,128)S(1)} %get-tuple-element.76), channel_id=1, source_target_pairs={{0,2},{1,3},{2,0},{3,1},{4,6},{5,7},{6,4},{7,5},{8,10},{9,11},{10,... | collective-permute-start | bytes 270344 | tf_op jit(solution)/shard_map/ppermute | solution.py:549
  42.1 1.7 %collective-permute-start.11 = (f32[56,256]{1,0:T(8,128)S(1)}, f32[56,256]{1,0:T(8,128)S(1)}, u32[]{:S(2)}, u32[]{:S(2)}) collective-permute-start(f32[56,256]{1,0:T(8,128)S(1)} %get-tuple-element.82), channel_id=1, source_target_pairs={{0,16},{8,24},{16,0},{24,8},{1,17},{9,25},{17,1},{25,9},{2,18},{10... | collective-permute-start | bytes 172040 | tf_op jit(solution)/shard_map/ppermute | solution.py:549
  43.8 1.2 %collective-permute-start.12 = (f32[56,256]{1,0:T(8,128)S(1)}, f32[56,256]{1,0:T(8,128)S(1)}, u32[]{:S(2)}, u32[]{:S(2)}) collective-permute-start(f32[56,256]{1,0:T(8,128)S(1)} %get-tuple-element.83), channel_id=1, source_target_pairs={{0,24},{8,16},{16,8},{24,0},{1,25},{9,17},{17,9},{25,1},{2,26},{10... | collective-permute-start | bytes 172040 | tf_op jit(solution)/shard_map/ppermute | solution.py:549
  45.0 5.9 %shard_map.64 = (bf16[75,45,256]{2,1,0:T(8,128)(2,1)S(1)}, bf16[90,45,256]{2,1,0:T(8,128)(2,1)}) custom-call(s32[2]{0:T(128)S(1)} %pad_add_fusion.refs_0_, bf16[4416,768]{1,0:T(8,128)(2,1)S(1)} %shard_map.59.refs_1_, bf16[3,768,256]{2,1,0:T(8,128)(2,1)S(1)} %shard_map.60.refs_2_, ...), custom_call_target="tpu_custom_call", output_to_operand_aliasing={{1}: (4, {})} | custom-call | flops 4246732800 | bytes 3686400 | tf_op jit(solution)/shard_map/pallas_call | solution.py:220
  51.0 1.8 %collective-permute-start.13 = (f32[144,256]{1,0:T(8,128)S(1)}, f32[144,256]{1,0:T(8,128)S(1)}, u32[]{:S(2)}, u32[]{:S(2)}) collective-permute-start(f32[144,256]{1,0:T(8,128)S(1)} %shard_map.72.first), channel_id=1, source_target_pairs={{0,4},{1,5},{2,6},{3,7},{4,0},{5,1},{6,2},{7,3},{8,12},{9,13},{10,... | collective-permute-start | bytes 442376 | tf_op jit(solution)/shard_map/ppermute | solution.py:549
  52.8 1.3 %shard_map.65 = (bf16[15,45,256]{2,1,0:T(8,128)(2,1)S(1)}, bf16[90,45,256]{2,1,0:T(8,128)(2,1)}) custom-call(bf16[4416,768]{1,0:T(8,128)(2,1)S(1)} %shard_map.61.refs_0_, bf16[3,768,256]{2,1,0:T(8,128)(2,1)S(1)} %bitcast.131, bf16[75,45,256]{2,1,0:T(8,128)(2,1)S(1)} %get-tuple-element.59.refs_2_), custom_call_target="tpu_custom_call" | custom-call | flops 849346560 | bytes 737280 | tf_op jit(solution)/shard_map/pallas_call | solution.py:220
  54.1 1.6 %shard_map.66 = (bf16[15,45,256]{2,1,0:T(8,128)(2,1)S(1)}, bf16[90,45,256]{2,1,0:T(8,128)(2,1)}) custom-call(s32[2]{0:T(128)S(1)} %pad_add_fusion.refs_0_, bf16[4416,768]{1,0:T(8,128)(2,1)S(1)} %shard_map.59.refs_1_, bf16[3,768,256]{2,1,0:T(8,128)(2,1)S(1)} %shard_map.60.refs_2_, ...), custom_call_target="tpu_custom_call", output_to_operand_aliasing={{1}: (4, {})} | custom-call | flops 849346560 | bytes 737280 | tf_op jit(solution)/shard_map/pallas_call | solution.py:220
  55.7 3.6 %collective-permute-done.13.second = f32[144,256]{1,0:T(8,128)S(1)} collective-permute-done((f32[144,256]{1,0:T(8,128)S(1)}, f32[144,256]{1,0:T(8,128)S(1)}, u32[]{:S(2)}, u32[]{:S(2)}) %collective-permute-start.13) | collective-permute-done | bytes 147488 | tf_op jit(solution)/shard_map/ppermute | solution.py:549
  59.4 1.3 %collective-permute-start.16 = (f16[152,256]{1,0:T(8,128)(2,1)S(1)}, f16[152,256]{1,0:T(8,128)(2,1)S(1)}, u32[]{:S(2)}, u32[]{:S(2)}) collective-permute-start(f16[152,256]{1,0:T(8,128)(2,1)S(1)} %convert_element_type.27), channel_id=1, source_target_pairs={{0,24},{8,16},{16,8},{24,0},{1,25},{9,17},{17,9},{25,1},{2,26},{10... | collective-permute-start | bytes 233480 | tf_op jit(solution)/shard_map/ppermute | solution.py:549
  60.7 0.8 %collective-permute-start.15 = (f16[152,256]{1,0:T(8,128)(2,1)S(1)}, f16[152,256]{1,0:T(8,128)(2,1)S(1)}, u32[]{:S(2)}, u32[]{:S(2)}) collective-permute-start(f16[152,256]{1,0:T(8,128)(2,1)S(1)} %convert_element_type.27), channel_id=1, source_target_pairs={{0,16},{8,24},{16,0},{24,8},{1,17},{9,25},{17,1},{25,9},{2,18},{10... | collective-permute-start | bytes 233480 | tf_op jit(solution)/shard_map/ppermute | solution.py:549
  61.5 1.4 %collective-permute-start.14 = (f16[152,256]{1,0:T(8,128)(2,1)S(1)}, f16[152,256]{1,0:T(8,128)(2,1)S(1)}, u32[]{:S(2)}, u32[]{:S(2)}) collective-permute-start(f16[152,256]{1,0:T(8,128)(2,1)S(1)} %convert_element_type.27), channel_id=1, source_target_pairs={{0,8},{8,0},{16,24},{24,16},{1,9},{9,1},{17,25},{25,17},{2,10},{10... | collective-permute-start | bytes 233480 | tf_op jit(solution)/shard_map/ppermute | solution.py:549
  63.1 1.8 %collective-permute-done.16 = f16[152,256]{1,0:T(8,128)(2,1)S(1)} collective-permute-done((f16[152,256]{1,0:T(8,128)(2,1)S(1)}, f16[152,256]{1,0:T(8,128)(2,1)S(1)}, u32[]{:S(2)}, u32[]{:S(2)}) %collective-permute-start.16) | collective-permute-done | bytes 77856 | tf_op jit(solution)/shard_map/ppermute | solution.py:549
  66.2 1.3 %collective-permute-done.17 = f16[152,256]{1,0:T(8,128)(2,1)S(1)} collective-permute-done((f16[152,256]{1,0:T(8,128)(2,1)S(1)}, f16[152,256]{1,0:T(8,128)(2,1)S(1)}, u32[]{:S(2)}, u32[]{:S(2)}) %collective-permute-start.17) | collective-permute-done | bytes 77856 | tf_op jit(solution)/shard_map/ppermute | solution.py:549
  67.5 1.2 %collective-permute-start.20 = (f16[152,256]{1,0:T(8,128)(2,1)S(1)}, f16[152,256]{1,0:T(8,128)(2,1)S(1)}, u32[]{:S(2)}, u32[]{:S(2)}) collective-permute-start(f16[152,256]{1,0:T(8,128)(2,1)S(1)} %collective-permute-done.17), channel_id=1, source_target_pairs={{0,24},{8,16},{16,8},{24,0},{1,25},{9,17},{17,9},{25,1},{2,26},{10... | collective-permute-start | bytes 233480 | tf_op jit(solution)/shard_map/ppermute | solution.py:549
  69.5 1.4 %collective-permute-start.18 = (f16[152,256]{1,0:T(8,128)(2,1)S(1)}, f16[152,256]{1,0:T(8,128)(2,1)S(1)}, u32[]{:S(2)}, u32[]{:S(2)}) collective-permute-start(f16[152,256]{1,0:T(8,128)(2,1)S(1)} %collective-permute-done.17), channel_id=1, source_target_pairs={{0,8},{8,0},{16,24},{24,16},{1,9},{9,1},{17,25},{25,17},{2,10},{10... | collective-permute-start | bytes 233480 | tf_op jit(solution)/shard_map/ppermute | solution.py:549
  71.0 2.5 %collective-permute-done.20 = f16[152,256]{1,0:T(8,128)(2,1)S(1)} collective-permute-done((f16[152,256]{1,0:T(8,128)(2,1)S(1)}, f16[152,256]{1,0:T(8,128)(2,1)S(1)}, u32[]{:S(2)}, u32[]{:S(2)}) %collective-permute-start.20) | collective-permute-done | bytes 77856 | tf_op jit(solution)/shard_map/ppermute | solution.py:549
  74.4 1.9 %shard_map.74 = (f32[2304,256]{1,0:T(8,128)}, bf16[90,45,256]{2,1,0:T(8,128)(2,1)}) custom-call(s32[24]{0:T(128)S(1)} %concatenate.18.where, f32[12,144,256]{2,1,0:T(8,128)S(1)} %pad_maximum_fusion.blocks, bf16[15,45,256]{2,1,0:T(8,128)(2,1)S(1)} %get-tuple-element.84.rest_0_, ...), custom_call_target="tpu_custom_call", output_to_operand_aliasing={{1}: (3, {})} | custom-call | tf_op jit(solution)/shard_map/pallas_call | solution.py:533
  76.4 1.4 %shard_map.75 = f32[2304,256]{1,0:T(8,128)} custom-call(s32[8]{0:T(128)S(1)} %stack.285.where, f32[4,144,256]{2,1,0:T(8,128)S(1)} %convert_multiply_fusion.blocks, f32[2304,256]{1,0:T(8,128)} %get-tuple-element.88.rest_0_), custom_call_target="tpu_custom_call", output_to_operand_aliasing={{}: (2, {})} | custom-call | tf_op jit(solution)/shard_map/pallas_call | solution.py:533
  (74 shorter events, 9.6 us)
Async XLA Ops:
  2.1 13.9 %collective-permute-start = (bf16[2,45,256]{2,1,0:T(8,128)(2,1)S(1)}, bf16[2,45,256]{2,1,0:T(8,128)(2,1)S(1)}, u32[]{:S(2)}, u32[]{:S(2)}) collective-permute-start(bf16[2,45,256]{2,1,0:T(8,128)(2,1)S(1)} %pad_maximum_fusion.7), channel_id=1, source_target_pairs={{0,4},{1,5},{2,6},{3,7},{4,0},{5,1},{6,2},{7,3},{8,16},{9,17},{10,... | collective-permute-start | bytes 138248 | tf_op jit(solution)/shard_map/ppermute | solution.py:567
  6.3 9.8 %collective-permute-start.1 = (bf16[2,45,256]{2,1,0:T(8,128)(2,1)S(1)}, bf16[2,45,256]{2,1,0:T(8,128)(2,1)S(1)}, u32[]{:S(2)}, u32[]{:S(2)}) collective-permute-start(bf16[2,45,256]{2,1,0:T(8,128)(2,1)S(1)} %pad_maximum_fusion.8), channel_id=1, source_target_pairs={{0,8},{8,0},{16,24},{24,16},{1,9},{9,1},{17,25},{25,17},{2,10},{10... | collective-permute-start | bytes 138248 | tf_op jit(solution)/shard_map/ppermute | solution.py:549
  16.1 7.3 %copy-start = (bf16[3,3,256,256]{3,2,1,0:T(8,128)(2,1)S(1)}, bf16[3,3,256,256]{3,2,1,0:T(8,128)(2,1)}, u32[]{:S(2)}) copy-start(bf16[3,3,256,256]{3,2,1,0:T(8,128)(2,1)} %kernel) | copy-start | bytes 3538948
  16.3 3.8 %collective-permute-start.3 = (bf16[2,92,256]{2,1,0:T(8,128)(2,1)S(1)}, bf16[2,92,256]{2,1,0:T(8,128)(2,1)S(1)}, u32[]{:S(2)}, u32[]{:S(2)}) collective-permute-start(bf16[2,92,256]{2,1,0:T(8,128)(2,1)S(1)} %get-tuple-element.99), channel_id=1, source_target_pairs={{0,1},{1,0},{2,3},{3,2},{4,5},{5,4},{6,7},{7,6},{8,9},{9,8},{10,11... | collective-permute-start | bytes 282632 | tf_op jit(solution)/shard_map/ppermute | solution.py:549
  16.4 6.3 %collective-permute-start.2 = (bf16[2,92,256]{2,1,0:T(8,128)(2,1)S(1)}, bf16[2,92,256]{2,1,0:T(8,128)(2,1)S(1)}, u32[]{:S(2)}, u32[]{:S(2)}) collective-permute-start(bf16[2,92,256]{2,1,0:T(8,128)(2,1)S(1)} %get-tuple-element.100), channel_id=1, source_target_pairs={{0,7},{1,2},{2,1},{3,4},{4,3},{5,6},{6,5},{7,0},{8,15},{9,10},{10,... | collective-permute-start | bytes 282632 | tf_op jit(solution)/shard_map/ppermute | solution.py:554
  23.3 2.9 %collective-permute-start.4 = (f32[1152,256]{1,0:T(8,128)S(1)}, f32[1152,256]{1,0:T(8,128)S(1)}, u32[]{:S(2)}, u32[]{:S(2)}) collective-permute-start(f32[1152,256]{1,0:T(8,128)S(1)} %get-tuple-element.70), channel_id=1, source_target_pairs={{0,1},{1,0},{2,3},{3,2},{4,5},{5,4},{6,7},{7,6},{8,9},{9,8},{10,11... | collective-permute-start | bytes 3538952 | tf_op jit(solution)/shard_map/ppermute | solution.py:549
  26.9 11.2 %collective-permute-start.5 = (f32[176,256]{1,0:T(8,128)S(1)}, f32[176,256]{1,0:T(8,128)S(1)}, u32[]{:S(2)}, u32[]{:S(2)}) collective-permute-start(f32[176,256]{1,0:T(8,128)S(1)} %get-tuple-element.72), channel_id=1, source_target_pairs={{0,8},{8,0},{16,24},{24,16},{1,9},{9,1},{17,25},{25,17},{2,10},{10... | collective-permute-start | bytes 540680 | tf_op jit(solution)/shard_map/ppermute | solution.py:549
  28.6 9.6 %collective-permute-start.6 = (f32[176,256]{1,0:T(8,128)S(1)}, f32[176,256]{1,0:T(8,128)S(1)}, u32[]{:S(2)}, u32[]{:S(2)}) collective-permute-start(f32[176,256]{1,0:T(8,128)S(1)} %get-tuple-element.73), channel_id=1, source_target_pairs={{0,16},{8,24},{16,0},{24,8},{1,17},{9,25},{17,1},{25,9},{2,18},{10... | collective-permute-start | bytes 540680 | tf_op jit(solution)/shard_map/ppermute | solution.py:549
  30.0 9.1 %collective-permute-start.7 = (f32[176,256]{1,0:T(8,128)S(1)}, f32[176,256]{1,0:T(8,128)S(1)}, u32[]{:S(2)}, u32[]{:S(2)}) collective-permute-start(f32[176,256]{1,0:T(8,128)S(1)} %get-tuple-element.74), channel_id=1, source_target_pairs={{0,24},{8,16},{16,8},{24,0},{1,25},{9,17},{17,9},{25,1},{2,26},{10... | collective-permute-start | bytes 540680 | tf_op jit(solution)/shard_map/ppermute | solution.py:549
  30.7 10.1 %collective-permute-start.9 = (f32[224,256]{1,0:T(8,128)S(1)}, f32[224,256]{1,0:T(8,128)S(1)}, u32[]{:S(2)}, u32[]{:S(2)}) collective-permute-start(f32[224,256]{1,0:T(8,128)S(1)} %get-tuple-element.79), channel_id=1, source_target_pairs={{0,2},{1,3},{2,0},{3,1},{4,6},{5,7},{6,4},{7,5},{8,10},{9,11},{10,... | collective-permute-start | bytes 688136 | tf_op jit(solution)/shard_map/ppermute | solution.py:549
  39.7 11.2 %collective-permute-start.8 = (f32[88,256]{1,0:T(8,128)S(1)}, f32[88,256]{1,0:T(8,128)S(1)}, u32[]{:S(2)}, u32[]{:S(2)}) collective-permute-start(f32[88,256]{1,0:T(8,128)S(1)} %get-tuple-element.76), channel_id=1, source_target_pairs={{0,2},{1,3},{2,0},{3,1},{4,6},{5,7},{6,4},{7,5},{8,10},{9,11},{10,... | collective-permute-start | bytes 270344 | tf_op jit(solution)/shard_map/ppermute | solution.py:549
  41.4 9.5 %collective-permute-start.10 = (f32[56,256]{1,0:T(8,128)S(1)}, f32[56,256]{1,0:T(8,128)S(1)}, u32[]{:S(2)}, u32[]{:S(2)}) collective-permute-start(f32[56,256]{1,0:T(8,128)S(1)} %get-tuple-element.81), channel_id=1, source_target_pairs={{0,8},{8,0},{16,24},{24,16},{1,9},{9,1},{17,25},{25,17},{2,10},{10... | collective-permute-start | bytes 172040 | tf_op jit(solution)/shard_map/ppermute | solution.py:549
  42.1 8.9 %collective-permute-start.11 = (f32[56,256]{1,0:T(8,128)S(1)}, f32[56,256]{1,0:T(8,128)S(1)}, u32[]{:S(2)}, u32[]{:S(2)}) collective-permute-start(f32[56,256]{1,0:T(8,128)S(1)} %get-tuple-element.82), channel_id=1, source_target_pairs={{0,16},{8,24},{16,0},{24,8},{1,17},{9,25},{17,1},{25,9},{2,18},{10... | collective-permute-start | bytes 172040 | tf_op jit(solution)/shard_map/ppermute | solution.py:549
  43.8 7.1 %collective-permute-start.12 = (f32[56,256]{1,0:T(8,128)S(1)}, f32[56,256]{1,0:T(8,128)S(1)}, u32[]{:S(2)}, u32[]{:S(2)}) collective-permute-start(f32[56,256]{1,0:T(8,128)S(1)} %get-tuple-element.83), channel_id=1, source_target_pairs={{0,24},{8,16},{16,8},{24,0},{1,25},{9,17},{17,9},{25,1},{2,26},{10... | collective-permute-start | bytes 172040 | tf_op jit(solution)/shard_map/ppermute | solution.py:549
  51.0 8.3 %collective-permute-start.13 = (f32[144,256]{1,0:T(8,128)S(1)}, f32[144,256]{1,0:T(8,128)S(1)}, u32[]{:S(2)}, u32[]{:S(2)}) collective-permute-start(f32[144,256]{1,0:T(8,128)S(1)} %shard_map.72.first), channel_id=1, source_target_pairs={{0,4},{1,5},{2,6},{3,7},{4,0},{5,1},{6,2},{7,3},{8,12},{9,13},{10,... | collective-permute-start | bytes 442376 | tf_op jit(solution)/shard_map/ppermute | solution.py:549
  59.4 5.4 %collective-permute-start.16 = (f16[152,256]{1,0:T(8,128)(2,1)S(1)}, f16[152,256]{1,0:T(8,128)(2,1)S(1)}, u32[]{:S(2)}, u32[]{:S(2)}) collective-permute-start(f16[152,256]{1,0:T(8,128)(2,1)S(1)} %convert_element_type.27), channel_id=1, source_target_pairs={{0,24},{8,16},{16,8},{24,0},{1,25},{9,17},{17,9},{25,1},{2,26},{10... | collective-permute-start | bytes 233480 | tf_op jit(solution)/shard_map/ppermute | solution.py:549
  60.7 4.9 %collective-permute-start.15 = (f16[152,256]{1,0:T(8,128)(2,1)S(1)}, f16[152,256]{1,0:T(8,128)(2,1)S(1)}, u32[]{:S(2)}, u32[]{:S(2)}) collective-permute-start(f16[152,256]{1,0:T(8,128)(2,1)S(1)} %convert_element_type.27), channel_id=1, source_target_pairs={{0,16},{8,24},{16,0},{24,8},{1,17},{9,25},{17,1},{25,9},{2,18},{10... | collective-permute-start | bytes 233480 | tf_op jit(solution)/shard_map/ppermute | solution.py:549
  61.5 4.4 %collective-permute-start.14 = (f16[152,256]{1,0:T(8,128)(2,1)S(1)}, f16[152,256]{1,0:T(8,128)(2,1)S(1)}, u32[]{:S(2)}, u32[]{:S(2)}) collective-permute-start(f16[152,256]{1,0:T(8,128)(2,1)S(1)} %convert_element_type.27), channel_id=1, source_target_pairs={{0,8},{8,0},{16,24},{24,16},{1,9},{9,1},{17,25},{25,17},{2,10},{10... | collective-permute-start | bytes 233480 | tf_op jit(solution)/shard_map/ppermute | solution.py:549
  63.0 4.5 %collective-permute-start.17 = (f16[152,256]{1,0:T(8,128)(2,1)S(1)}, f16[152,256]{1,0:T(8,128)(2,1)S(1)}, u32[]{:S(2)}, u32[]{:S(2)}) collective-permute-start(f16[152,256]{1,0:T(8,128)(2,1)S(1)} %convert_element_type.27), channel_id=1, source_target_pairs={{0,2},{1,3},{2,0},{3,1},{4,6},{5,7},{6,4},{7,5},{8,10},{9,11},{10,... | collective-permute-start | bytes 233480 | tf_op jit(solution)/shard_map/ppermute | solution.py:549
  66.1 8.1 %collective-permute-start.21 = (f16[4,152,256]{2,1,0:T(8,128)(2,1)S(1)}, f16[4,152,256]{2,1,0:T(8,128)(2,1)S(1)}, u32[]{:S(2)}, u32[]{:S(2)}) collective-permute-start(f16[4,152,256]{2,1,0:T(8,128)(2,1)S(1)} %pad_maximum_fusion.1), channel_id=1, source_target_pairs={{0,1},{1,0},{2,3},{3,2},{4,5},{5,4},{6,7},{7,6},{8,9},{9,8},{10,11... | collective-permute-start | bytes 933896 | tf_op jit(solution)/shard_map/ppermute | solution.py:549
  67.5 6.1 %collective-permute-start.20 = (f16[152,256]{1,0:T(8,128)(2,1)S(1)}, f16[152,256]{1,0:T(8,128)(2,1)S(1)}, u32[]{:S(2)}, u32[]{:S(2)}) collective-permute-start(f16[152,256]{1,0:T(8,128)(2,1)S(1)} %collective-permute-done.17), channel_id=1, source_target_pairs={{0,24},{8,16},{16,8},{24,0},{1,25},{9,17},{17,9},{25,1},{2,26},{10... | collective-permute-start | bytes 233480 | tf_op jit(solution)/shard_map/ppermute | solution.py:549
  68.7 5.1 %collective-permute-start.19 = (f16[152,256]{1,0:T(8,128)(2,1)S(1)}, f16[152,256]{1,0:T(8,128)(2,1)S(1)}, u32[]{:S(2)}, u32[]{:S(2)}) collective-permute-start(f16[152,256]{1,0:T(8,128)(2,1)S(1)} %collective-permute-done.17), channel_id=1, source_target_pairs={{0,16},{8,24},{16,0},{24,8},{1,17},{9,25},{17,1},{25,9},{2,18},{10... | collective-permute-start | bytes 233480 | tf_op jit(solution)/shard_map/ppermute | solution.py:549
  69.5 4.4 %collective-permute-start.18 = (f16[152,256]{1,0:T(8,128)(2,1)S(1)}, f16[152,256]{1,0:T(8,128)(2,1)S(1)}, u32[]{:S(2)}, u32[]{:S(2)}) collective-permute-start(f16[152,256]{1,0:T(8,128)(2,1)S(1)} %collective-permute-done.17), channel_id=1, source_target_pairs={{0,8},{8,0},{16,24},{24,16},{1,9},{9,1},{17,25},{25,17},{2,10},{10... | collective-permute-start | bytes 233480 | tf_op jit(solution)/shard_map/ppermute | solution.py:549
  74.0 2.3 %collective-permute-start.22 = (f16[4,152,256]{2,1,0:T(8,128)(2,1)S(1)}, f16[4,152,256]{2,1,0:T(8,128)(2,1)S(1)}, u32[]{:S(2)}, u32[]{:S(2)}) collective-permute-start(f16[4,152,256]{2,1,0:T(8,128)(2,1)S(1)} %pad_maximum_fusion.2), channel_id=1, source_target_pairs={{0,1},{1,0},{2,3},{3,2},{4,5},{5,4},{6,7},{7,6},{8,9},{9,8},{10,11... | collective-permute-start | bytes 933896 | tf_op jit(solution)/shard_map/ppermute | solution.py:549

commit v5 on v4

--- a/solution.py
+++ b/solution.py
@@ -22,6 +22,11 @@
 
 def in_hbm(value):
     return pltpu.with_memory_space_constraint(value, pltpu.HBM)
+
+
+def spot():
+    sector = lax.axis_index("lon")
+    return lax.axis_index("lat"), sector & 1, (sector >> 1) & 1
 
 
 def params(mib):
@@ -200,33 +205,31 @@
 def conv(taps, window, weights, shape, first, rows, name, flush):
     total, cols, width = shape
     wide = padded_width(cols)
-    flags = [] if taps is None else [taps]
     more = flush.operands()
-    inputs = len(flags) + 2
+    inputs = 2
 
     def body(*refs):
-        taps = refs[0] if flags else None
-        window, weights = refs[len(flags) : inputs]
+        window, weights = refs[:inputs]
         result = refs[inputs + len(more)]
         copy = None
         if more:
             copy = flush.copy(refs[inputs], refs[-2], refs[-1])
             copy.start()
         view = window.at[first * wide : (first + rows + 2) * wide]
-        conv_rows(taps, view, weights, result, cols, first, rows, total)
+        conv_rows(taps and taps(), view, weights, result, cols, first, rows, total)
         if copy is not None:
             copy.wait()
 
     results = pl.pallas_call(
         body,
         out_shape=[jax.ShapeDtypeStruct((rows, cols, width), BF16)] + flush.shapes(shape),
-        in_specs=[SMEM] * len(flags) + [VMEM] * 2 + flush.specs(),
+        in_specs=[VMEM] * 2 + flush.specs(),
         out_specs=[VMEM] + [HBM] * bool(more),
         scratch_shapes=flush.scratch(),
         input_output_aliases=flush.aliases(inputs, 1),
         compiler_params=params(8),
         cost_estimate=conv_cost(rows, cols, width),
-    )(*flags, window, weights, *more)
+    )(window, weights, *more)
     if more:
         flush.outputs[flush.name] = results[1]
     flush.piece, flush.first, flush.name = results[0], first, name
@@ -380,7 +383,7 @@
     )(window, turned, middle)
 
 
-def edge_kernel(half, taps, ends, sides, rows, columns, send, every, side_rows):
+def edge_kernel(taps, ends, sides, rows, columns, send, every, side_rows):
     _, cols, width = ends.shape
     wide = padded_width(cols)
     total = columns.shape[1]
@@ -412,10 +415,10 @@
                 preferred_element_type=F32,
             )
         every[tap * width : (tap + 1) * width] = value
-    send[...] = every[pl.ds(pl.multiple_of((1 - half[0]) * size, 8), size)]
-
-
-def with_edges(half, taps, ends, sides, rows, columns):
+    send[...] = every[pl.ds(pl.multiple_of((1 - spot()[1]) * size, 8), size)]
+
+
+def with_edges(taps, ends, sides, rows, columns):
     _, _, width = ends.shape
     total = columns.shape[1]
     return pl.pallas_call(
@@ -424,21 +427,22 @@
             jax.ShapeDtypeStruct((9 * width // 2, width), F32),
             jax.ShapeDtypeStruct((9 * width, width), F32),
         ),
-        in_specs=[SMEM] + [VMEM] * 5,
+        in_specs=[VMEM] * 5,
         out_specs=(VMEM, VMEM),
         scratch_shapes=[pltpu.VMEM((2, total + 2, width), F32)],
         compiler_params=params(12),
         cost_estimate=pl.CostEstimate(
             flops=16 * 144 * width * width, bytes_accessed=72 * width * width, transcendentals=0
         ),
-    )(half, taps, ends, sides, rows, columns)
+    )(taps, ends, sides, rows, columns)
 
 
 def add_blocks(places, terms, sizes):
     width = terms[0].shape[1]
     count = len(sizes)
 
-    def body(where, *refs):
+    def body(*refs):
+        where = places(*spot())
         sources, outs = refs[: len(terms)], refs[len(terms) :]
         for k, size in enumerate(sizes):
             value = None
@@ -450,13 +454,13 @@
     return pl.pallas_call(
         body,
         out_shape=tuple(jax.ShapeDtypeStruct((size, width), F32) for size in sizes),
-        in_specs=[SMEM] + [VMEM] * len(terms),
+        in_specs=[VMEM] * len(terms),
         out_specs=(VMEM,) * count,
         compiler_params=params(8),
         cost_estimate=pl.CostEstimate(
             flops=sum(sizes) * width, bytes_accessed=4 * sum(sizes) * width * (len(terms) + 1), transcendentals=0
         ),
-    )(places, *terms)
+    )(*terms)
 
 
 def join_sums(upper, lower):
@@ -511,9 +515,10 @@
     count, _, width = blocks.shape
     more = [] if out is None else [out]
     late = [] if flush is None else flush.operands()
-    inputs = 2 + len(more)
-
-    def body(where, blocks, *rest):
+    inputs = 1 + len(more)
+
+    def body(blocks, *rest):
+        where = places(*spot())
         refs = rest[len(more) + len(late) :]
         out, sem = refs[0], refs[-1]
         copy = None
@@ -533,12 +538,12 @@
     results = pl.pallas_call(
         body,
         out_shape=[jax.ShapeDtypeStruct((total, width), F32)] + (flush.shapes(shape) if late else []),
-        in_specs=[SMEM, VMEM] + [HBM] * len(more) + (flush.specs() if late else []),
+        in_specs=[VMEM] + [HBM] * len(more) + (flush.specs() if late else []),
         out_specs=[HBM] * (1 + bool(late)),
         scratch_shapes=(flush.scratch() if late else []) + [pltpu.SemaphoreType.DMA],
-        input_output_aliases={**({2: 0} if more else {}), **(flush.aliases(inputs, 1) if late else {})},
-        compiler_params=params(8),
-    )(places, blocks, *more, *late)
+        input_output_aliases={**({1: 0} if more else {}), **(flush.aliases(inputs, 1) if late else {})},
+        compiler_params=params(8),
+    )(blocks, *more, *late)
     if late:
         flush.outputs[flush.name] = results[1]
     return results[0]
@@ -570,50 +575,54 @@
 def local(inputs, kernel, cotangent):
     rows, cols, width = inputs.shape
     bands, sectors = lax.axis_size("lat"), lax.axis_size("lon")
-    band, sector = lax.axis_index("lat"), lax.axis_index("lon")
-
-    def vector(*values):
-        return jnp.stack([jnp.asarray(v, jnp.int32) for v in values])
-
-    mine, place = sector & 1, (sector >> 1) & 1
+
+    band, mine, _ = spot()
     odd = band & 1
     half_rows = 9 * width // 2
     unit = 16 * bands
-    upper = half_rows * 5 // 8 // unit * unit
+    upper = half_rows * 9 // 16 // unit * unit
     lower = half_rows - upper
     upper_part, lower_part = upper // bands, lower // 2
     upper_end, lower_end = upper_part // 2, lower_part // bands
     first_sizes = [upper_part] * bands + [lower_part] * 2
-    first_rows = [(band ^ m) * upper_part for m in range(bands)]
-    first_rows += [upper + p * lower_part for p in (place, 1 - place)]
-
-    def homes(h, p):
-        return vector(
-            *[
-                h * half_rows + row
+
+    def first_rows(band, mine, place):
+        rows = [(band ^ m) * upper_part for m in range(bands)]
+        rows += [upper + p * lower_part for p in (place, 1 - place)]
+        return [mine * half_rows + row for row in rows] + rows
+
+    def upper_rows(band, mine, place):
+        return [p * upper_end for _ in range(bands) for p in (place, 1 - place)]
+
+    def lower_rows(band, mine, place):
+        return [(band ^ m) * lower_end for _ in range(2) for m in range(bands)]
+
+    def homes(*flips):
+        def rows(band, mine, place):
+            return [
+                (mine ^ h) * half_rows + row
+                for h, p in flips
                 for m in range(bands)
                 for row in (
-                    (band ^ m) * upper_part + p * upper_end,
-                    upper + p * lower_part + (band ^ m) * lower_end,
+                    (band ^ m) * upper_part + (place ^ p) * upper_end,
+                    upper + (place ^ p) * lower_part + (band ^ m) * lower_end,
                 )
             ]
-        )
+
+        return rows
+
+    def poles():
+        band = lax.axis_index("lat")
+        return jnp.where(band == 0, 2, 0), jnp.where(band == bands - 1, 0, 2)
 
     facts = dict(
         even_band=odd == 0,
         even_sector=mine == 0,
-        half=vector(mine),
         near_row=(1 - odd) * (rows - 1),
         far_row=odd * (rows - 1),
-        first=vector(*[mine * half_rows + row for row in first_rows], *first_rows),
-        upper=vector(*[p * upper_end for _ in range(bands) for p in (place, 1 - place)]),
-        lower=vector(*[(band ^ m) * lower_end for _ in range(2) for m in range(bands)]),
-        poles=vector(jnp.where(band == 0, 2, 0), jnp.where(band == bands - 1, 0, 2)),
-        most_homes=jnp.concatenate([homes(mine, place), homes(mine, 1 - place), homes(1 - mine, place)]),
-        last_homes=homes(1 - mine, 1 - place),
     )
     inputs, kernel, cotangent, facts = lax.optimization_barrier((inputs, kernel, cotangent, facts))
-    even_band, even_sector, half = facts["even_band"], facts["even_sector"], facts["half"]
+    even_band, even_sector = facts["even_band"], facts["even_sector"]
 
     near, far = (
         jnp.stack([lax.dynamic_index_in_dim(field, facts[name], 0, False) for field in (inputs, cotangent)])
@@ -640,7 +649,7 @@
     sides = jnp.stack([jnp.where(even_sector, far, near), jnp.where(even_sector, near, far)], 1)
 
     edge_rows = jnp.stack([cotangent[0], cotangent[-1]])
-    send, every = with_edges(half, outer, ends[0], sides[0], edge_rows, columns[2:])
+    send, every = with_edges(outer, ends[0], sides[0], edge_rows, columns[2:])
 
     weights = kernel.reshape(3, 3 * width, width)
     flipped = flip(kernel)
@@ -651,16 +660,16 @@
         if name.startswith("forward"):
             conv(None, window, weights, inputs.shape, start, count, "outputs", flush)
         else:
-            conv(facts["poles"], cot_window, flipped, inputs.shape, start, count, "input_grad", flush)
+            conv(poles, cot_window, flipped, inputs.shape, start, count, "input_grad", flush)
 
     got = swap(send, "lon", 1)
-    *parts, low_keep, low_send = add_blocks(facts["first"], [every, got], first_sizes)
+    *parts, low_keep, low_send = add_blocks(first_rows, [every, got], first_sizes)
     low_got = swap(low_send, "lon", 2)
     got = []
     for m in range(1, bands):
         got.append(swap(parts[m], "lat", m))
-    lows = add_blocks(facts["lower"], [low_keep, low_got], [lower_end] * bands)
-    keep, send = add_blocks(facts["upper"], [parts[0], *got], [upper_end] * 2)
+    lows = add_blocks(lower_rows, [low_keep, low_got], [lower_end] * bands)
+    keep, send = add_blocks(upper_rows, [parts[0], *got], [upper_end] * 2)
     low_got = []
     got = swap(send, "lon", 2)
     for m in range(1, bands):
@@ -692,16 +701,15 @@
     far = jnp.stack(far)
     far_other = swap(far, "lon", 1)
     most = jnp.concatenate([near_blocks, decode(far), decode(near_other)])
-    kernel_grad = put_blocks(facts["most_homes"], most, cuts, whole, None, flush, inputs.shape)
-    kernel_grad = put_blocks(facts["last_homes"], decode(far_other), cuts, whole, kernel_grad)
+    kernel_grad = put_blocks(homes((0, 0), (0, 1), (1, 0)), most, cuts, whole, None, flush, inputs.shape)
+    kernel_grad = put_blocks(homes((1, 1)), decode(far_other), cuts, whole, kernel_grad)
     return (flush.outputs["outputs"], flush.outputs["input_grad"], kernel_grad.reshape(3, 3, width, width))
 
 
 PIECES = (
-    ("forward_0", 0, 45),
-    ("forward_1", 45, 75),
+    ("forward_0", 0, 60),
+    ("forward_1", 60, 90),
     ("backward_0", 0, 75),
-    ("forward_2", 75, 90),
     ("backward_1", 75, 90),
 )
 

time: 78.1 us -> 73.4 us (0.940)
  Pallas kernels: 31.7 us -> 28.1 us
  starting transfers between devices: 26.8 us -> 24.4 us
  waiting for transfers between devices: 15.7 us -> 17.8 us
    pallas_call x3, Pallas kernels: 1.83 us -> 0.18 us  [add_blocks(): pl.pallas_call(body, out_shape=tuple((jax.ShapeDtypeStruct((size, width),...]
    ppermute x1, waiting for transfers between devices: 2.59 us -> 4.04 us  [swap_next(): lax.ppermute(value, axis, [(i, (i + (1 if i % 2 else -1)) % count) for i...]
    ppermute x21, starting transfers between devices: 18.9 us -> 17.7 us  [swap(): return lax.ppermute(value, axis, [(i, i ^ mask) for i in range(count)])]
    ppermute x1, starting transfers between devices: 3.7 us -> 2.55 us  [swap_next(): lax.ppermute(value, axis, [(i, (i + (1 if i % 2 else -1)) % count) for i...]
    pallas_call x5 -> x4, Pallas kernels: 14 us -> 12.9 us  [conv(): pl.pallas_call(body, out_shape=[jax.ShapeDtypeStruct((rows, cols, width),...]
    pallas_call x2, Pallas kernels: 3.22 us -> 2.17 us  [put_blocks(): pl.pallas_call(body, out_shape=[jax.ShapeDtypeStruct((total, width), F32)...]
  transfers between devices with their start and end apart: 23 -> 23, of which waited for: 11 -> 12; matrix products, arithmetic and copies ran while one was open for 1% -> 1% of each run, Pallas kernels for 37% -> 36%
where the time goes in v5:
time: 73.4 us; the launch traced here: 73.2 us
  Pallas kernels  28.1 us (38%)
  starting transfers between devices  24.4 us (33%)
  waiting for transfers between devices  17.8 us (24%)
  between operations  1.27 us (2%)
  local copies, waits for them, and re-layouts  0.9 us (1%)
  other arithmetic  0.79 us (1%)
    ppermute x21, starting transfers between devices, swap(): return lax.ppermute(value, axis, [(i, i ^ mask) for i in range(count)])  17.7 us
    ppermute x21, waiting for transfers between devices, swap(): return lax.ppermute(value, axis, [(i, i ^ mask) for i in range(count)])  13.8 us
    pallas_call x4, Pallas kernels, conv(): pl.pallas_call(body, out_shape=[jax.ShapeDtypeStruct((rows, cols, width),...  12.9 us
    pallas_call x1, Pallas kernels, begin(): pl.pallas_call(begin_kernel, out_shape=(jax.ShapeDtypeStruct((4, total, w...  5.51 us
    ppermute x1, starting transfers between devices, swap_rows(): return lax.ppermute(value, ('lat', 'lon'), pairs)  4.13 us
    ppermute x1, waiting for transfers between devices, swap_next(): lax.ppermute(value, axis, [(i, (i + (1 if i % 2 else -1)) % count) for i...  4.04 us
    pallas_call x1, Pallas kernels, all_taps(): pl.pallas_call(body, out_shape=jax.ShapeDtypeStruct((9, width, width), F3...  3.74 us
    ppermute x1, starting transfers between devices, swap_next(): lax.ppermute(value, axis, [(i, (i + (1 if i % 2 else -1)) % count) for i...  2.55 us
  transfers between devices with their start and end apart: 23, of which 12 were waited for; matrix products, arithmetic and copies ran while one was open for 1% of the time, Pallas kernels for 36%

profile of v5, /device:TPU:0, one launch (start us, length us, event | category | flops | bytes accessed | tf_op | source)
XLA Modules:
  0.0 73.2 jit_solution(8589098792370051981)
XLA Ops:
  1.5 4.1 %collective-permute-start = (bf16[2,45,256]{2,1,0:T(8,128)(2,1)S(1)}, bf16[2,45,256]{2,1,0:T(8,128)(2,1)S(1)}, u32[]{:S(2)}, u32[]{:S(2)}) collective-permute-start(bf16[2,45,256]{2,1,0:T(8,128)(2,1)S(1)} %pad_maximum_fusion.7), channel_id=1, source_target_pairs={{0,4},{1,5},{2,6},{3,7},{4,0},{5,1},{6,2},{7,3},{8,16},{9,17},{10,... | collective-permute-start | bytes 138248 | tf_op jit(solution)/shard_map/ppermute | solution.py:572
  6.1 5.5 %shard_map.58 = (bf16[4,90,256]{2,1,0:T(8,128)(2,1)S(1)}, bf16[4416,768]{1,0:T(8,128)(2,1)S(1)}, bf16[256,4608]{1,0:T(8,128)(2,1)S(1)}, f32[256,768]{1,0:T(8,128)S(1)}, bf16[90,45,256]{2,1,0:T(8,128)(2,1)S(1)}) custom-call(bf16[90,45,256]{2,1,0:T(8,128)(2,1)} %field_hbm, bf16[90,45,256]{2,1,0:T(8,128)(2,1)} %cot_hbm), custom_call_target="tpu_custom_call" | custom-call | flops 2264924160 | bytes 4423680 | tf_op jit(solution)/shard_map/pallas_call | solution.py:322
  11.6 3.7 %shard_map.65.taps = f32[9,256,256]{2,1,0:T(8,128)S(1)} custom-call(bf16[4416,768]{1,0:T(8,128)(2,1)S(1)} %get-tuple-element.46.old.window, bf16[256,4608]{1,0:T(8,128)(2,1)S(1)} %get-tuple-element.50.turned, f32[256,768]{1,0:T(8,128)S(1)} %get-tuple-element.51.middle), custom_call_target="tpu_custom_call" | custom-call | flops 3397386240 | bytes 4423680 | tf_op jit(solution)/shard_map/pallas_call | solution.py:374
  15.7 2.5 %collective-permute-start.2 = (bf16[2,92,256]{2,1,0:T(8,128)(2,1)S(1)}, bf16[2,92,256]{2,1,0:T(8,128)(2,1)S(1)}, u32[]{:S(2)}, u32[]{:S(2)}) collective-permute-start(bf16[2,92,256]{2,1,0:T(8,128)(2,1)S(1)} %get-tuple-element.82), channel_id=1, source_target_pairs={{0,7},{1,2},{2,1},{3,4},{4,3},{5,6},{6,5},{7,0},{8,15},{9,10},{10,... | collective-permute-start | bytes 282632 | tf_op jit(solution)/shard_map/ppermute | solution.py:559
  18.2 4.0 %collective-permute-done.2 = bf16[2,92,256]{2,1,0:T(8,128)(2,1)S(1)} collective-permute-done((bf16[2,92,256]{2,1,0:T(8,128)(2,1)S(1)}, bf16[2,92,256]{2,1,0:T(8,128)(2,1)S(1)}, u32[]{:S(2)}, u32[]{:S(2)}) %collective-permute-start.2) | collective-permute-done | bytes 94240 | tf_op jit(solution)/shard_map/ppermute | solution.py:559
  23.5 1.0 %shard_map.61.refs_0_ = bf16[4416,768]{1,0:T(8,128)(2,1)S(1)} custom-call(bf16[4416,768]{1,0:T(8,128)(2,1)S(1)} %get-tuple-element.46.old.window, bf16[2,45,256]{2,1,0:T(8,128)(2,1)S(1)} %get-tuple-element.87.ends, bf16[2,92,256]{2,1,0:T(8,128)(2,1)S(1)} %get-tuple-element.77.sides), custom_call_target="tpu_custom_call", output_to_operand_aliasing={{}: (0, {})} | custom-call | bytes 5898240 | tf_op jit(solution)/shard_map/pallas_call | solution.py:166
  24.5 1.5 %collective-permute-done.4.refs_1_ = f32[1152,256]{1,0:T(8,128)S(1)} collective-permute-done((f32[1152,256]{1,0:T(8,128)S(1)}, f32[1152,256]{1,0:T(8,128)S(1)}, u32[]{:S(2)}, u32[]{:S(2)}) %collective-permute-start.4) | collective-permute-done | bytes 1179680 | tf_op jit(solution)/shard_map/ppermute | solution.py:554
  26.2 1.6 %collective-permute-start.5 = (f32[160,256]{1,0:T(8,128)S(1)}, f32[160,256]{1,0:T(8,128)S(1)}, u32[]{:S(2)}, u32[]{:S(2)}) collective-permute-start(f32[160,256]{1,0:T(8,128)S(1)} %get-tuple-element.55), channel_id=1, source_target_pairs={{0,8},{8,0},{16,24},{24,16},{1,9},{9,1},{17,25},{25,17},{2,10},{10... | collective-permute-start | bytes 491528 | tf_op jit(solution)/shard_map/ppermute | solution.py:554
  27.8 1.2 %collective-permute-start.6 = (f32[160,256]{1,0:T(8,128)S(1)}, f32[160,256]{1,0:T(8,128)S(1)}, u32[]{:S(2)}, u32[]{:S(2)}) collective-permute-start(f32[160,256]{1,0:T(8,128)S(1)} %get-tuple-element.56), channel_id=1, source_target_pairs={{0,16},{8,24},{16,0},{24,8},{1,17},{9,25},{17,1},{25,9},{2,18},{10... | collective-permute-start | bytes 491528 | tf_op jit(solution)/shard_map/ppermute | solution.py:554
  29.7 4.1 %shard_map.62.refs_2_ = bf16[60,45,256]{2,1,0:T(8,128)(2,1)S(1)} custom-call(bf16[4416,768]{1,0:T(8,128)(2,1)S(1)} %shard_map.61.refs_0_, bf16[3,768,256]{2,1,0:T(8,128)(2,1)S(1)} %bitcast.76), custom_call_target="tpu_custom_call" | custom-call | flops 3397386240 | bytes 2949120 | tf_op jit(solution)/shard_map/pallas_call | solution.py:223
  33.9 2.1 %collective-permute-done.6.refs_2_ = f32[160,256]{1,0:T(8,128)S(1)} collective-permute-done((f32[160,256]{1,0:T(8,128)S(1)}, f32[160,256]{1,0:T(8,128)S(1)}, u32[]{:S(2)}, u32[]{:S(2)}) %collective-permute-start.6) | collective-permute-done | bytes 163872 | tf_op jit(solution)/shard_map/ppermute | solution.py:554
  35.9 1.4 %collective-permute-done.7.refs_3_ = f32[160,256]{1,0:T(8,128)S(1)} collective-permute-done((f32[160,256]{1,0:T(8,128)S(1)}, f32[160,256]{1,0:T(8,128)S(1)}, u32[]{:S(2)}, u32[]{:S(2)}) %collective-permute-start.7) | collective-permute-done | bytes 163872 | tf_op jit(solution)/shard_map/ppermute | solution.py:554
  37.4 1.7 %collective-permute-start.8 = (f32[80,256]{1,0:T(8,128)S(1)}, f32[80,256]{1,0:T(8,128)S(1)}, u32[]{:S(2)}, u32[]{:S(2)}) collective-permute-start(f32[80,256]{1,0:T(8,128)S(1)} %get-tuple-element.59), channel_id=1, source_target_pairs={{0,2},{1,3},{2,0},{3,1},{4,6},{5,7},{6,4},{7,5},{8,10},{9,11},{10,... | collective-permute-start | bytes 245768 | tf_op jit(solution)/shard_map/ppermute | solution.py:554
  40.0 1.5 %collective-permute-start.11 = (f32[64,256]{1,0:T(8,128)S(1)}, f32[64,256]{1,0:T(8,128)S(1)}, u32[]{:S(2)}, u32[]{:S(2)}) collective-permute-start(f32[64,256]{1,0:T(8,128)S(1)} %get-tuple-element.64), channel_id=1, source_target_pairs={{0,16},{8,24},{16,0},{24,8},{1,17},{9,25},{17,1},{25,9},{2,18},{10... | collective-permute-start | bytes 196616 | tf_op jit(solution)/shard_map/ppermute | solution.py:554
  41.5 1.2 %collective-permute-start.12 = (f32[64,256]{1,0:T(8,128)S(1)}, f32[64,256]{1,0:T(8,128)S(1)}, u32[]{:S(2)}, u32[]{:S(2)}) collective-permute-start(f32[64,256]{1,0:T(8,128)S(1)} %get-tuple-element.65), channel_id=1, source_target_pairs={{0,24},{8,16},{16,8},{24,0},{1,25},{9,17},{17,9},{25,1},{2,26},{10... | collective-permute-start | bytes 196616 | tf_op jit(solution)/shard_map/ppermute | solution.py:554
  42.7 2.1 %shard_map.63 = (bf16[30,45,256]{2,1,0:T(8,128)(2,1)S(1)}, bf16[90,45,256]{2,1,0:T(8,128)(2,1)}) custom-call(bf16[4416,768]{1,0:T(8,128)(2,1)S(1)} %shard_map.61.refs_0_, bf16[3,768,256]{2,1,0:T(8,128)(2,1)S(1)} %bitcast.77, bf16[60,45,256]{2,1,0:T(8,128)(2,1)S(1)} %shard_map.62.refs_2_), custom_call_target="tpu_custom_call" | custom-call | flops 1698693120 | bytes 1474560 | tf_op jit(solution)/shard_map/pallas_call | solution.py:223
  44.8 1.4 %shard_map.59.refs_0_ = bf16[4416,768]{1,0:T(8,128)(2,1)S(1)} custom-call(bf16[90,45,256]{2,1,0:T(8,128)(2,1)S(1)} %get-tuple-element.39.field, bf16[2,45,256]{2,1,0:T(8,128)(2,1)S(1)} %get-tuple-element.88.ends, bf16[2,92,256]{2,1,0:T(8,128)(2,1)S(1)} %get-tuple-element.78.sides), custom_call_target="tpu_custom_call" | custom-call | bytes 8847360 | tf_op jit(solution)/shard_map/pallas_call | solution.py:134
  46.8 5.4 %shard_map.64 = (bf16[75,45,256]{2,1,0:T(8,128)(2,1)S(1)}, bf16[90,45,256]{2,1,0:T(8,128)(2,1)}) custom-call(bf16[4416,768]{1,0:T(8,128)(2,1)S(1)} %shard_map.59.refs_0_, bf16[3,768,256]{2,1,0:T(8,128)(2,1)S(1)} %shard_map.60.refs_1_, bf16[30,45,256]{2,1,0:T(8,128)(2,1)S(1)} %get-tuple-element.47.refs_2_, ...), custom_call_target="tpu_custom_call", output_to_operand_aliasing={{1}: (3, {})} | custom-call | flops 4246732800 | bytes 3686400 | tf_op jit(solution)/shard_map/pallas_call | solution.py:223
  52.2 1.3 %shard_map.72 = (bf16[15,45,256]{2,1,0:T(8,128)(2,1)S(1)}, bf16[90,45,256]{2,1,0:T(8,128)(2,1)}) custom-call(bf16[4416,768]{1,0:T(8,128)(2,1)S(1)} %shard_map.59.refs_0_, bf16[3,768,256]{2,1,0:T(8,128)(2,1)S(1)} %shard_map.60.refs_1_, bf16[75,45,256]{2,1,0:T(8,128)(2,1)S(1)} %get-tuple-element.66.refs_2_), custom_call_target="tpu_custom_call" | custom-call | flops 849346560 | bytes 737280 | tf_op jit(solution)/shard_map/pallas_call | solution.py:223
  54.4 1.0 %collective-permute-start.17 = (f16[152,256]{1,0:T(8,128)(2,1)S(1)}, f16[152,256]{1,0:T(8,128)(2,1)S(1)}, u32[]{:S(2)}, u32[]{:S(2)}) collective-permute-start(f16[152,256]{1,0:T(8,128)(2,1)S(1)} %convert_element_type.27), channel_id=1, source_target_pairs={{0,2},{1,3},{2,0},{3,1},{4,6},{5,7},{6,4},{7,5},{8,10},{9,11},{10,... | collective-permute-start | bytes 233480 | tf_op jit(solution)/shard_map/ppermute | solution.py:554
  55.4 1.2 %collective-permute-start.14 = (f16[152,256]{1,0:T(8,128)(2,1)S(1)}, f16[152,256]{1,0:T(8,128)(2,1)S(1)}, u32[]{:S(2)}, u32[]{:S(2)}) collective-permute-start(f16[152,256]{1,0:T(8,128)(2,1)S(1)} %convert_element_type.27), channel_id=1, source_target_pairs={{0,8},{8,0},{16,24},{24,16},{1,9},{9,1},{17,25},{25,17},{2,10},{10... | collective-permute-start | bytes 233480 | tf_op jit(solution)/shard_map/ppermute | solution.py:554
  56.5 1.0 %collective-permute-start.15 = (f16[152,256]{1,0:T(8,128)(2,1)S(1)}, f16[152,256]{1,0:T(8,128)(2,1)S(1)}, u32[]{:S(2)}, u32[]{:S(2)}) collective-permute-start(f16[152,256]{1,0:T(8,128)(2,1)S(1)} %convert_element_type.27), channel_id=1, source_target_pairs={{0,16},{8,24},{16,0},{24,8},{1,17},{9,25},{17,1},{25,9},{2,18},{10... | collective-permute-start | bytes 233480 | tf_op jit(solution)/shard_map/ppermute | solution.py:554
  57.6 1.3 %collective-permute-start.16 = (f16[152,256]{1,0:T(8,128)(2,1)S(1)}, f16[152,256]{1,0:T(8,128)(2,1)S(1)}, u32[]{:S(2)}, u32[]{:S(2)}) collective-permute-start(f16[152,256]{1,0:T(8,128)(2,1)S(1)} %convert_element_type.27), channel_id=1, source_target_pairs={{0,24},{8,16},{16,8},{24,0},{1,25},{9,17},{17,9},{25,1},{2,26},{10... | collective-permute-start | bytes 233480 | tf_op jit(solution)/shard_map/ppermute | solution.py:554
  58.9 0.9 %collective-permute-done.14 = f16[152,256]{1,0:T(8,128)(2,1)S(1)} collective-permute-done((f16[152,256]{1,0:T(8,128)(2,1)S(1)}, f16[152,256]{1,0:T(8,128)(2,1)S(1)}, u32[]{:S(2)}, u32[]{:S(2)}) %collective-permute-start.14) | collective-permute-done | bytes 77856 | tf_op jit(solution)/shard_map/ppermute | solution.py:554
  59.8 1.2 %collective-permute-done.15 = f16[152,256]{1,0:T(8,128)(2,1)S(1)} collective-permute-done((f16[152,256]{1,0:T(8,128)(2,1)S(1)}, f16[152,256]{1,0:T(8,128)(2,1)S(1)}, u32[]{:S(2)}, u32[]{:S(2)}) %collective-permute-start.15) | collective-permute-done | bytes 77856 | tf_op jit(solution)/shard_map/ppermute | solution.py:554
  60.9 1.9 %collective-permute-done.16 = f16[152,256]{1,0:T(8,128)(2,1)S(1)} collective-permute-done((f16[152,256]{1,0:T(8,128)(2,1)S(1)}, f16[152,256]{1,0:T(8,128)(2,1)S(1)}, u32[]{:S(2)}, u32[]{:S(2)}) %collective-permute-start.16) | collective-permute-done | bytes 77856 | tf_op jit(solution)/shard_map/ppermute | solution.py:554
  63.1 0.9 %collective-permute-start.18 = (f16[152,256]{1,0:T(8,128)(2,1)S(1)}, f16[152,256]{1,0:T(8,128)(2,1)S(1)}, u32[]{:S(2)}, u32[]{:S(2)}) collective-permute-start(f16[152,256]{1,0:T(8,128)(2,1)S(1)} %collective-permute-done.17), channel_id=1, source_target_pairs={{0,8},{8,0},{16,24},{24,16},{1,9},{9,1},{17,25},{25,17},{2,10},{10... | collective-permute-start | bytes 233480 | tf_op jit(solution)/shard_map/ppermute | solution.py:554
  64.0 1.0 %collective-permute-start.19 = (f16[152,256]{1,0:T(8,128)(2,1)S(1)}, f16[152,256]{1,0:T(8,128)(2,1)S(1)}, u32[]{:S(2)}, u32[]{:S(2)}) collective-permute-start(f16[152,256]{1,0:T(8,128)(2,1)S(1)} %collective-permute-done.17), channel_id=1, source_target_pairs={{0,16},{8,24},{16,0},{24,8},{1,17},{9,25},{17,1},{25,9},{2,18},{10... | collective-permute-start | bytes 233480 | tf_op jit(solution)/shard_map/ppermute | solution.py:554
  65.0 1.7 %collective-permute-start.20 = (f16[152,256]{1,0:T(8,128)(2,1)S(1)}, f16[152,256]{1,0:T(8,128)(2,1)S(1)}, u32[]{:S(2)}, u32[]{:S(2)}) collective-permute-start(f16[152,256]{1,0:T(8,128)(2,1)S(1)} %collective-permute-done.17), channel_id=1, source_target_pairs={{0,24},{8,16},{16,8},{24,0},{1,25},{9,17},{17,9},{25,1},{2,26},{10... | collective-permute-start | bytes 233480 | tf_op jit(solution)/shard_map/ppermute | solution.py:554
  66.7 1.1 %collective-permute-done.18 = f16[152,256]{1,0:T(8,128)(2,1)S(1)} collective-permute-done((f16[152,256]{1,0:T(8,128)(2,1)S(1)}, f16[152,256]{1,0:T(8,128)(2,1)S(1)}, u32[]{:S(2)}, u32[]{:S(2)}) %collective-permute-start.18) | collective-permute-done | bytes 77856 | tf_op jit(solution)/shard_map/ppermute | solution.py:554
  68.4 1.9 %collective-permute-done.20 = f16[152,256]{1,0:T(8,128)(2,1)S(1)} collective-permute-done((f16[152,256]{1,0:T(8,128)(2,1)S(1)}, f16[152,256]{1,0:T(8,128)(2,1)S(1)}, u32[]{:S(2)}, u32[]{:S(2)}) %collective-permute-start.20) | collective-permute-done | bytes 77856 | tf_op jit(solution)/shard_map/ppermute | solution.py:554
  70.8 1.3 %shard_map.73 = (f32[2304,256]{1,0:T(8,128)}, bf16[90,45,256]{2,1,0:T(8,128)(2,1)}) custom-call(f32[12,144,256]{2,1,0:T(8,128)S(1)} %pad_maximum_fusion.blocks, bf16[15,45,256]{2,1,0:T(8,128)(2,1)S(1)} %get-tuple-element.67.rest_0_, bf16[90,45,256]{2,1,0:T(8,128)(2,1)} %get-tuple-element.68.rest_1_), custom_call_target="tpu_custom_call", output_to_operand_aliasing={{1}: (2, {})} | custom-call | tf_op jit(solution)/shard_map/pallas_call | solution.py:538
  (67 shorter events, 8.2 us)
Async XLA Ops:
  1.5 13.9 %collective-permute-start = (bf16[2,45,256]{2,1,0:T(8,128)(2,1)S(1)}, bf16[2,45,256]{2,1,0:T(8,128)(2,1)S(1)}, u32[]{:S(2)}, u32[]{:S(2)}) collective-permute-start(bf16[2,45,256]{2,1,0:T(8,128)(2,1)S(1)} %pad_maximum_fusion.7), channel_id=1, source_target_pairs={{0,4},{1,5},{2,6},{3,7},{4,0},{5,1},{6,2},{7,3},{8,16},{9,17},{10,... | collective-permute-start | bytes 138248 | tf_op jit(solution)/shard_map/ppermute | solution.py:572
  5.6 9.8 %collective-permute-start.1 = (bf16[2,45,256]{2,1,0:T(8,128)(2,1)S(1)}, bf16[2,45,256]{2,1,0:T(8,128)(2,1)S(1)}, u32[]{:S(2)}, u32[]{:S(2)}) collective-permute-start(bf16[2,45,256]{2,1,0:T(8,128)(2,1)S(1)} %pad_maximum_fusion.8), channel_id=1, source_target_pairs={{0,8},{8,0},{16,24},{24,16},{1,9},{9,1},{17,25},{25,17},{2,10},{10... | collective-permute-start | bytes 138248 | tf_op jit(solution)/shard_map/ppermute | solution.py:554
  15.5 7.6 %copy-start = (bf16[3,3,256,256]{3,2,1,0:T(8,128)(2,1)S(1)}, bf16[3,3,256,256]{3,2,1,0:T(8,128)(2,1)}, u32[]{:S(2)}) copy-start(bf16[3,3,256,256]{3,2,1,0:T(8,128)(2,1)} %kernel) | copy-start | bytes 3538948
  15.7 6.6 %collective-permute-start.2 = (bf16[2,92,256]{2,1,0:T(8,128)(2,1)S(1)}, bf16[2,92,256]{2,1,0:T(8,128)(2,1)S(1)}, u32[]{:S(2)}, u32[]{:S(2)}) collective-permute-start(bf16[2,92,256]{2,1,0:T(8,128)(2,1)S(1)} %get-tuple-element.82), channel_id=1, source_target_pairs={{0,7},{1,2},{2,1},{3,4},{4,3},{5,6},{6,5},{7,0},{8,15},{9,10},{10,... | collective-permute-start | bytes 282632 | tf_op jit(solution)/shard_map/ppermute | solution.py:559
  18.2 4.1 %collective-permute-start.3 = (bf16[2,92,256]{2,1,0:T(8,128)(2,1)S(1)}, bf16[2,92,256]{2,1,0:T(8,128)(2,1)S(1)}, u32[]{:S(2)}, u32[]{:S(2)}) collective-permute-start(bf16[2,92,256]{2,1,0:T(8,128)(2,1)S(1)} %get-tuple-element.81), channel_id=1, source_target_pairs={{0,1},{1,0},{2,3},{3,2},{4,5},{5,4},{6,7},{7,6},{8,9},{9,8},{10,11... | collective-permute-start | bytes 282632 | tf_op jit(solution)/shard_map/ppermute | solution.py:554
  23.0 2.9 %collective-permute-start.4 = (f32[1152,256]{1,0:T(8,128)S(1)}, f32[1152,256]{1,0:T(8,128)S(1)}, u32[]{:S(2)}, u32[]{:S(2)}) collective-permute-start(f32[1152,256]{1,0:T(8,128)S(1)} %get-tuple-element.53), channel_id=1, source_target_pairs={{0,1},{1,0},{2,3},{3,2},{4,5},{5,4},{6,7},{7,6},{8,9},{9,8},{10,11... | collective-permute-start | bytes 3538952 | tf_op jit(solution)/shard_map/ppermute | solution.py:554
  26.1 13.0 %collective-permute-start.9 = (f32[256,256]{1,0:T(8,128)S(1)}, f32[256,256]{1,0:T(8,128)S(1)}, u32[]{:S(2)}, u32[]{:S(2)}) collective-permute-start(f32[256,256]{1,0:T(8,128)S(1)} %get-tuple-element.61), channel_id=1, source_target_pairs={{0,2},{1,3},{2,0},{3,1},{4,6},{5,7},{6,4},{7,5},{8,10},{9,11},{10,... | collective-permute-start | bytes 786440 | tf_op jit(solution)/shard_map/ppermute | solution.py:554
  26.2 7.7 %collective-permute-start.5 = (f32[160,256]{1,0:T(8,128)S(1)}, f32[160,256]{1,0:T(8,128)S(1)}, u32[]{:S(2)}, u32[]{:S(2)}) collective-permute-start(f32[160,256]{1,0:T(8,128)S(1)} %get-tuple-element.55), channel_id=1, source_target_pairs={{0,8},{8,0},{16,24},{24,16},{1,9},{9,1},{17,25},{25,17},{2,10},{10... | collective-permute-start | bytes 491528 | tf_op jit(solution)/shard_map/ppermute | solution.py:554
  27.8 8.2 %collective-permute-start.6 = (f32[160,256]{1,0:T(8,128)S(1)}, f32[160,256]{1,0:T(8,128)S(1)}, u32[]{:S(2)}, u32[]{:S(2)}) collective-permute-start(f32[160,256]{1,0:T(8,128)S(1)} %get-tuple-element.56), channel_id=1, source_target_pairs={{0,16},{8,24},{16,0},{24,8},{1,17},{9,25},{17,1},{25,9},{2,18},{10... | collective-permute-start | bytes 491528 | tf_op jit(solution)/shard_map/ppermute | solution.py:554
  28.9 8.4 %collective-permute-start.7 = (f32[160,256]{1,0:T(8,128)S(1)}, f32[160,256]{1,0:T(8,128)S(1)}, u32[]{:S(2)}, u32[]{:S(2)}) collective-permute-start(f32[160,256]{1,0:T(8,128)S(1)} %get-tuple-element.57), channel_id=1, source_target_pairs={{0,24},{8,16},{16,8},{24,0},{1,25},{9,17},{17,9},{25,1},{2,26},{10... | collective-permute-start | bytes 491528 | tf_op jit(solution)/shard_map/ppermute | solution.py:554
  37.4 8.8 %collective-permute-start.8 = (f32[80,256]{1,0:T(8,128)S(1)}, f32[80,256]{1,0:T(8,128)S(1)}, u32[]{:S(2)}, u32[]{:S(2)}) collective-permute-start(f32[80,256]{1,0:T(8,128)S(1)} %get-tuple-element.59), channel_id=1, source_target_pairs={{0,2},{1,3},{2,0},{3,1},{4,6},{5,7},{6,4},{7,5},{8,10},{9,11},{10,... | collective-permute-start | bytes 245768 | tf_op jit(solution)/shard_map/ppermute | solution.py:554
  39.1 7.0 %collective-permute-start.10 = (f32[64,256]{1,0:T(8,128)S(1)}, f32[64,256]{1,0:T(8,128)S(1)}, u32[]{:S(2)}, u32[]{:S(2)}) collective-permute-start(f32[64,256]{1,0:T(8,128)S(1)} %get-tuple-element.63), channel_id=1, source_target_pairs={{0,8},{8,0},{16,24},{24,16},{1,9},{9,1},{17,25},{25,17},{2,10},{10... | collective-permute-start | bytes 196616 | tf_op jit(solution)/shard_map/ppermute | solution.py:554
  40.0 6.2 %collective-permute-start.11 = (f32[64,256]{1,0:T(8,128)S(1)}, f32[64,256]{1,0:T(8,128)S(1)}, u32[]{:S(2)}, u32[]{:S(2)}) collective-permute-start(f32[64,256]{1,0:T(8,128)S(1)} %get-tuple-element.64), channel_id=1, source_target_pairs={{0,16},{8,24},{16,0},{24,8},{1,17},{9,25},{17,1},{25,9},{2,18},{10... | collective-permute-start | bytes 196616 | tf_op jit(solution)/shard_map/ppermute | solution.py:554
  41.5 5.2 %collective-permute-start.12 = (f32[64,256]{1,0:T(8,128)S(1)}, f32[64,256]{1,0:T(8,128)S(1)}, u32[]{:S(2)}, u32[]{:S(2)}) collective-permute-start(f32[64,256]{1,0:T(8,128)S(1)} %get-tuple-element.65), channel_id=1, source_target_pairs={{0,24},{8,16},{16,8},{24,0},{1,25},{9,17},{17,9},{25,1},{2,26},{10... | collective-permute-start | bytes 196616 | tf_op jit(solution)/shard_map/ppermute | solution.py:554
  46.7 7.5 %collective-permute-start.13 = (f32[144,256]{1,0:T(8,128)S(1)}, f32[144,256]{1,0:T(8,128)S(1)}, u32[]{:S(2)}, u32[]{:S(2)}) collective-permute-start(f32[144,256]{1,0:T(8,128)S(1)} %shard_map.70.first), channel_id=1, source_target_pairs={{0,4},{1,5},{2,6},{3,7},{4,0},{5,1},{6,2},{7,3},{8,12},{9,13},{10,... | collective-permute-start | bytes 442376 | tf_op jit(solution)/shard_map/ppermute | solution.py:554
  54.4 8.7 %collective-permute-start.17 = (f16[152,256]{1,0:T(8,128)(2,1)S(1)}, f16[152,256]{1,0:T(8,128)(2,1)S(1)}, u32[]{:S(2)}, u32[]{:S(2)}) collective-permute-start(f16[152,256]{1,0:T(8,128)(2,1)S(1)} %convert_element_type.27), channel_id=1, source_target_pairs={{0,2},{1,3},{2,0},{3,1},{4,6},{5,7},{6,4},{7,5},{8,10},{9,11},{10,... | collective-permute-start | bytes 233480 | tf_op jit(solution)/shard_map/ppermute | solution.py:554
  55.4 4.4 %collective-permute-start.14 = (f16[152,256]{1,0:T(8,128)(2,1)S(1)}, f16[152,256]{1,0:T(8,128)(2,1)S(1)}, u32[]{:S(2)}, u32[]{:S(2)}) collective-permute-start(f16[152,256]{1,0:T(8,128)(2,1)S(1)} %convert_element_type.27), channel_id=1, source_target_pairs={{0,8},{8,0},{16,24},{24,16},{1,9},{9,1},{17,25},{25,17},{2,10},{10... | collective-permute-start | bytes 233480 | tf_op jit(solution)/shard_map/ppermute | solution.py:554
  56.5 4.4 %collective-permute-start.15 = (f16[152,256]{1,0:T(8,128)(2,1)S(1)}, f16[152,256]{1,0:T(8,128)(2,1)S(1)}, u32[]{:S(2)}, u32[]{:S(2)}) collective-permute-start(f16[152,256]{1,0:T(8,128)(2,1)S(1)} %convert_element_type.27), channel_id=1, source_target_pairs={{0,16},{8,24},{16,0},{24,8},{1,17},{9,25},{17,1},{25,9},{2,18},{10... | collective-permute-start | bytes 233480 | tf_op jit(solution)/shard_map/ppermute | solution.py:554
  57.6 5.3 %collective-permute-start.16 = (f16[152,256]{1,0:T(8,128)(2,1)S(1)}, f16[152,256]{1,0:T(8,128)(2,1)S(1)}, u32[]{:S(2)}, u32[]{:S(2)}) collective-permute-start(f16[152,256]{1,0:T(8,128)(2,1)S(1)} %convert_element_type.27), channel_id=1, source_target_pairs={{0,24},{8,16},{16,8},{24,0},{1,25},{9,17},{17,9},{25,1},{2,26},{10... | collective-permute-start | bytes 233480 | tf_op jit(solution)/shard_map/ppermute | solution.py:554
  63.0 7.6 %collective-permute-start.21 = (f16[4,152,256]{2,1,0:T(8,128)(2,1)S(1)}, f16[4,152,256]{2,1,0:T(8,128)(2,1)S(1)}, u32[]{:S(2)}, u32[]{:S(2)}) collective-permute-start(f16[4,152,256]{2,1,0:T(8,128)(2,1)S(1)} %pad_maximum_fusion.1), channel_id=1, source_target_pairs={{0,1},{1,0},{2,3},{3,2},{4,5},{5,4},{6,7},{7,6},{8,9},{9,8},{10,11... | collective-permute-start | bytes 933896 | tf_op jit(solution)/shard_map/ppermute | solution.py:554
  63.1 4.7 %collective-permute-start.18 = (f16[152,256]{1,0:T(8,128)(2,1)S(1)}, f16[152,256]{1,0:T(8,128)(2,1)S(1)}, u32[]{:S(2)}, u32[]{:S(2)}) collective-permute-start(f16[152,256]{1,0:T(8,128)(2,1)S(1)} %collective-permute-done.17), channel_id=1, source_target_pairs={{0,8},{8,0},{16,24},{24,16},{1,9},{9,1},{17,25},{25,17},{2,10},{10... | collective-permute-start | bytes 233480 | tf_op jit(solution)/shard_map/ppermute | solution.py:554
  64.0 4.4 %collective-permute-start.19 = (f16[152,256]{1,0:T(8,128)(2,1)S(1)}, f16[152,256]{1,0:T(8,128)(2,1)S(1)}, u32[]{:S(2)}, u32[]{:S(2)}) collective-permute-start(f16[152,256]{1,0:T(8,128)(2,1)S(1)} %collective-permute-done.17), channel_id=1, source_target_pairs={{0,16},{8,24},{16,0},{24,8},{1,17},{9,25},{17,1},{25,9},{2,18},{10... | collective-permute-start | bytes 233480 | tf_op jit(solution)/shard_map/ppermute | solution.py:554
  65.0 5.3 %collective-permute-start.20 = (f16[152,256]{1,0:T(8,128)(2,1)S(1)}, f16[152,256]{1,0:T(8,128)(2,1)S(1)}, u32[]{:S(2)}, u32[]{:S(2)}) collective-permute-start(f16[152,256]{1,0:T(8,128)(2,1)S(1)} %collective-permute-done.17), channel_id=1, source_target_pairs={{0,24},{8,16},{16,8},{24,0},{1,25},{9,17},{17,9},{25,1},{2,26},{10... | collective-permute-start | bytes 233480 | tf_op jit(solution)/shard_map/ppermute | solution.py:554
  70.4 1.8 %collective-permute-start.22 = (f16[4,152,256]{2,1,0:T(8,128)(2,1)S(1)}, f16[4,152,256]{2,1,0:T(8,128)(2,1)S(1)}, u32[]{:S(2)}, u32[]{:S(2)}) collective-permute-start(f16[4,152,256]{2,1,0:T(8,128)(2,1)S(1)} %pad_maximum_fusion.2), channel_id=1, source_target_pairs={{0,1},{1,0},{2,3},{3,2},{4,5},{5,4},{6,7},{7,6},{8,9},{9,8},{10,11... | collective-permute-start | bytes 933896 | tf_op jit(solution)/shard_map/ppermute | solution.py:554

commit v6 on v5

--- a/solution.py
+++ b/solution.py
@@ -242,7 +242,7 @@
 def begin_kernel(field_hbm, cot_hbm, columns, window, turned, sums, cot, field, column_rows, sems):
     total, cols, width = field.shape
     wide = padded_width(cols)
-    part = 2 * turn_group(wide)
+    part = 3 * turn_group(wide)
     chunks = -(-total // part)
     sizes = [min(part, total - at) for at in range(0, total, part)]
 
@@ -266,8 +266,8 @@
     def lay(i, size):
         for copy in copies(i, size):
             copy.wait()
-        step = size if size % 2 else size // 2
-        for low in range(0, size, step):
+        for low in range(0, size, turn_group(wide)):
+            step = min(turn_group(wide), size - low)
             flat = []
             for u in range(low, low + step):
                 r = i * part + u
@@ -280,11 +280,7 @@
                     column_rows[k, pl.ds(r, 1)] = value
                 flat += [other, blank]
             value = jnp.concatenate(flat, 0).T.astype(BF16)
-            if step * wide % 128 == 0:
-                at = pl.multiple_of((i * part + low) * wide, 128)
-                turned[:, pl.ds(at, step * wide)] = value
-            else:
-                turned[:, (i * part + low) * wide : (i * part + low + step) * wide] = value
+            turned[:, pl.ds(pl.multiple_of((i * part + low) * wide, 128), step * wide)] = value
 
     def multiply(i, size):
         at = i * part * wide
@@ -333,7 +329,7 @@
         scratch_shapes=[
             pltpu.VMEM(field.shape, BF16),
             pltpu.VMEM((4, total, width), F32),
-            pltpu.SemaphoreType.DMA((-(-total // (2 * group)), 2)),
+            pltpu.SemaphoreType.DMA((-(-total // (3 * group)), 2)),
         ],
         compiler_params=params(12),
         cost_estimate=pl.CostEstimate(
@@ -383,7 +379,7 @@
     )(window, turned, middle)
 
 
-def edge_kernel(taps, ends, sides, rows, columns, send, every, side_rows):
+def edge_kernel(taps, ends, sides, rows, columns, send_upper, send_lower, every, side_rows):
     _, cols, width = ends.shape
     wide = padded_width(cols)
     total = columns.shape[1]
@@ -415,20 +411,24 @@
                 preferred_element_type=F32,
             )
         every[tap * width : (tap + 1) * width] = value
-    send[...] = every[pl.ds(pl.multiple_of((1 - spot()[1]) * size, 8), size)]
-
-
-def with_edges(taps, ends, sides, rows, columns):
+    at = (1 - spot()[1]) * size
+    for send in (send_upper, send_lower):
+        send[...] = every[pl.ds(pl.multiple_of(at, 8), send.shape[0])]
+        at = at + send.shape[0]
+
+
+def with_edges(taps, ends, sides, rows, columns, upper):
     _, _, width = ends.shape
     total = columns.shape[1]
     return pl.pallas_call(
         edge_kernel,
         out_shape=(
-            jax.ShapeDtypeStruct((9 * width // 2, width), F32),
+            jax.ShapeDtypeStruct((upper, width), F32),
+            jax.ShapeDtypeStruct((9 * width // 2 - upper, width), F32),
             jax.ShapeDtypeStruct((9 * width, width), F32),
         ),
         in_specs=[VMEM] * 5,
-        out_specs=(VMEM, VMEM),
+        out_specs=(VMEM,) * 3,
         scratch_shapes=[pltpu.VMEM((2, total + 2, width), F32)],
         compiler_params=params(12),
         cost_estimate=pl.CostEstimate(
@@ -493,7 +493,7 @@
     def body(first, second, out):
         value = (first[...] + second[...]) * scale
         top = jnp.max(jnp.max(jnp.abs(value), axis=1, keepdims=True), axis=0, keepdims=True)
-        exponent = jnp.ceil(jnp.log2(jnp.maximum(top, 1e-30)))
+        exponent = jnp.ceil(jnp.log2(jnp.maximum(top, 1e-37)))
         out[:rows] = value * jnp.exp2(-exponent)
         out[rows:] = jnp.broadcast_to(exponent, (8, width))
 
@@ -580,16 +580,18 @@
     odd = band & 1
     half_rows = 9 * width // 2
     unit = 16 * bands
-    upper = half_rows * 9 // 16 // unit * unit
+    upper = half_rows // 2 // unit * unit
     lower = half_rows - upper
     upper_part, lower_part = upper // bands, lower // 2
     upper_end, lower_end = upper_part // 2, lower_part // bands
-    first_sizes = [upper_part] * bands + [lower_part] * 2
-
-    def first_rows(band, mine, place):
+
+    def first_upper(band, mine, place):
         rows = [(band ^ m) * upper_part for m in range(bands)]
-        rows += [upper + p * lower_part for p in (place, 1 - place)]
         return [mine * half_rows + row for row in rows] + rows
+
+    def first_lower(band, mine, place):
+        rows = [p * lower_part for p in (place, 1 - place)]
+        return [mine * half_rows + upper + row for row in rows] + rows
 
     def upper_rows(band, mine, place):
         return [p * upper_end for _ in range(bands) for p in (place, 1 - place)]
@@ -649,7 +651,7 @@
     sides = jnp.stack([jnp.where(even_sector, far, near), jnp.where(even_sector, near, far)], 1)
 
     edge_rows = jnp.stack([cotangent[0], cotangent[-1]])
-    send, every = with_edges(outer, ends[0], sides[0], edge_rows, columns[2:])
+    send_upper, send_lower, every = with_edges(outer, ends[0], sides[0], edge_rows, columns[2:], upper)
 
     weights = kernel.reshape(3, 3 * width, width)
     flipped = flip(kernel)
@@ -662,8 +664,10 @@
         else:
             conv(poles, cot_window, flipped, inputs.shape, start, count, "input_grad", flush)
 
-    got = swap(send, "lon", 1)
-    *parts, low_keep, low_send = add_blocks(first_rows, [every, got], first_sizes)
+    got = swap(send_lower, "lon", 1)
+    low_keep, low_send = add_blocks(first_lower, [every, got], [lower_part] * 2)
+    got = swap(send_upper, "lon", 1)
+    parts = add_blocks(first_upper, [every, got], [upper_part] * bands)
     low_got = swap(low_send, "lon", 2)
     got = []
     for m in range(1, bands):

time: 73.4 us -> 71.8 us (0.978)
  waiting for transfers between devices: 17.8 us -> 16.2 us
    ppermute x21 -> x22, waiting for transfers between devices: 13.8 us -> 12.2 us  [swap(): return lax.ppermute(value, axis, [(i, i ^ mask) for i in range(count)])]
    ppermute x21 -> x22, starting transfers between devices: 17.7 us -> 17.8 us  [swap(): return lax.ppermute(value, axis, [(i, i ^ mask) for i in range(count)])]
  transfers between devices with their start and end apart: 23 -> 24, of which waited for: 12 -> 13; matrix products, arithmetic and copies ran while one was open for 1% -> 1% of each run, Pallas kernels for 36% -> 37%
where the time goes in v6:
time: 71.8 us; the launch traced here: 71.6 us
  Pallas kernels  27.9 us (39%)
  starting transfers between devices  24.5 us (34%)
  waiting for transfers between devices  16.2 us (23%)
  between operations  1.27 us (2%)
  local copies, waits for them, and re-layouts  0.9 us (1%)
  other arithmetic  0.79 us (1%)
    ppermute x22, starting transfers between devices, swap(): return lax.ppermute(value, axis, [(i, i ^ mask) for i in range(count)])  17.8 us
    pallas_call x4, Pallas kernels, conv(): pl.pallas_call(body, out_shape=[jax.ShapeDtypeStruct((rows, cols, width),...  12.9 us
    ppermute x22, waiting for transfers between devices, swap(): return lax.ppermute(value, axis, [(i, i ^ mask) for i in range(count)])  12.2 us
    pallas_call x1, Pallas kernels, begin(): pl.pallas_call(begin_kernel, out_shape=(jax.ShapeDtypeStruct((4, total, w...  5.34 us
    ppermute x1, starting transfers between devices, swap_rows(): return lax.ppermute(value, ('lat', 'lon'), pairs)  4.13 us
    ppermute x1, waiting for transfers between devices, swap_next(): lax.ppermute(value, axis, [(i, (i + (1 if i % 2 else -1)) % count) for i...  4.03 us
    pallas_call x1, Pallas kernels, all_taps(): pl.pallas_call(body, out_shape=jax.ShapeDtypeStruct((9, width, width), F3...  3.74 us
    ppermute x1, starting transfers between devices, swap_next(): lax.ppermute(value, axis, [(i, (i + (1 if i % 2 else -1)) % count) for i...  2.54 us
  transfers between devices with their start and end apart: 24, of which 13 were waited for; matrix products, arithmetic and copies ran while one was open for 1% of the time, Pallas kernels for 37%

profile of v6, /device:TPU:0, one launch (start us, length us, event | category | flops | bytes accessed | tf_op | source)
XLA Modules:
  0.0 71.6 jit_solution(2574165430306389006)
XLA Ops:
  0.6 0.8 %constant_dynamic-slice_fusion.1 = (bf16[1,45,256]{2,1,0:T(8,128)(2,1)S(1)}, bf16[1,45,256]{2,1,0:T(8,128)(2,1)S(1)}, bf16[1,45,256]{2,1,0:T(8,128)(2,1)S(1)}, b...) fusion(bf16[90,45,256]{2,1,0:T(8,128)(2,1)} %field_hbm, ...), kind=kLoop, calls=%fused_computation.65 | loop fusion | bytes 276488 | tf_op jit(solution)/shard_map/jit(dynamic_index_in_dim)/dynamic_slice | solution.py:630
  1.5 4.1 %collective-permute-start = (bf16[2,45,256]{2,1,0:T(8,128)(2,1)S(1)}, bf16[2,45,256]{2,1,0:T(8,128)(2,1)S(1)}, u32[]{:S(2)}, u32[]{:S(2)}) collective-permute-start(bf16[2,45,256]{2,1,0:T(8,128)(2,1)S(1)} %pad_maximum_fusion.7), channel_id=1, source_target_pairs={{0,4},{1,5},{2,6},{3,7},{4,0},{5,1},{6,2},{7,3},{8,16},{9,17},{10,... | collective-permute-start | bytes 138248 | tf_op jit(solution)/shard_map/ppermute | solution.py:572
  6.1 5.3 %shard_map.58 = (bf16[4,90,256]{2,1,0:T(8,128)(2,1)S(1)}, bf16[4416,768]{1,0:T(8,128)(2,1)S(1)}, bf16[256,4608]{1,0:T(8,128)(2,1)S(1)}, f32[256,768]{1,0:T(8,128)S(1)}, bf16[90,45,256]{2,1,0:T(8,128)(2,1)S(1)}) custom-call(bf16[90,45,256]{2,1,0:T(8,128)(2,1)} %field_hbm, bf16[90,45,256]{2,1,0:T(8,128)(2,1)} %cot_hbm), custom_call_target="tpu_custom_call" | custom-call | flops 2264924160 | bytes 4423680 | tf_op jit(solution)/shard_map/pallas_call | solution.py:318
  11.5 3.7 %shard_map.65.taps = f32[9,256,256]{2,1,0:T(8,128)S(1)} custom-call(bf16[4416,768]{1,0:T(8,128)(2,1)S(1)} %get-tuple-element.47.old.window, bf16[256,4608]{1,0:T(8,128)(2,1)S(1)} %get-tuple-element.51.turned, f32[256,768]{1,0:T(8,128)S(1)} %get-tuple-element.52.middle), custom_call_target="tpu_custom_call" | custom-call | flops 3397386240 | bytes 4423680 | tf_op jit(solution)/shard_map/pallas_call | solution.py:370
  15.5 2.5 %collective-permute-start.2 = (bf16[2,92,256]{2,1,0:T(8,128)(2,1)S(1)}, bf16[2,92,256]{2,1,0:T(8,128)(2,1)S(1)}, u32[]{:S(2)}, u32[]{:S(2)}) collective-permute-start(bf16[2,92,256]{2,1,0:T(8,128)(2,1)S(1)} %get-tuple-element.84), channel_id=1, source_target_pairs={{0,7},{1,2},{2,1},{3,4},{4,3},{5,6},{6,5},{7,0},{8,15},{9,10},{10,... | collective-permute-start | bytes 282632 | tf_op jit(solution)/shard_map/ppermute | solution.py:559
  18.0 4.0 %collective-permute-done.2 = bf16[2,92,256]{2,1,0:T(8,128)(2,1)S(1)} collective-permute-done((bf16[2,92,256]{2,1,0:T(8,128)(2,1)S(1)}, bf16[2,92,256]{2,1,0:T(8,128)(2,1)S(1)}, u32[]{:S(2)}, u32[]{:S(2)}) %collective-permute-start.2) | collective-permute-done | bytes 94240 | tf_op jit(solution)/shard_map/ppermute | solution.py:559
  23.8 1.0 %shard_map.61.refs_0_ = bf16[4416,768]{1,0:T(8,128)(2,1)S(1)} custom-call(bf16[4416,768]{1,0:T(8,128)(2,1)S(1)} %get-tuple-element.47.old.window, bf16[2,45,256]{2,1,0:T(8,128)(2,1)S(1)} %get-tuple-element.89.ends, bf16[2,92,256]{2,1,0:T(8,128)(2,1)S(1)} %get-tuple-element.79.sides), custom_call_target="tpu_custom_call", output_to_operand_aliasing={{}: (0, {})} | custom-call | bytes 5898240 | tf_op jit(solution)/shard_map/pallas_call | solution.py:166
  25.8 1.0 %collective-permute-start.5 = (f32[144,256]{1,0:T(8,128)S(1)}, f32[144,256]{1,0:T(8,128)S(1)}, u32[]{:S(2)}, u32[]{:S(2)}) collective-permute-start(f32[144,256]{1,0:T(8,128)S(1)} %get-tuple-element.56), channel_id=1, source_target_pairs={{0,8},{8,0},{16,24},{24,16},{1,9},{9,1},{17,25},{25,17},{2,10},{10... | collective-permute-start | bytes 442376 | tf_op jit(solution)/shard_map/ppermute | solution.py:554
  26.9 1.8 %collective-permute-start.6 = (f32[144,256]{1,0:T(8,128)S(1)}, f32[144,256]{1,0:T(8,128)S(1)}, u32[]{:S(2)}, u32[]{:S(2)}) collective-permute-start(f32[144,256]{1,0:T(8,128)S(1)} %get-tuple-element.57), channel_id=1, source_target_pairs={{0,16},{8,24},{16,0},{24,8},{1,17},{9,25},{17,1},{25,9},{2,18},{10... | collective-permute-start | bytes 442376 | tf_op jit(solution)/shard_map/ppermute | solution.py:554
  29.4 4.1 %shard_map.62.refs_2_ = bf16[60,45,256]{2,1,0:T(8,128)(2,1)S(1)} custom-call(bf16[4416,768]{1,0:T(8,128)(2,1)S(1)} %shard_map.61.refs_0_, bf16[3,768,256]{2,1,0:T(8,128)(2,1)S(1)} %bitcast.76), custom_call_target="tpu_custom_call" | custom-call | flops 3397386240 | bytes 2949120 | tf_op jit(solution)/shard_map/pallas_call | solution.py:223
  33.6 1.4 %collective-permute-done.6.refs_2_ = f32[144,256]{1,0:T(8,128)S(1)} collective-permute-done((f32[144,256]{1,0:T(8,128)S(1)}, f32[144,256]{1,0:T(8,128)S(1)}, u32[]{:S(2)}, u32[]{:S(2)}) %collective-permute-start.6) | collective-permute-done | bytes 147488 | tf_op jit(solution)/shard_map/ppermute | solution.py:554
  34.9 1.4 %collective-permute-done.7.refs_3_ = f32[144,256]{1,0:T(8,128)S(1)} collective-permute-done((f32[144,256]{1,0:T(8,128)S(1)}, f32[144,256]{1,0:T(8,128)S(1)}, u32[]{:S(2)}, u32[]{:S(2)}) %collective-permute-start.7) | collective-permute-done | bytes 147488 | tf_op jit(solution)/shard_map/ppermute | solution.py:554
  36.4 1.1 %collective-permute-start.8 = (f32[72,256]{1,0:T(8,128)S(1)}, f32[72,256]{1,0:T(8,128)S(1)}, u32[]{:S(2)}, u32[]{:S(2)}) collective-permute-start(f32[72,256]{1,0:T(8,128)S(1)} %get-tuple-element.60), channel_id=1, source_target_pairs={{0,2},{1,3},{2,0},{3,1},{4,6},{5,7},{6,4},{7,5},{8,10},{9,11},{10,... | collective-permute-start | bytes 221192 | tf_op jit(solution)/shard_map/ppermute | solution.py:554
  37.5 0.9 %collective-permute-start.11 = (f32[72,256]{1,0:T(8,128)S(1)}, f32[72,256]{1,0:T(8,128)S(1)}, u32[]{:S(2)}, u32[]{:S(2)}) collective-permute-start(f32[72,256]{1,0:T(8,128)S(1)} %get-tuple-element.65), channel_id=1, source_target_pairs={{0,8},{8,0},{16,24},{24,16},{1,9},{9,1},{17,25},{25,17},{2,10},{10... | collective-permute-start | bytes 221192 | tf_op jit(solution)/shard_map/ppermute | solution.py:554
  38.4 1.5 %collective-permute-start.12 = (f32[72,256]{1,0:T(8,128)S(1)}, f32[72,256]{1,0:T(8,128)S(1)}, u32[]{:S(2)}, u32[]{:S(2)}) collective-permute-start(f32[72,256]{1,0:T(8,128)S(1)} %get-tuple-element.66), channel_id=1, source_target_pairs={{0,16},{8,24},{16,0},{24,8},{1,17},{9,25},{17,1},{25,9},{2,18},{10... | collective-permute-start | bytes 221192 | tf_op jit(solution)/shard_map/ppermute | solution.py:554
  39.9 1.2 %collective-permute-start.13 = (f32[72,256]{1,0:T(8,128)S(1)}, f32[72,256]{1,0:T(8,128)S(1)}, u32[]{:S(2)}, u32[]{:S(2)}) collective-permute-start(f32[72,256]{1,0:T(8,128)S(1)} %get-tuple-element.67), channel_id=1, source_target_pairs={{0,24},{8,16},{16,8},{24,0},{1,25},{9,17},{17,9},{25,1},{2,26},{10... | collective-permute-start | bytes 221192 | tf_op jit(solution)/shard_map/ppermute | solution.py:554
  41.1 2.1 %shard_map.63 = (bf16[30,45,256]{2,1,0:T(8,128)(2,1)S(1)}, bf16[90,45,256]{2,1,0:T(8,128)(2,1)}) custom-call(bf16[4416,768]{1,0:T(8,128)(2,1)S(1)} %shard_map.61.refs_0_, bf16[3,768,256]{2,1,0:T(8,128)(2,1)S(1)} %bitcast.77, bf16[60,45,256]{2,1,0:T(8,128)(2,1)S(1)} %shard_map.62.refs_2_), custom_call_target="tpu_custom_call" | custom-call | flops 1698693120 | bytes 1474560 | tf_op jit(solution)/shard_map/pallas_call | solution.py:223
  43.1 1.4 %shard_map.59.refs_0_ = bf16[4416,768]{1,0:T(8,128)(2,1)S(1)} custom-call(bf16[90,45,256]{2,1,0:T(8,128)(2,1)S(1)} %get-tuple-element.40.field, bf16[2,45,256]{2,1,0:T(8,128)(2,1)S(1)} %get-tuple-element.90.ends, bf16[2,92,256]{2,1,0:T(8,128)(2,1)S(1)} %get-tuple-element.80.sides), custom_call_target="tpu_custom_call" | custom-call | bytes 8847360 | tf_op jit(solution)/shard_map/pallas_call | solution.py:134
  45.8 5.4 %shard_map.64 = (bf16[75,45,256]{2,1,0:T(8,128)(2,1)S(1)}, bf16[90,45,256]{2,1,0:T(8,128)(2,1)}) custom-call(bf16[4416,768]{1,0:T(8,128)(2,1)S(1)} %shard_map.59.refs_0_, bf16[3,768,256]{2,1,0:T(8,128)(2,1)S(1)} %shard_map.60.refs_1_, bf16[30,45,256]{2,1,0:T(8,128)(2,1)S(1)} %get-tuple-element.48.refs_2_, ...), custom_call_target="tpu_custom_call", output_to_operand_aliasing={{1}: (3, {})} | custom-call | flops 4246732800 | bytes 3686400 | tf_op jit(solution)/shard_map/pallas_call | solution.py:223
  51.2 1.3 %shard_map.73 = (bf16[15,45,256]{2,1,0:T(8,128)(2,1)S(1)}, bf16[90,45,256]{2,1,0:T(8,128)(2,1)}) custom-call(bf16[4416,768]{1,0:T(8,128)(2,1)S(1)} %shard_map.59.refs_0_, bf16[3,768,256]{2,1,0:T(8,128)(2,1)S(1)} %shard_map.60.refs_1_, bf16[75,45,256]{2,1,0:T(8,128)(2,1)S(1)} %get-tuple-element.68.refs_2_), custom_call_target="tpu_custom_call" | custom-call | flops 849346560 | bytes 737280 | tf_op jit(solution)/shard_map/pallas_call | solution.py:223
  53.7 1.3 %collective-permute-start.15 = (f16[152,256]{1,0:T(8,128)(2,1)S(1)}, f16[152,256]{1,0:T(8,128)(2,1)S(1)}, u32[]{:S(2)}, u32[]{:S(2)}) collective-permute-start(f16[152,256]{1,0:T(8,128)(2,1)S(1)} %convert_element_type.27), channel_id=1, source_target_pairs={{0,8},{8,0},{16,24},{24,16},{1,9},{9,1},{17,25},{25,17},{2,10},{10... | collective-permute-start | bytes 233480 | tf_op jit(solution)/shard_map/ppermute | solution.py:554
  55.0 1.0 %collective-permute-start.16 = (f16[152,256]{1,0:T(8,128)(2,1)S(1)}, f16[152,256]{1,0:T(8,128)(2,1)S(1)}, u32[]{:S(2)}, u32[]{:S(2)}) collective-permute-start(f16[152,256]{1,0:T(8,128)(2,1)S(1)} %convert_element_type.27), channel_id=1, source_target_pairs={{0,16},{8,24},{16,0},{24,8},{1,17},{9,25},{17,1},{25,9},{2,18},{10... | collective-permute-start | bytes 233480 | tf_op jit(solution)/shard_map/ppermute | solution.py:554
  56.0 1.2 %collective-permute-start.17 = (f16[152,256]{1,0:T(8,128)(2,1)S(1)}, f16[152,256]{1,0:T(8,128)(2,1)S(1)}, u32[]{:S(2)}, u32[]{:S(2)}) collective-permute-start(f16[152,256]{1,0:T(8,128)(2,1)S(1)} %convert_element_type.27), channel_id=1, source_target_pairs={{0,24},{8,16},{16,8},{24,0},{1,25},{9,17},{17,9},{25,1},{2,26},{10... | collective-permute-start | bytes 233480 | tf_op jit(solution)/shard_map/ppermute | solution.py:554
  57.2 0.9 %collective-permute-done.15 = f16[152,256]{1,0:T(8,128)(2,1)S(1)} collective-permute-done((f16[152,256]{1,0:T(8,128)(2,1)S(1)}, f16[152,256]{1,0:T(8,128)(2,1)S(1)}, u32[]{:S(2)}, u32[]{:S(2)}) %collective-permute-start.15) | collective-permute-done | bytes 77856 | tf_op jit(solution)/shard_map/ppermute | solution.py:554
  58.1 1.3 %collective-permute-done.16 = f16[152,256]{1,0:T(8,128)(2,1)S(1)} collective-permute-done((f16[152,256]{1,0:T(8,128)(2,1)S(1)}, f16[152,256]{1,0:T(8,128)(2,1)S(1)}, u32[]{:S(2)}, u32[]{:S(2)}) %collective-permute-start.16) | collective-permute-done | bytes 77856 | tf_op jit(solution)/shard_map/ppermute | solution.py:554
  59.4 1.9 %collective-permute-done.17 = f16[152,256]{1,0:T(8,128)(2,1)S(1)} collective-permute-done((f16[152,256]{1,0:T(8,128)(2,1)S(1)}, f16[152,256]{1,0:T(8,128)(2,1)S(1)}, u32[]{:S(2)}, u32[]{:S(2)}) %collective-permute-start.17) | collective-permute-done | bytes 77856 | tf_op jit(solution)/shard_map/ppermute | solution.py:554
  61.6 0.9 %collective-permute-start.19 = (f16[152,256]{1,0:T(8,128)(2,1)S(1)}, f16[152,256]{1,0:T(8,128)(2,1)S(1)}, u32[]{:S(2)}, u32[]{:S(2)}) collective-permute-start(f16[152,256]{1,0:T(8,128)(2,1)S(1)} %collective-permute-done.18), channel_id=1, source_target_pairs={{0,8},{8,0},{16,24},{24,16},{1,9},{9,1},{17,25},{25,17},{2,10},{10... | collective-permute-start | bytes 233480 | tf_op jit(solution)/shard_map/ppermute | solution.py:554
  62.4 0.9 %collective-permute-start.20 = (f16[152,256]{1,0:T(8,128)(2,1)S(1)}, f16[152,256]{1,0:T(8,128)(2,1)S(1)}, u32[]{:S(2)}, u32[]{:S(2)}) collective-permute-start(f16[152,256]{1,0:T(8,128)(2,1)S(1)} %collective-permute-done.18), channel_id=1, source_target_pairs={{0,16},{8,24},{16,0},{24,8},{1,17},{9,25},{17,1},{25,9},{2,18},{10... | collective-permute-start | bytes 233480 | tf_op jit(solution)/shard_map/ppermute | solution.py:554
  63.4 1.7 %collective-permute-start.21 = (f16[152,256]{1,0:T(8,128)(2,1)S(1)}, f16[152,256]{1,0:T(8,128)(2,1)S(1)}, u32[]{:S(2)}, u32[]{:S(2)}) collective-permute-start(f16[152,256]{1,0:T(8,128)(2,1)S(1)} %collective-permute-done.18), channel_id=1, source_target_pairs={{0,24},{8,16},{16,8},{24,0},{1,25},{9,17},{17,9},{25,1},{2,26},{10... | collective-permute-start | bytes 233480 | tf_op jit(solution)/shard_map/ppermute | solution.py:554
  65.2 1.1 %collective-permute-done.19 = f16[152,256]{1,0:T(8,128)(2,1)S(1)} collective-permute-done((f16[152,256]{1,0:T(8,128)(2,1)S(1)}, f16[152,256]{1,0:T(8,128)(2,1)S(1)}, u32[]{:S(2)}, u32[]{:S(2)}) %collective-permute-start.19) | collective-permute-done | bytes 77856 | tf_op jit(solution)/shard_map/ppermute | solution.py:554
  66.9 1.8 %collective-permute-done.21 = f16[152,256]{1,0:T(8,128)(2,1)S(1)} collective-permute-done((f16[152,256]{1,0:T(8,128)(2,1)S(1)}, f16[152,256]{1,0:T(8,128)(2,1)S(1)}, u32[]{:S(2)}, u32[]{:S(2)}) %collective-permute-start.21) | collective-permute-done | bytes 77856 | tf_op jit(solution)/shard_map/ppermute | solution.py:554
  69.2 1.4 %shard_map.74 = (f32[2304,256]{1,0:T(8,128)}, bf16[90,45,256]{2,1,0:T(8,128)(2,1)}) custom-call(f32[12,144,256]{2,1,0:T(8,128)S(1)} %pad_maximum_fusion.blocks, bf16[15,45,256]{2,1,0:T(8,128)(2,1)S(1)} %get-tuple-element.69.rest_0_, bf16[90,45,256]{2,1,0:T(8,128)(2,1)} %get-tuple-element.70.rest_1_), custom_call_target="tpu_custom_call", output_to_operand_aliasing={{1}: (2, {})} | custom-call | tf_op jit(solution)/shard_map/pallas_call | solution.py:538
  (70 shorter events, 8.9 us)
Async XLA Ops:
  1.5 13.7 %collective-permute-start = (bf16[2,45,256]{2,1,0:T(8,128)(2,1)S(1)}, bf16[2,45,256]{2,1,0:T(8,128)(2,1)S(1)}, u32[]{:S(2)}, u32[]{:S(2)}) collective-permute-start(bf16[2,45,256]{2,1,0:T(8,128)(2,1)S(1)} %pad_maximum_fusion.7), channel_id=1, source_target_pairs={{0,4},{1,5},{2,6},{3,7},{4,0},{5,1},{6,2},{7,3},{8,16},{9,17},{10,... | collective-permute-start | bytes 138248 | tf_op jit(solution)/shard_map/ppermute | solution.py:572
  5.6 9.6 %collective-permute-start.1 = (bf16[2,45,256]{2,1,0:T(8,128)(2,1)S(1)}, bf16[2,45,256]{2,1,0:T(8,128)(2,1)S(1)}, u32[]{:S(2)}, u32[]{:S(2)}) collective-permute-start(bf16[2,45,256]{2,1,0:T(8,128)(2,1)S(1)} %pad_maximum_fusion.8), channel_id=1, source_target_pairs={{0,8},{8,0},{16,24},{24,16},{1,9},{9,1},{17,25},{25,17},{2,10},{10... | collective-permute-start | bytes 138248 | tf_op jit(solution)/shard_map/ppermute | solution.py:554
  15.3 8.1 %copy-start = (bf16[3,3,256,256]{3,2,1,0:T(8,128)(2,1)S(1)}, bf16[3,3,256,256]{3,2,1,0:T(8,128)(2,1)}, u32[]{:S(2)}) copy-start(bf16[3,3,256,256]{3,2,1,0:T(8,128)(2,1)} %kernel) | copy-start | bytes 3538948
  15.5 6.6 %collective-permute-start.2 = (bf16[2,92,256]{2,1,0:T(8,128)(2,1)S(1)}, bf16[2,92,256]{2,1,0:T(8,128)(2,1)S(1)}, u32[]{:S(2)}, u32[]{:S(2)}) collective-permute-start(bf16[2,92,256]{2,1,0:T(8,128)(2,1)S(1)} %get-tuple-element.84), channel_id=1, source_target_pairs={{0,7},{1,2},{2,1},{3,4},{4,3},{5,6},{6,5},{7,0},{8,15},{9,10},{10,... | collective-permute-start | bytes 282632 | tf_op jit(solution)/shard_map/ppermute | solution.py:559
  18.0 4.1 %collective-permute-start.3 = (bf16[2,92,256]{2,1,0:T(8,128)(2,1)S(1)}, bf16[2,92,256]{2,1,0:T(8,128)(2,1)S(1)}, u32[]{:S(2)}, u32[]{:S(2)}) collective-permute-start(bf16[2,92,256]{2,1,0:T(8,128)(2,1)S(1)} %get-tuple-element.83), channel_id=1, source_target_pairs={{0,1},{1,0},{2,3},{3,2},{4,5},{5,4},{6,7},{7,6},{8,9},{9,8},{10,11... | collective-permute-start | bytes 282632 | tf_op jit(solution)/shard_map/ppermute | solution.py:554
  22.9 2.1 %collective-permute-start.9 = (f32[576,256]{1,0:T(8,128)S(1)}, f32[576,256]{1,0:T(8,128)S(1)}, u32[]{:S(2)}, u32[]{:S(2)}) collective-permute-start(f32[576,256]{1,0:T(8,128)S(1)} %get-tuple-element.61), channel_id=1, source_target_pairs={{0,1},{1,0},{2,3},{3,2},{4,5},{5,4},{6,7},{7,6},{8,9},{9,8},{10,11... | collective-permute-start | bytes 1769480 | tf_op jit(solution)/shard_map/ppermute | solution.py:554
  22.9 2.8 %collective-permute-start.4 = (f32[576,256]{1,0:T(8,128)S(1)}, f32[576,256]{1,0:T(8,128)S(1)}, u32[]{:S(2)}, u32[]{:S(2)}) collective-permute-start(f32[576,256]{1,0:T(8,128)S(1)} %get-tuple-element.54), channel_id=1, source_target_pairs={{0,1},{1,0},{2,3},{3,2},{4,5},{5,4},{6,7},{7,6},{8,9},{9,8},{10,11... | collective-permute-start | bytes 1769480 | tf_op jit(solution)/shard_map/ppermute | solution.py:554
  25.0 12.5 %collective-permute-start.10 = (f32[288,256]{1,0:T(8,128)S(1)}, f32[288,256]{1,0:T(8,128)S(1)}, u32[]{:S(2)}, u32[]{:S(2)}) collective-permute-start(f32[288,256]{1,0:T(8,128)S(1)} %get-tuple-element.63), channel_id=1, source_target_pairs={{0,2},{1,3},{2,0},{3,1},{4,6},{5,7},{6,4},{7,5},{8,10},{9,11},{10,... | collective-permute-start | bytes 884744 | tf_op jit(solution)/shard_map/ppermute | solution.py:554
  25.8 7.7 %collective-permute-start.5 = (f32[144,256]{1,0:T(8,128)S(1)}, f32[144,256]{1,0:T(8,128)S(1)}, u32[]{:S(2)}, u32[]{:S(2)}) collective-permute-start(f32[144,256]{1,0:T(8,128)S(1)} %get-tuple-element.56), channel_id=1, source_target_pairs={{0,8},{8,0},{16,24},{24,16},{1,9},{9,1},{17,25},{25,17},{2,10},{10... | collective-permute-start | bytes 442376 | tf_op jit(solution)/shard_map/ppermute | solution.py:554
  26.9 8.1 %collective-permute-start.6 = (f32[144,256]{1,0:T(8,128)S(1)}, f32[144,256]{1,0:T(8,128)S(1)}, u32[]{:S(2)}, u32[]{:S(2)}) collective-permute-start(f32[144,256]{1,0:T(8,128)S(1)} %get-tuple-element.57), channel_id=1, source_target_pairs={{0,16},{8,24},{16,0},{24,8},{1,17},{9,25},{17,1},{25,9},{2,18},{10... | collective-permute-start | bytes 442376 | tf_op jit(solution)/shard_map/ppermute | solution.py:554
  28.6 7.7 %collective-permute-start.7 = (f32[144,256]{1,0:T(8,128)S(1)}, f32[144,256]{1,0:T(8,128)S(1)}, u32[]{:S(2)}, u32[]{:S(2)}) collective-permute-start(f32[144,256]{1,0:T(8,128)S(1)} %get-tuple-element.58), channel_id=1, source_target_pairs={{0,24},{8,16},{16,8},{24,0},{1,25},{9,17},{17,9},{25,1},{2,26},{10... | collective-permute-start | bytes 442376 | tf_op jit(solution)/shard_map/ppermute | solution.py:554
  36.4 8.2 %collective-permute-start.8 = (f32[72,256]{1,0:T(8,128)S(1)}, f32[72,256]{1,0:T(8,128)S(1)}, u32[]{:S(2)}, u32[]{:S(2)}) collective-permute-start(f32[72,256]{1,0:T(8,128)S(1)} %get-tuple-element.60), channel_id=1, source_target_pairs={{0,2},{1,3},{2,0},{3,1},{4,6},{5,7},{6,4},{7,5},{8,10},{9,11},{10,... | collective-permute-start | bytes 221192 | tf_op jit(solution)/shard_map/ppermute | solution.py:554
  37.5 7.0 %collective-permute-start.11 = (f32[72,256]{1,0:T(8,128)S(1)}, f32[72,256]{1,0:T(8,128)S(1)}, u32[]{:S(2)}, u32[]{:S(2)}) collective-permute-start(f32[72,256]{1,0:T(8,128)S(1)} %get-tuple-element.65), channel_id=1, source_target_pairs={{0,8},{8,0},{16,24},{24,16},{1,9},{9,1},{17,25},{25,17},{2,10},{10... | collective-permute-start | bytes 221192 | tf_op jit(solution)/shard_map/ppermute | solution.py:554
  38.4 6.2 %collective-permute-start.12 = (f32[72,256]{1,0:T(8,128)S(1)}, f32[72,256]{1,0:T(8,128)S(1)}, u32[]{:S(2)}, u32[]{:S(2)}) collective-permute-start(f32[72,256]{1,0:T(8,128)S(1)} %get-tuple-element.66), channel_id=1, source_target_pairs={{0,16},{8,24},{16,0},{24,8},{1,17},{9,25},{17,1},{25,9},{2,18},{10... | collective-permute-start | bytes 221192 | tf_op jit(solution)/shard_map/ppermute | solution.py:554
  39.9 5.3 %collective-permute-start.13 = (f32[72,256]{1,0:T(8,128)S(1)}, f32[72,256]{1,0:T(8,128)S(1)}, u32[]{:S(2)}, u32[]{:S(2)}) collective-permute-start(f32[72,256]{1,0:T(8,128)S(1)} %get-tuple-element.67), channel_id=1, source_target_pairs={{0,24},{8,16},{16,8},{24,0},{1,25},{9,17},{17,9},{25,1},{2,26},{10... | collective-permute-start | bytes 221192 | tf_op jit(solution)/shard_map/ppermute | solution.py:554
  45.2 7.7 %collective-permute-start.14 = (f32[144,256]{1,0:T(8,128)S(1)}, f32[144,256]{1,0:T(8,128)S(1)}, u32[]{:S(2)}, u32[]{:S(2)}) collective-permute-start(f32[144,256]{1,0:T(8,128)S(1)} %shard_map.71.first), channel_id=1, source_target_pairs={{0,4},{1,5},{2,6},{3,7},{4,0},{5,1},{6,2},{7,3},{8,12},{9,13},{10,... | collective-permute-start | bytes 442376 | tf_op jit(solution)/shard_map/ppermute | solution.py:554
  53.0 8.5 %collective-permute-start.18 = (f16[152,256]{1,0:T(8,128)(2,1)S(1)}, f16[152,256]{1,0:T(8,128)(2,1)S(1)}, u32[]{:S(2)}, u32[]{:S(2)}) collective-permute-start(f16[152,256]{1,0:T(8,128)(2,1)S(1)} %convert_element_type.27), channel_id=1, source_target_pairs={{0,2},{1,3},{2,0},{3,1},{4,6},{5,7},{6,4},{7,5},{8,10},{9,11},{10,... | collective-permute-start | bytes 233480 | tf_op jit(solution)/shard_map/ppermute | solution.py:554
  53.7 4.4 %collective-permute-start.15 = (f16[152,256]{1,0:T(8,128)(2,1)S(1)}, f16[152,256]{1,0:T(8,128)(2,1)S(1)}, u32[]{:S(2)}, u32[]{:S(2)}) collective-permute-start(f16[152,256]{1,0:T(8,128)(2,1)S(1)} %convert_element_type.27), channel_id=1, source_target_pairs={{0,8},{8,0},{16,24},{24,16},{1,9},{9,1},{17,25},{25,17},{2,10},{10... | collective-permute-start | bytes 233480 | tf_op jit(solution)/shard_map/ppermute | solution.py:554
  55.0 4.4 %collective-permute-start.16 = (f16[152,256]{1,0:T(8,128)(2,1)S(1)}, f16[152,256]{1,0:T(8,128)(2,1)S(1)}, u32[]{:S(2)}, u32[]{:S(2)}) collective-permute-start(f16[152,256]{1,0:T(8,128)(2,1)S(1)} %convert_element_type.27), channel_id=1, source_target_pairs={{0,16},{8,24},{16,0},{24,8},{1,17},{9,25},{17,1},{25,9},{2,18},{10... | collective-permute-start | bytes 233480 | tf_op jit(solution)/shard_map/ppermute | solution.py:554
  56.0 5.3 %collective-permute-start.17 = (f16[152,256]{1,0:T(8,128)(2,1)S(1)}, f16[152,256]{1,0:T(8,128)(2,1)S(1)}, u32[]{:S(2)}, u32[]{:S(2)}) collective-permute-start(f16[152,256]{1,0:T(8,128)(2,1)S(1)} %convert_element_type.27), channel_id=1, source_target_pairs={{0,24},{8,16},{16,8},{24,0},{1,25},{9,17},{17,9},{25,1},{2,26},{10... | collective-permute-start | bytes 233480 | tf_op jit(solution)/shard_map/ppermute | solution.py:554
  61.5 7.5 %collective-permute-start.22 = (f16[4,152,256]{2,1,0:T(8,128)(2,1)S(1)}, f16[4,152,256]{2,1,0:T(8,128)(2,1)S(1)}, u32[]{:S(2)}, u32[]{:S(2)}) collective-permute-start(f16[4,152,256]{2,1,0:T(8,128)(2,1)S(1)} %pad_maximum_fusion.1), channel_id=1, source_target_pairs={{0,1},{1,0},{2,3},{3,2},{4,5},{5,4},{6,7},{7,6},{8,9},{9,8},{10,11... | collective-permute-start | bytes 933896 | tf_op jit(solution)/shard_map/ppermute | solution.py:554
  61.6 4.7 %collective-permute-start.19 = (f16[152,256]{1,0:T(8,128)(2,1)S(1)}, f16[152,256]{1,0:T(8,128)(2,1)S(1)}, u32[]{:S(2)}, u32[]{:S(2)}) collective-permute-start(f16[152,256]{1,0:T(8,128)(2,1)S(1)} %collective-permute-done.18), channel_id=1, source_target_pairs={{0,8},{8,0},{16,24},{24,16},{1,9},{9,1},{17,25},{25,17},{2,10},{10... | collective-permute-start | bytes 233480 | tf_op jit(solution)/shard_map/ppermute | solution.py:554
  62.4 4.4 %collective-permute-start.20 = (f16[152,256]{1,0:T(8,128)(2,1)S(1)}, f16[152,256]{1,0:T(8,128)(2,1)S(1)}, u32[]{:S(2)}, u32[]{:S(2)}) collective-permute-start(f16[152,256]{1,0:T(8,128)(2,1)S(1)} %collective-permute-done.18), channel_id=1, source_target_pairs={{0,16},{8,24},{16,0},{24,8},{1,17},{9,25},{17,1},{25,9},{2,18},{10... | collective-permute-start | bytes 233480 | tf_op jit(solution)/shard_map/ppermute | solution.py:554
  63.4 5.3 %collective-permute-start.21 = (f16[152,256]{1,0:T(8,128)(2,1)S(1)}, f16[152,256]{1,0:T(8,128)(2,1)S(1)}, u32[]{:S(2)}, u32[]{:S(2)}) collective-permute-start(f16[152,256]{1,0:T(8,128)(2,1)S(1)} %collective-permute-done.18), channel_id=1, source_target_pairs={{0,24},{8,16},{16,8},{24,0},{1,25},{9,17},{17,9},{25,1},{2,26},{10... | collective-permute-start | bytes 233480 | tf_op jit(solution)/shard_map/ppermute | solution.py:554
  68.8 1.8 %collective-permute-start.23 = (f16[4,152,256]{2,1,0:T(8,128)(2,1)S(1)}, f16[4,152,256]{2,1,0:T(8,128)(2,1)S(1)}, u32[]{:S(2)}, u32[]{:S(2)}) collective-permute-start(f16[4,152,256]{2,1,0:T(8,128)(2,1)S(1)} %pad_maximum_fusion.2), channel_id=1, source_target_pairs={{0,1},{1,0},{2,3},{3,2},{4,5},{5,4},{6,7},{7,6},{8,9},{9,8},{10,11... | collective-permute-start | bytes 933896 | tf_op jit(solution)/shard_map/ppermute | solution.py:554
